TPU v7x, 512 devices: a whole 4x8x8 slice. The times are simulated.
512 devices in a mesh: dp: 16 (over x, y_hi), expert: 32 (over z, y_lo, core).
Axes of the slice: x: 4, y: 8 (y_hi: 4, y_lo: 2; y = y_hi * 2 + y_lo), z: 8, core: 2. Of those that a mesh axis runs over, the one named last changes fastest.
Arguments:
- patches: bfloat16 [65536, 1024], P(('dp', 'expert')), may hold values from -6 to 6
- expert_ids: int32 [65536, 2], P(('dp', 'expert')), may hold values from 0 to 31, all different within a row; in each aligned block of 128 rows (0 to 127, 128 to 255, ...) at most 16 rows name the same one
- gate_weights: float32 [65536, 2], P(('dp', 'expert')), may hold values from 0.2 to 1
- conv_weight: float32 [49, 1024], replicated, may hold values from -2 to 2
- conv_bias: float32 [1024], replicated, may hold values from -6 to 6
- ln_gain: float32 [1024], replicated, may hold values from 0.1 to 1.9
- ln_shift: float32 [1024], replicated, may hold values from -6 to 6
- w_in: bfloat16 [32, 1024, 1024], P('expert', 'dp'), may hold values from -0.1875 to 0.1875
- w_out: bfloat16 [32, 1024, 1024], P('expert', 'dp'), may hold values from -0.1875 to 0.1875
- grad_mixed: bfloat16 [65536, 1024], P(('dp', 'expert')), may hold values from -6 to 6
Outputs:
- mixed: bfloat16 [65536, 1024], P(('dp', 'expert'))
- grad_input: float32 [65536, 1024], P(('dp', 'expert'))
- grad_w_in: float32 [32, 1024, 1024], P('expert', 'dp')
- grad_w_out: float32 [32, 1024, 1024], P('expert', 'dp')
Inputs may be any that keep to these rules, and one draw needn't show every extreme that they name: `expert_ids`: the two ids of a row differ. Within the 128 rows of one device no expert is named more than 16 times, a bound that some block reaches in every draw.
All inputs are finite; a program needn't handle non-finite values.
Results may differ from a plain program's by a relative error of at most 0.013.
Values may be sent and summed in bfloat16 or wider, within the bound.
No kernel may reach another device: no remote copies, remote signals or barrier semaphores. Data moves between devices by JAX's collectives and lax.ppermute only.
A program may use at most 64 MiB of HBM per device.

v0:
```python
from functools import partial

import jax
import jax.numpy as jnp
from jax import lax
from jax.sharding import PartitionSpec as P

KSIZE = 7
TOP = 2
IMG_W = 16
IMG_H = 8


EPS = 1e-06


def front(images, conv_weight, conv_bias, ln_gain, ln_shift):
    half = KSIZE // 2
    padded = jnp.pad(images, ((0, 0), (half, half), (half, half), (0, 0)))
    total = jnp.zeros_like(images) + conv_bias
    for row in range(KSIZE):
        for col in range(KSIZE):
            total = (
                total
                + padded[:, row : row + IMG_H, col : col + IMG_W, :]
                * conv_weight[row * KSIZE + col]
            )
    mean = jnp.mean(total, axis=-1, keepdims=True)
    centred = total - mean
    spread = jnp.mean(centred * centred, axis=-1, keepdims=True)
    return centred * lax.rsqrt(spread + EPS) * ln_gain + ln_shift


def slot_positions(ids, capacity, count):
    flat = ids.reshape(-1)
    table = (flat[:, None] == jnp.arange(count, dtype=jnp.int32)[None, :]).astype(jnp.int32)
    earlier = jnp.cumsum(table, axis=0) - table
    slots = jnp.sum(earlier * table, axis=1)
    return (flat * capacity + slots).reshape(ids.shape)


def contract_last(left, right):
    return lax.dot_general(
        left, right, (((1,), (1,)), ((), ())), preferred_element_type=jnp.float32
    )


def contract_first(left, right):
    return lax.dot_general(
        left, right, (((0,), (0,)), ((), ())), preferred_element_type=jnp.float32
    )


def local(
    patches,
    expert_ids,
    gate_weights,
    conv_weight,
    conv_bias,
    ln_gain,
    ln_shift,
    w_in,
    w_out,
    grad_mixed,
):
    tokens_here = patches.shape[0]
    width = patches.shape[1]
    hid_width = w_in.shape[2]
    experts = lax.axis_size("expert")
    capacity = 4 * tokens_here // experts
    shaped = partial(
        front, conv_weight=conv_weight, conv_bias=conv_bias, ln_gain=ln_gain, ln_shift=ln_shift
    )
    images = patches.astype(jnp.float32).reshape(1, IMG_H, IMG_W, width)
    pre, back_front = jax.vjp(shaped, images)
    normed = pre.reshape(tokens_here, width).astype(jnp.bfloat16)
    positions = slot_positions(expert_ids, capacity, experts)
    all_slots = jnp.arange(experts * capacity, dtype=jnp.int32)
    hits = positions[None, :, :] == all_slots[:, None, None]
    select = jnp.sum(hits.astype(jnp.float32), axis=2).astype(jnp.bfloat16)
    sent = jnp.dot(select, normed, preferred_element_type=jnp.float32).astype(jnp.bfloat16)
    sent = sent.reshape(experts, capacity, width)
    full_in, full_out = (
        lax.all_gather(w_in, "dp", axis=1, tiled=True),
        lax.all_gather(w_out, "dp", axis=1, tiled=True),
    )
    full_in = full_in[0]
    full_out = full_out[0]
    rows = lax.all_to_all(sent, "expert", split_axis=0, concat_axis=0, tiled=True)
    sources = rows.shape[0]
    count = rows.shape[1]
    flat = rows.reshape(sources * count, width)
    hidden_pre = jnp.dot(flat, full_in, preferred_element_type=jnp.float32)
    hidden = jax.nn.gelu(hidden_pre).astype(jnp.bfloat16)
    result = contract_last(hidden, full_out).astype(jnp.bfloat16).reshape(sources, count, width)
    returned = lax.all_to_all(result, "expert", split_axis=0, concat_axis=0, tiled=True)
    returned, received, hidden_pre, hidden = (
        returned,
        rows,
        hidden_pre.reshape(sources, count, hid_width),
        hidden.reshape(sources, count, hid_width),
    )
    back_flat = returned.reshape(experts * capacity, width)
    picked = (
        jnp.take(back_flat, positions.reshape(-1), axis=0)
        .reshape(tokens_here, TOP, width)
        .astype(jnp.float32)
    )
    combined = jnp.sum(picked * gate_weights[:, :, None], axis=1)
    mixed = (patches.astype(jnp.float32) + combined).astype(jnp.bfloat16)
    gated_pairs = (gate_weights[:, :, None] * grad_mixed.astype(jnp.float32)[:, None, :]).astype(
        jnp.bfloat16
    )
    gated_pairs = gated_pairs.reshape(tokens_here * TOP, width)
    pair_select = hits.reshape(experts * capacity, tokens_here * TOP).astype(jnp.bfloat16)
    grad_sent = jnp.dot(pair_select, gated_pairs, preferred_element_type=jnp.float32).astype(
        jnp.bfloat16
    )
    grad_rows = lax.all_to_all(
        grad_sent.reshape(experts, capacity, width),
        "expert",
        split_axis=0,
        concat_axis=0,
        tiled=True,
    )
    row_count = grad_rows.shape[0] * grad_rows.shape[1]
    grad_flat = grad_rows.reshape(row_count, width)
    recv_flat = received.reshape(row_count, width)
    pre_flat = hidden_pre.reshape(row_count, hid_width)
    hidden_flat = hidden.reshape(row_count, hid_width)
    raw = jnp.dot(
        grad_flat,
        lax.all_gather(w_out, "dp", axis=1, tiled=True)[0],
        preferred_element_type=jnp.float32,
    )
    grad_hidden = jax.vjp(jax.nn.gelu, pre_flat)[1](raw)[0].astype(jnp.bfloat16)
    grad_back = contract_last(grad_hidden, lax.all_gather(w_in, "dp", axis=1, tiled=True)[0])
    term_in = contract_first(recv_flat, grad_hidden)
    term_out = contract_first(grad_flat, hidden_flat)
    both_grads = lax.psum_scatter(
        jnp.concatenate([term_in, term_out], axis=1).astype(jnp.bfloat16),
        "dp",
        scatter_dimension=0,
        tiled=True,
    ).astype(jnp.float32)
    grad_w_in = both_grads[:, :hid_width][None]
    grad_w_out = both_grads[:, hid_width:][None]
    grad_back = grad_back.astype(jnp.bfloat16).reshape(
        grad_rows.shape[0], grad_rows.shape[1], width
    )
    grad_returned = lax.all_to_all(grad_back, "expert", split_axis=0, concat_axis=0, tiled=True)
    picked_grad = jnp.take(
        grad_returned.reshape(experts * capacity, width), positions.reshape(-1), axis=0
    )
    grad_normed = jnp.sum(picked_grad.reshape(tokens_here, TOP, width).astype(jnp.float32), axis=1)
    grad_front = back_front(grad_normed.reshape(1, IMG_H, IMG_W, width))[0]
    grad_input = grad_mixed.astype(jnp.float32) + grad_front.reshape(tokens_here, width)
    return (mixed, grad_input, grad_w_in, grad_w_out)


def solution(mesh):
    placed = (
        P(("dp", "expert"), None),
        P(("dp", "expert"), None),
        P(("dp", "expert"), None),
        P(),
        P(),
        P(),
        P(),
        P("expert", "dp", None),
        P("expert", "dp", None),
        P(("dp", "expert"), None),
    )
    return jax.shard_map(
        local,
        mesh=mesh,
        in_specs=placed,
        out_specs=(
            P(("dp", "expert"), None),
            P(("dp", "expert"), None),
            P("expert", "dp", None),
            P("expert", "dp", None),
        ),
        check_vma=False,
    )
```

profile of v0, /device:TPU:1, one launch (start us, length us, event | category | flops | bytes accessed | tf_op | source)
XLA Modules:
  0.0 277.6 jit_solution(14860297189709608677)
XLA Ops:
  12.0 1.4 fusion.133
  13.5 1.4 fusion.134
  15.9 5.0 %fusion.131 = (f32[8,16]{1,0:T(8,128)S(1)}, f32[1,8,16,1024]{3,2,1,0:T(8,128)S(1)}) fusion(f32[1024]{0:T(1024)S(1)} %bitcast.198, f32[1024]{0:T(1024)S(1)} %bitcast.144, f32[1024]{0:T(1024)S(1)} %bitcast.162, f32[1024]{0:T(1024)S(1)} %bitcast.202, f32[1024]{0:T(1024)S(1)} %bitcast.204, f32[1024]{0:T(1024)S(1)} %bitcast.206, f32[1024]{0:T(1024)S(1)} %bitcast.208, ...), kind=kLoop, calls=%fused_computation.267 | loop fusion | flops 12976000 | bytes 1253888 | tf_op jit(solution)/shard_map/jvp()/reduce_sum | solution.py:28
  21.3 1.4 convolution_convert_fusion.2
  22.9 13.0 %all-to-all-start = ((bf16[32,16,1024]{2,1,0:T(8,128)(2,1)}), bf16[32,16,1024]{2,1,0:T(8,128)(2,1)S(1)}, u32[]{:S(2)}, u32[]{:S(2)}) async-start(bf16[32,16,1024]{2,1,0:T(8,128)(2,1)} %bitcast.52), calls=%async_computation | async-start | bytes 2097152 | tf_op jit(solution)/shard_map/all_to_all | solution.py:89
  36.7 1.5 bitcast_convert_fusion
  38.2 26.6 %all-to-all-done = bf16[32,16,1024]{2,1,0:T(8,128)(2,1)S(1)} async-done(((bf16[32,16,1024]{2,1,0:T(8,128)(2,1)}), bf16[32,16,1024]{2,1,0:T(8,128)(2,1)S(1)}, u32[]{:S(2)}, u32[]{:S(2)}) %all-to-all-start) | async-done | bytes 1048608 | tf_op jit(solution)/shard_map/all_to_all | solution.py:89
  64.7 4.2 %all-to-all-start.2 = ((bf16[32,16,1024]{2,1,0:T(8,128)(2,1)}), bf16[32,16,1024]{2,1,0:T(8,128)(2,1)S(1)}, u32[]{:S(2)}, u32[]{:S(2)}) async-start(bf16[32,16,1024]{2,1,0:T(8,128)(2,1)} %bitcast.59), calls=%async_computation.2 | async-start | bytes 2097152 | tf_op jit(solution)/shard_map/all_to_all | solution.py:119
  69.2 14.3 %all-gather.3.cloned.1.call-done = bf16[1,1024,1024]{2,1,0:T(8,128)(2,1)} async-done(((bf16[1,64,1024]{2,1,0:T(8,128)(2,1)}), bf16[1,1024,1024]{2,1,0:T(8,128)(2,1)}) %all-gather.3.cloned.1.call-update) | async-done | bytes 2097168 | tf_op jit(solution)/shard_map/all_gather | solution.py:84
  83.5 4.2 %fusion.13 = f32[512,1024]{1,0:T(8,128)} fusion(bf16[512,1024]{1,0:T(8,128)(2,1)S(1)} %bitcast.120, bf16[1,1024,1024]{2,1,0:T(8,128)(2,1)} %all-gather.3.cloned.1.call-done), kind=kOutput, calls=%fused_computation.67 | convolution fusion | flops 1073741824 | bytes 5242880 | tf_op jit(solution)/shard_map/dot_general | solution.py:93
  87.7 9.4 %all-to-all-done.2 = bf16[32,16,1024]{2,1,0:T(8,128)(2,1)S(1)} async-done(((bf16[32,16,1024]{2,1,0:T(8,128)(2,1)}), bf16[32,16,1024]{2,1,0:T(8,128)(2,1)S(1)}, u32[]{:S(2)}, u32[]{:S(2)}) %all-to-all-start.2) | async-done | bytes 1048608 | tf_op jit(solution)/shard_map/all_to_all | solution.py:119
  98.0 3.4 %convolution_convert_fusion = bf16[1024,1024]{0,1:T(8,128)(2,1)S(1)} fusion(bf16[512,1024]{1,0:T(8,128)(2,1)} %bitcast.123, f32[512,1024]{1,0:T(8,128)} %fusion.13), kind=kOutput, calls=%fused_computation.70 | convolution fusion | flops 1079508992 | bytes 5242880 | tf_op jit(solution)/shard_map/dot_general | solution.py:49
  101.4 47.9 %all-gather.5.cloned.1.call-done = bf16[1,1024,1024]{2,1,0:T(8,128)(2,1)} async-done(((bf16[1,64,1024]{2,1,0:T(8,128)(2,1)}), bf16[1,1024,1024]{2,1,0:T(8,128)(2,1)}) %all-gather.5.cloned.1.call-update) | async-done | bytes 2097168 | tf_op jit(solution)/shard_map/all_gather | solution.py:85
  149.3 4.9 %fusion.6 = bf16[512,1024]{1,0:T(8,128)(2,1)S(1)} fusion(f32[512,1024]{1,0:T(8,128)} %fusion.13, bf16[512,1024]{1,0:T(8,128)(2,1)} %bitcast.124, bf16[1,1024,1024]{2,1,0:T(8,128)(2,1)} %all-gather.5.cloned.1.call-done), kind=kOutput, calls=%fused_computation.59 | convolution fusion | flops 1084227584 | bytes 6291456 | tf_op jit(solution)/shard_map/dot_general | solution.py:131
  155.2 1.3 convolution_convert_fusion.1
  156.5 2.5 pad_maximum_fusion
  159.0 6.5 %copy.42 = bf16[1024,2048]{1,0:T(8,128)(2,1)} copy(bf16[1024,2048]{0,1:T(8,128)(2,1)} %pad_maximum_fusion) | data formatting | bytes 8388608
  165.5 1.6 copy-done.45
  167.1 4.0 %fusion.20 = bf16[512,1024]{1,0:T(8,128)(2,1)} fusion(bf16[1,1024,1024]{2,1,0:T(8,128)(2,1)S(1)} %copy-done.45, f32[512,1024]{1,0:T(8,128)} %fusion.13), kind=kOutput, calls=%fused_computation.74 | convolution fusion | flops 1078984704 | bytes 5242880 | tf_op jit(solution)/shard_map/dot_general | solution.py:43
  171.1 8.9 %all-to-all-start.1 = ((bf16[32,16,1024]{2,1,0:T(8,128)(2,1)}), bf16[32,16,1024]{2,1,0:T(8,128)(2,1)S(1)}, u32[]{:S(2)}, u32[]{:S(2)}) async-start(bf16[32,16,1024]{2,1,0:T(8,128)(2,1)} %bitcast.56), calls=%async_computation.1 | async-start | bytes 2097152 | tf_op jit(solution)/shard_map/all_to_all | solution.py:96
  180.0 3.9 %fusion.17 = bf16[512,1024]{1,0:T(8,128)(2,1)} fusion(bf16[512,1024]{1,0:T(8,128)(2,1)S(1)} %copy-done.47, bf16[1,1024,1024]{2,1,0:T(8,128)(2,1)} %all-gather.3.cloned.1.call-done), kind=kOutput, calls=%fused_computation.73 | convolution fusion | flops 1074266112 | bytes 4194304 | tf_op jit(solution)/shard_map/dot_general | solution.py:43
  183.9 27.2 %all-to-all-done.1 = bf16[32,16,1024]{2,1,0:T(8,128)(2,1)S(1)} async-done(((bf16[32,16,1024]{2,1,0:T(8,128)(2,1)}), bf16[32,16,1024]{2,1,0:T(8,128)(2,1)S(1)}, u32[]{:S(2)}, u32[]{:S(2)}) %all-to-all-start.1) | async-done | bytes 1048608 | tf_op jit(solution)/shard_map/all_to_all | solution.py:96
  211.1 4.3 %all-to-all-start.3 = ((bf16[32,16,1024]{2,1,0:T(8,128)(2,1)}), bf16[32,16,1024]{2,1,0:T(8,128)(2,1)S(1)}, u32[]{:S(2)}, u32[]{:S(2)}) async-start(bf16[32,16,1024]{2,1,0:T(8,128)(2,1)} %bitcast.122), calls=%async_computation.3 | async-start | bytes 2097152 | tf_op jit(solution)/shard_map/all_to_all | solution.py:151
  216.6 1.3 gather_fusion
  217.9 25.9 %all-to-all-done.3 = bf16[32,16,1024]{2,1,0:T(8,128)(2,1)S(1)} async-done(((bf16[32,16,1024]{2,1,0:T(8,128)(2,1)}), bf16[32,16,1024]{2,1,0:T(8,128)(2,1)S(1)}, u32[]{:S(2)}, u32[]{:S(2)}) %all-to-all-start.3) | async-done | bytes 1048608 | tf_op jit(solution)/shard_map/all_to_all | solution.py:151
  243.8 2.1 gather_fusion.1
  245.9 1.2 select_convert_fusion
  247.2 1.6 reshape.335
  248.8 1.6 reshape.334
  252.0 1.6 fusion.23
  257.6 5.8 %pad_add_fusion = f32[1,14,22,1024]{3,2,1,0:T(8,128)S(1)} fusion(f32[1,8,16,1024]{3,2,1,0:T(8,128)S(1)} %get-tuple-element.35, f32[1,8,16,1024]{3,2,1,0:T(8,128)S(1)} %get-tuple-element.36, f32[1,8,16,1024]{3,2,1,0:T(8,128)S(1)} %get-tuple-element.37, f32[1,8,16,1024]{3,2,1,0:T(8,128)S(1)} %get-tuple-element.38, ...), kind=kLoop, calls=%fused_computation.75 | loop fusion | flops 13246464 | bytes 23805952 | tf_op jit(solution)/shard_map/transpose(jvp())/add_any | solution.py:25
  265.4 2.5 reduce-scatter.4.cloned.1.call-done
  (139 shorter events, 20.7 us)
Async XLA Ops:
  7.2 8.7 %copy-start.41 = (f32[1024]{0:T(1024)S(1)}, f32[1024]{0:T(1024)}, u32[]{:S(2)}) copy-start(f32[1024]{0:T(1024)} %param.16) | copy-start | bytes 12292
  7.2 14.0 %copy-start.6 = (f32[1024]{0:T(1024)S(1)}, f32[1024]{0:T(1024)}, u32[]{:S(2)}) copy-start(f32[1024]{0:T(1024)} %param.17) | copy-start | bytes 12292
  7.2 14.0 %copy-start.42 = (f32[1024]{0:T(1024)S(1)}, f32[1024]{0:T(1024)}, u32[]{:S(2)}) copy-start(f32[1024]{0:T(1024)} %param.18) | copy-start | bytes 12292
  7.2 76.3 %all-gather.3.cloned.1.call-start = ((), (), s32[]{:S(2)}) async-start(), calls=%async_computation.5 | async-start | bytes 2228224 | tf_op jit(solution)/shard_map/all_gather | solution.py:84
  12.0 10.8 %copy-start.13 = (f32[1,1024]{1,0:T(1,128)}, f32[1,1024]{1,0:T(1,128)S(1)}, u32[]{:S(2)}) copy-start(f32[1,1024]{1,0:T(1,128)S(1)} %get-tuple-element.124) | copy-start | bytes 12292
  13.4 7.5 %copy-start.17 = (f32[1,1024]{1,0:T(1,128)}, f32[1,1024]{1,0:T(1,128)S(1)}, u32[]{:S(2)}) copy-start(f32[1,1024]{1,0:T(1,128)S(1)} %get-tuple-element.77) | copy-start | bytes 12292
  13.4 9.4 %copy-start.19 = (f32[1,1024]{1,0:T(1,128)}, f32[1,1024]{1,0:T(1,128)S(1)}, u32[]{:S(2)}) copy-start(f32[1,1024]{1,0:T(1,128)S(1)} %get-tuple-element.79) | copy-start | bytes 12292
  13.4 9.4 %copy-start.21 = (f32[1,1024]{1,0:T(1,128)}, f32[1,1024]{1,0:T(1,128)S(1)}, u32[]{:S(2)}) copy-start(f32[1,1024]{1,0:T(1,128)S(1)} %get-tuple-element.80) | copy-start | bytes 12292
  13.4 9.4 %copy-start.23 = (f32[1,1024]{1,0:T(1,128)}, f32[1,1024]{1,0:T(1,128)S(1)}, u32[]{:S(2)}) copy-start(f32[1,1024]{1,0:T(1,128)S(1)} %get-tuple-element.81) | copy-start | bytes 12292
  13.4 9.4 %copy-start.25 = (f32[1,1024]{1,0:T(1,128)}, f32[1,1024]{1,0:T(1,128)S(1)}, u32[]{:S(2)}) copy-start(f32[1,1024]{1,0:T(1,128)S(1)} %get-tuple-element.82) | copy-start | bytes 12292
  13.4 9.4 %copy-start.27 = (f32[1,1024]{1,0:T(1,128)}, f32[1,1024]{1,0:T(1,128)S(1)}, u32[]{:S(2)}) copy-start(f32[1,1024]{1,0:T(1,128)S(1)} %get-tuple-element.83) | copy-start | bytes 12292
  13.4 9.4 %copy-start.29 = (f32[1,1024]{1,0:T(1,128)}, f32[1,1024]{1,0:T(1,128)S(1)}, u32[]{:S(2)}) copy-start(f32[1,1024]{1,0:T(1,128)S(1)} %get-tuple-element.84) | copy-start | bytes 12292
  13.4 9.4 %copy-start.31 = (f32[1,1024]{1,0:T(1,128)}, f32[1,1024]{1,0:T(1,128)S(1)}, u32[]{:S(2)}) copy-start(f32[1,1024]{1,0:T(1,128)S(1)} %get-tuple-element.85) | copy-start | bytes 12292
  13.4 9.4 %copy-start.33 = (f32[1,1024]{1,0:T(1,128)}, f32[1,1024]{1,0:T(1,128)S(1)}, u32[]{:S(2)}) copy-start(f32[1,1024]{1,0:T(1,128)S(1)} %get-tuple-element.86) | copy-start | bytes 12292
  13.5 9.4 %copy-start.35 = (f32[1,1024]{1,0:T(1,128)}, f32[1,1024]{1,0:T(1,128)S(1)}, u32[]{:S(2)}) copy-start(f32[1,1024]{1,0:T(1,128)S(1)} %get-tuple-element.87) | copy-start | bytes 12292
  13.5 9.4 %copy-start.37 = (f32[1,1024]{1,0:T(1,128)}, f32[1,1024]{1,0:T(1,128)S(1)}, u32[]{:S(2)}) copy-start(f32[1,1024]{1,0:T(1,128)S(1)} %get-tuple-element.88) | copy-start | bytes 12292
  13.5 9.4 %copy-start.39 = (f32[1,1024]{1,0:T(1,128)}, f32[1,1024]{1,0:T(1,128)S(1)}, u32[]{:S(2)}) copy-start(f32[1,1024]{1,0:T(1,128)S(1)} %get-tuple-element.89) | copy-start | bytes 12292
  14.9 6.0 %copy-start.7 = (f32[1,1024]{1,0:T(1,128)}, f32[1,1024]{1,0:T(1,128)S(1)}, u32[]{:S(2)}) copy-start(f32[1,1024]{1,0:T(1,128)S(1)} %get-tuple-element.105) | copy-start | bytes 12292
  14.9 8.0 %copy-start.9 = (f32[1,1024]{1,0:T(1,128)}, f32[1,1024]{1,0:T(1,128)S(1)}, u32[]{:S(2)}) copy-start(f32[1,1024]{1,0:T(1,128)S(1)} %get-tuple-element.106) | copy-start | bytes 12292
  14.9 8.0 %copy-start.11 = (f32[1,1024]{1,0:T(1,128)}, f32[1,1024]{1,0:T(1,128)S(1)}, u32[]{:S(2)}) copy-start(f32[1,1024]{1,0:T(1,128)S(1)} %get-tuple-element.107) | copy-start | bytes 12292
  21.1 15.5 %copy-start.2 = (bf16[128,1024]{1,0:T(8,128)(2,1)S(1)}, bf16[128,1024]{1,0:T(8,128)(2,1)}, u32[]{:S(2)}) copy-start(bf16[128,1024]{1,0:T(8,128)(2,1)} %param.21) | copy-start | bytes 786436
  21.3 15.4 %copy-start.43 = (f32[128,2]{0,1:T(2,128)S(1)}, f32[128,2]{0,1:T(2,128)}, u32[]{:S(2)}) copy-start(f32[128,2]{0,1:T(2,128)} %param.14) | copy-start | bytes 3076
  22.9 41.9 %all-to-all-start = ((bf16[32,16,1024]{2,1,0:T(8,128)(2,1)}), bf16[32,16,1024]{2,1,0:T(8,128)(2,1)S(1)}, u32[]{:S(2)}, u32[]{:S(2)}) async-start(bf16[32,16,1024]{2,1,0:T(8,128)(2,1)} %bitcast.52), calls=%async_computation | async-start | bytes 2097152 | tf_op jit(solution)/shard_map/all_to_all | solution.py:89
  35.9 113.5 %all-gather.5.cloned.1.call-start = ((), (), s32[]{:S(2)}) async-start(), calls=%async_computation.6 | async-start | bytes 2228224 | tf_op jit(solution)/shard_map/all_gather | solution.py:85
  64.7 22.9 %copy-start.3 = (bf16[32,16,1024]{2,1,0:T(8,128)(2,1)}, bf16[32,16,1024]{2,1,0:T(8,128)(2,1)S(1)}, u32[]{:S(2)}) copy-start(bf16[32,16,1024]{2,1,0:T(8,128)(2,1)S(1)} %all-to-all-done) | copy-start | bytes 3145732
  64.7 32.3 %all-to-all-start.2 = ((bf16[32,16,1024]{2,1,0:T(8,128)(2,1)}), bf16[32,16,1024]{2,1,0:T(8,128)(2,1)S(1)}, u32[]{:S(2)}, u32[]{:S(2)}) async-start(bf16[32,16,1024]{2,1,0:T(8,128)(2,1)} %bitcast.59), calls=%async_computation.2 | async-start | bytes 2097152 | tf_op jit(solution)/shard_map/all_to_all | solution.py:119
  68.9 199.0 %reduce-scatter.4.cloned.1.call-start = ((), (), s32[]{:S(2)}) async-start(), calls=%async_computation.7 | async-start | bytes 4456448
  149.3 5.9 %copy-start.4 = (bf16[32,16,1024]{2,1,0:T(8,128)(2,1)S(1)}, bf16[32,16,1024]{2,1,0:T(8,128)(2,1)}, u32[]{:S(2)}) copy-start(bf16[32,16,1024]{2,1,0:T(8,128)(2,1)} %copy-done.3) | copy-start | bytes 3145732
  171.1 8.9 %copy-start.47 = (bf16[512,1024]{1,0:T(8,128)(2,1)S(1)}, bf16[512,1024]{1,0:T(8,128)(2,1)}, u32[]{:S(2)}) copy-start(bf16[512,1024]{1,0:T(8,128)(2,1)} %copy-done.46) | copy-start | bytes 3145732
  171.1 40.0 %all-to-all-start.1 = ((bf16[32,16,1024]{2,1,0:T(8,128)(2,1)}), bf16[32,16,1024]{2,1,0:T(8,128)(2,1)S(1)}, u32[]{:S(2)}, u32[]{:S(2)}) async-start(bf16[32,16,1024]{2,1,0:T(8,128)(2,1)} %bitcast.56), calls=%async_computation.1 | async-start | bytes 2097152 | tf_op jit(solution)/shard_map/all_to_all | solution.py:96
  211.1 32.7 %all-to-all-start.3 = ((bf16[32,16,1024]{2,1,0:T(8,128)(2,1)}), bf16[32,16,1024]{2,1,0:T(8,128)(2,1)S(1)}, u32[]{:S(2)}, u32[]{:S(2)}) async-start(bf16[32,16,1024]{2,1,0:T(8,128)(2,1)} %bitcast.122), calls=%async_computation.3 | async-start | bytes 2097152 | tf_op jit(solution)/shard_map/all_to_all | solution.py:151
  250.4 3.2 %copy-start.16 = (f32[8,16]{1,0:T(8,128)S(1)}, f32[8,16]{1,0:T(8,128)}, u32[]{:S(2)}) copy-start(f32[8,16]{1,0:T(8,128)} %copy-done.15) | copy-start | bytes 1540
  (23 other events, 43.2 us)
Sparse Core Ops, SparseCore 0:
  11.0 72.4 all-gather.2
  86.5 62.7 all-gather.4
  165.7 102.1 reduce-scatter.3
where the time goes:
time: 279 us; the launch traced here: 278 us
  waiting for transfers between devices  155 us (56%)
  starting transfers between devices  30.7 us (11%)
  other arithmetic  26.8 us (10%)
  local copies, waits for them, and re-layouts  25.8 us (9%)
  matrix products  24.5 us (9%)
  between operations  14.6 us (5%)
    all_gather x1, waiting for transfers between devices, local(): lax.all_gather(w_out, 'dp', axis=1, tiled=True)  47.9 us
    all_to_all x1, waiting for transfers between devices, local(): lax.all_to_all(result, 'expert', split_axis=0, concat_axis=0, tiled=True)  27.2 us
    all_to_all x1, waiting for transfers between devices, local(): lax.all_to_all(sent, 'expert', split_axis=0, concat_axis=0, tiled=True)  26.6 us
    all_to_all x1, waiting for transfers between devices, local(): lax.all_to_all(grad_back, 'expert', split_axis=0, concat_axis=0, tiled=True)  25.9 us
    unnamed x101, local copies, waits for them, and re-layouts  14.6 us
    all_gather x1, waiting for transfers between devices, local(): lax.all_gather(w_in, 'dp', axis=1, tiled=True)  14.3 us
    all_to_all x1, starting transfers between devices, local(): lax.all_to_all(sent, 'expert', split_axis=0, concat_axis=0, tiled=True)  13 us
    all_to_all x1, waiting for transfers between devices, local(): lax.all_to_all(grad_sent.reshape(experts, capacity, width), 'expert', spl...  9.41 us
  transfers between devices with their start and end apart: 7, of which 7 were waited for; matrix products, arithmetic and copies ran while one was open for 20% of the time, Pallas kernels for 0%

commit v1 on v0

v1 whole, which is shorter than its diff:
```python
import jax
import jax.numpy as jnp
from jax import lax
from jax.experimental import pallas as pl
from jax.experimental.pallas import tpu as pltpu
from jax.sharding import Mesh, PartitionSpec as P


KSIZE = 7
TOP = 2
IMG_W = 16
IMG_H = 8
EPS = 1e-06
EXPERTS = 32
CAP = 16
TOK = 128
SLOTS = EXPERTS * CAP
LANES = 128
F32 = jnp.float32
BF16 = jnp.bfloat16
MIB = 1 << 20

VMEM = pl.BlockSpec(memory_space=pltpu.VMEM)


def dot(a, b):
    return jnp.dot(a, b, preferred_element_type=F32)


def iota(shape, dim):
    return lax.broadcasted_iota(jnp.int32, shape, dim)


def slot_selects(ids_ref):
    turned = [
        jnp.broadcast_to(ids_ref[:, k : k + 1].astype(F32), (TOK, TOK)).T.astype(jnp.int32)
        for k in range(TOP)
    ]
    hot = [row[:EXPERTS] == iota((EXPERTS, TOK), 0) for row in turned]
    table = (hot[0] | hot[1]).astype(F32).astype(BF16)
    before = (iota((TOK, TOK), 0) < iota((TOK, TOK), 1)).astype(F32).astype(BF16)
    earlier = dot(table, before)
    out = []
    for k in range(TOP):
        slot = jnp.sum(jnp.where(hot[k], earlier, 0.0), axis=0, keepdims=True)
        position = turned[k][:1] * CAP + slot.astype(jnp.int32)
        out.append(iota((SLOTS, TOK), 0) == position)
    return out


def patch_selects(ids_ref):
    hot = [ids_ref[:, k : k + 1] == iota((TOK, EXPERTS), 1) for k in range(TOP)]
    table = (hot[0] | hot[1]).astype(F32).astype(BF16)
    before = (iota((TOK, TOK), 1) < iota((TOK, TOK), 0)).astype(F32).astype(BF16)
    earlier = dot(before, table)
    out = []
    for k in range(TOP):
        slot = jnp.sum(jnp.where(hot[k], earlier, 0.0), axis=1, keepdims=True)
        position = ids_ref[:, k : k + 1] * CAP + slot.astype(jnp.int32)
        out.append(iota((TOK, SLOTS), 1) == position)
    return out


def as_bf16(mask):
    return mask.astype(F32).astype(BF16)


def send_grads_kernel(ids_ref, gates_ref, cot_ref, out_ref):
    select = slot_selects(ids_ref)
    cot = cot_ref[...].astype(F32)
    first = (gates_ref[:, 0:1] * cot).astype(BF16)
    second = (gates_ref[:, 1:2] * cot).astype(BF16)
    out_ref[...] = (dot(as_bf16(select[0]), first) + dot(as_bf16(select[1]), second)).astype(BF16)


def depthwise(padded, taps_ref, flip, start, put):
    half = KSIZE // 2

    def chunk(c, _):
        lanes = pl.ds(pl.multiple_of(c * LANES, LANES), LANES)
        total = start(lanes)
        for col in range(KSIZE):
            begin = 8 + col - half
            shifted = padded[:, begin : begin + IMG_W, lanes]
            for row in range(KSIZE):
                tap = (KSIZE - 1 - row) * KSIZE + KSIZE - 1 - col if flip else row * KSIZE + col
                weight = taps_ref[tap : tap + 1, lanes]
                total = total + shifted[row : row + IMG_H] * weight[None]
        put(lanes, total)
        return 0

    lax.fori_loop(0, padded.shape[2] // LANES, chunk, 0)


def front_kernel(
    ids_ref, x_ref, taps_ref, bias_ref, gain_ref, shift_ref, sent_ref, xhat_ref, rstd_ref, padded, total
):
    width = x_ref.shape[1]
    half = KSIZE // 2
    padded[...] = jnp.zeros_like(padded)
    padded[half : half + IMG_H, 8 : 8 + IMG_W, :] = (
        x_ref[...].astype(F32).reshape(IMG_H, IMG_W, width)
    )

    def start(lanes):
        return jnp.broadcast_to(bias_ref[:, lanes][None], (IMG_H, IMG_W, LANES))

    def put(lanes, value):
        total[:, lanes] = value.reshape(TOK, LANES)

    depthwise(padded, taps_ref, False, start, put)
    conv = total[...]
    mean = jnp.sum(conv, axis=1, keepdims=True) * (1.0 / width)
    centred = conv - mean
    spread = jnp.sum(centred * centred, axis=1, keepdims=True) * (1.0 / width)
    rstd = lax.rsqrt(spread + EPS)
    xhat = centred * rstd
    xhat_ref[...] = xhat
    rstd_ref[...] = jnp.broadcast_to(rstd, (TOK, LANES))
    normed = (xhat * gain_ref[...] + shift_ref[...]).astype(BF16)
    select = slot_selects(ids_ref)
    sent_ref[...] = dot(as_bf16(select[0] | select[1]), normed).astype(BF16)


def back_kernel(
    ids_ref, back_ref, xhat_ref, rstd_ref, gain_ref, taps_ref, cot_ref, out_ref, padded
):
    width = xhat_ref.shape[1]
    half = KSIZE // 2
    select = patch_selects(ids_ref)
    grad = dot(as_bf16(select[0] | select[1]), back_ref[...])
    grad = grad * gain_ref[...]
    xhat = xhat_ref[...]
    mean = jnp.sum(grad, axis=1, keepdims=True) * (1.0 / width)
    along = jnp.sum(grad * xhat, axis=1, keepdims=True) * (1.0 / width)
    grad = rstd_ref[:, 0:1] * (grad - mean - xhat * along)
    padded[...] = jnp.zeros_like(padded)
    padded[half : half + IMG_H, 8 : 8 + IMG_W, :] = grad.reshape(IMG_H, IMG_W, width)

    def start(lanes):
        return jnp.zeros((IMG_H, IMG_W, LANES), F32)

    def put(lanes, value):
        out_ref[:, lanes] = cot_ref[:, lanes].astype(F32) + value.reshape(TOK, LANES)

    depthwise(padded, taps_ref, True, start, put)


def mix_kernel(ids_ref, gates_ref, back_ref, x_ref, out_ref):
    select = patch_selects(ids_ref)
    rows = back_ref[...]
    combined = gates_ref[:, 0:1] * dot(as_bf16(select[0]), rows)
    combined = combined + gates_ref[:, 1:2] * dot(as_bf16(select[1]), rows)
    out_ref[...] = (x_ref[...].astype(F32) + combined).astype(BF16)


def contract_last(left, right):
    return lax.dot_general(left, right, (((1,), (1,)), ((), ())), preferred_element_type=F32)


def contract_first(left, right):
    return lax.dot_general(left, right, (((0,), (0,)), ((), ())), preferred_element_type=F32)


SQRT_2_OVER_PI = 0.7978845608028654


def expert_kernel(rows_ref, grads_ref, w_in_ref, w_out_ref, back_ref, hidden_ref, gh_ref, total):
    step = pl.program_id(0)
    pre = dot(rows_ref[...], w_in_ref[...])
    raw = dot(grads_ref[...], w_out_ref[...])
    square = pre * pre
    t = jnp.tanh(SQRT_2_OVER_PI * (pre + 0.044715 * (pre * square)))
    cdf = 0.5 * (1.0 + t)
    hidden_ref[...] = (pre * cdf).astype(BF16)
    slope = cdf + pre * (0.5 * (1.0 - t * t)) * (
        SQRT_2_OVER_PI * (1.0 + (3 * 0.044715) * square)
    )
    gh = (raw * slope).astype(BF16)
    gh_ref[...] = gh
    part = contract_last(gh, w_in_ref[...])

    @pl.when(step == 0)
    def _():
        total[...] = part

    @pl.when(step > 0)
    def _():
        total[...] += part

    @pl.when(step == pl.num_programs(0) - 1)
    def _():
        back_ref[...] = total[...].astype(BF16)


def terms_kernel(rows_ref, grads_ref, hidden_ref, gh_ref, out_ref):
    hid = hidden_ref.shape[1]
    out_ref[:, :hid] = contract_first(rows_ref[...], gh_ref[...]).astype(BF16)
    out_ref[:, hid:] = contract_first(grads_ref[...], hidden_ref[...]).astype(BF16)


def result_kernel(hidden_ref, w_out_ref, out_ref):
    out_ref[...] = contract_last(hidden_ref[...], w_out_ref[...]).astype(BF16)


def params(mib=16):
    return pltpu.CompilerParams(vmem_limit_bytes=mib * MIB)


def cost(flops, nbytes):
    return pl.CostEstimate(flops=int(flops), bytes_accessed=int(nbytes), transcendentals=0)


def shape(dims, dtype):
    return jax.ShapeDtypeStruct(dims, dtype)


def send_grads(ids, gates, cot):
    width = cot.shape[1]
    return pl.pallas_call(
        send_grads_kernel,
        out_shape=shape((SLOTS, width), BF16),
        in_specs=[VMEM] * 3,
        out_specs=VMEM,
        compiler_params=params(),
        cost_estimate=cost(4 * SLOTS * TOK * width, 2 * SLOTS * width),
        name="send_grads",
    )(ids, gates, cot)


def front(ids, x, taps, bias, gain, shift):
    width = x.shape[1]
    return pl.pallas_call(
        front_kernel,
        out_shape=(
            shape((SLOTS, width), BF16),
            shape((TOK, width), F32),
            shape((TOK, LANES), F32),
        ),
        in_specs=[VMEM] * 6,
        out_specs=[VMEM] * 3,
        scratch_shapes=[
            pltpu.VMEM((IMG_H + KSIZE - 1, IMG_W + 16, width), F32),
            pltpu.VMEM((TOK, width), F32),
        ],
        compiler_params=params(),
        cost_estimate=cost(100 * TOK * width * 20, 4 * SLOTS * width),
        name="front",
    )(ids, x, taps, bias.reshape(1, width), gain.reshape(1, width), shift.reshape(1, width))


def back(ids, grad_rows, xhat, rstd, gain, taps, cot):
    width = cot.shape[1]
    return pl.pallas_call(
        back_kernel,
        out_shape=shape((TOK, width), F32),
        in_specs=[VMEM] * 7,
        out_specs=VMEM,
        scratch_shapes=[pltpu.VMEM((IMG_H + KSIZE - 1, IMG_W + 16, width), F32)],
        compiler_params=params(),
        cost_estimate=cost(100 * TOK * width * 20, 4 * SLOTS * width),
        name="back",
    )(ids, grad_rows, xhat, rstd, gain.reshape(1, width), taps, cot)


def mix(ids, gates, rows, x):
    width = x.shape[1]
    return pl.pallas_call(
        mix_kernel,
        out_shape=shape((TOK, width), BF16),
        in_specs=[VMEM] * 4,
        out_specs=VMEM,
        compiler_params=params(),
        cost_estimate=cost(4 * SLOTS * TOK * width, 2 * SLOTS * width),
        name="mix",
    )(ids, gates, rows, x)


def expert(rows, grads, weights):
    count, width = rows.shape
    hid = weights.shape[1] // 2
    block = 256
    steps = hid // block
    whole = pl.BlockSpec((count, width), lambda j: (0, 0))
    return pl.pallas_call(
        expert_kernel,
        grid=(steps,),
        out_shape=(
            shape((count, width), BF16),
            shape((count, hid), BF16),
            shape((count, hid), BF16),
        ),
        in_specs=[
            whole,
            whole,
            pl.BlockSpec((width, block), lambda j: (0, j)),
            pl.BlockSpec((width, block), lambda j: (0, j + steps)),
        ],
        out_specs=[
            whole,
            pl.BlockSpec((count, block), lambda j: (0, j)),
            pl.BlockSpec((count, block), lambda j: (0, j)),
        ],
        scratch_shapes=[pltpu.VMEM((count, width), F32)],
        compiler_params=params(32),
        cost_estimate=cost(6 * count * width * hid, 4 * MIB),
        name="expert",
    )(rows, grads, weights, weights)


def terms(rows, grads, hidden, gh):
    count, width = rows.shape
    hid = hidden.shape[1]
    block = 256
    part = pl.BlockSpec((count, block), lambda i: (0, i))
    whole = pl.BlockSpec((count, hid), lambda i: (0, 0))
    return pl.pallas_call(
        terms_kernel,
        grid=(width // block,),
        out_shape=shape((width, 2 * hid), BF16),
        in_specs=[part, part, whole, whole],
        out_specs=pl.BlockSpec((block, 2 * hid), lambda i: (i, 0)),
        compiler_params=params(32),
        cost_estimate=cost(4 * count * width * hid, 4 * MIB),
        name="terms",
    )(rows, grads, hidden, gh)


def result_rows(hidden, weights):
    count, hid = hidden.shape
    width = weights.shape[0]
    block = 256
    return pl.pallas_call(
        result_kernel,
        grid=(width // block,),
        out_shape=shape((count, width), BF16),
        in_specs=[
            pl.BlockSpec((count, hid), lambda i: (0, 0)),
            pl.BlockSpec((block, hid), lambda i: (i, 1)),
        ],
        out_specs=pl.BlockSpec((count, block), lambda i: (0, i)),
        compiler_params=params(),
        cost_estimate=cost(2 * count * width * hid, 4 * MIB),
        name="result",
    )(hidden, weights)


def exchange(rows, axes):
    count, width = rows.shape
    out = lax.all_to_all(
        rows.reshape(EXPERTS, CAP, width), axes, split_axis=0, concat_axis=0, tiled=True
    )
    return out.reshape(count, width)


def scatter_sum(partial):
    over_x = lax.psum_scatter(partial, "x", scatter_dimension=0, tiled=True)
    parts = lax.axis_size("yh")
    own = lax.axis_index("yh")
    height = over_x.shape[0] // parts

    def piece(which):
        return lax.dynamic_slice_in_dim(over_x, lax.rem(which, parts) * height, height, axis=0)

    total = piece(own).astype(F32)
    for k in (2, 1, 3):
        got = lax.ppermute(piece(own + k), "yh", [(i, (i + k) % parts) for i in range(parts)])
        total = total + got.astype(F32)
    return total


def local(
    patches,
    expert_ids,
    gate_weights,
    conv_weight,
    conv_bias,
    ln_gain,
    ln_shift,
    w_in,
    w_out,
    grad_mixed,
):
    hid = w_in.shape[2]
    dp = ("x", "yh")
    ep = ("z", "yl", "core")
    weights = lax.all_gather(jnp.concatenate([w_in, w_out], axis=2), dp, axis=1, tiled=True)[0]

    gated = send_grads(expert_ids, gate_weights, grad_mixed)
    grads = exchange(gated, ep)
    sent, xhat, rstd = front(
        expert_ids, patches, conv_weight, conv_bias, ln_gain, ln_shift
    )
    rows = exchange(sent, ep)

    grad_back, hidden, gh = expert(rows, grads, weights)
    grad_rows = exchange(grad_back, ep)
    partial = terms(rows, grads, hidden, gh)
    total = scatter_sum(partial)
    result = result_rows(hidden, weights)
    returned = exchange(result, ep)
    grad_input = back(
        expert_ids, grad_rows, xhat, rstd, ln_gain, conv_weight, grad_mixed
    )
    mixed = mix(expert_ids, gate_weights, returned, patches)
    return (mixed, grad_input, total[:, :hid][None], total[:, hid:][None])


def solution(mesh):
    fine = Mesh(mesh.devices.reshape(4, 4, 8, 2, 2), ("x", "yh", "z", "yl", "core"))
    dp = ("x", "yh")
    ep = ("z", "yl", "core")
    rows = P(dp + ep, None)
    weight = P(ep, dp, None)
    return jax.shard_map(
        local,
        mesh=fine,
        in_specs=(rows, rows, rows, P(), P(), P(), P(), weight, weight, rows),
        out_specs=(rows, rows, weight, weight),
        check_vma=False,
    )
```

time: 279 us -> 224 us (0.80)
  the two profiles are of different devices: /device:TPU:1 before, /device:TPU:16 now
where the time goes in v1:
time: 224 us; the launch traced here: 223 us
  waiting for transfers between devices  71.7 us (32%)
  blocking collectives  46.3 us (21%)
  starting transfers between devices  39.7 us (18%)
  Pallas kernels  29.3 us (13%)
  local copies, waits for them, and re-layouts  18.9 us (8%)
  between operations  14.2 us (6%)
  other arithmetic  3 us (1%)
    all_to_all x3, waiting for transfers between devices, exchange(): lax.all_to_all(rows.reshape(EXPERTS, CAP, width), axes, split_axis=0, con...  49.8 us
    all_to_all x1, blocking collectives, exchange(): lax.all_to_all(rows.reshape(EXPERTS, CAP, width), axes, split_axis=0, con...  46.3 us
    all_to_all x3, starting transfers between devices, exchange(): lax.all_to_all(rows.reshape(EXPERTS, CAP, width), axes, split_axis=0, con...  26.1 us
    unnamed x40, local copies, waits for them, and re-layouts  16.1 us
    ppermute x3, starting transfers between devices, scatter_sum(): lax.ppermute(piece(own + k), 'yh', [(i, (i + k) % parts) for i in range(p...  13.5 us
    ppermute x3, waiting for transfers between devices, scatter_sum(): lax.ppermute(piece(own + k), 'yh', [(i, (i + k) % parts) for i in range(p...  11.8 us
    reduce_scatter x1, waiting for transfers between devices, scatter_sum(): over_x = lax.psum_scatter(partial, 'x', scatter_dimension=0, tiled=True)  10 us
    pallas_call x1, Pallas kernels, expert(): pl.pallas_call(expert_kernel, grid=(steps,), out_shape=(shape((count, wid...  7.45 us
  transfers between devices with their start and end apart: 8, of which 5 were waited for; matrix products, arithmetic and copies ran while one was open for 2% of the time, Pallas kernels for 8%

profile of v1, /device:TPU:16, one launch (start us, length us, event | category | flops | bytes accessed | tf_op | source)
XLA Modules:
  0.0 223.1 jit_solution(14846830318255416515)
XLA Ops:
  7.2 1.7 pad_maximum_fusion
  9.7 0.9 copy-done.9
  10.7 0.9 copy-done.11
  13.7 6.6 %front.1 = (bf16[512,1024]{1,0:T(8,128)(2,1)}, f32[128,1024]{1,0:T(8,128)S(1)}, f32[128,128]{1,0:T(8,128)S(1)}) custom-call(s32[128,2]{1,0:T(8,128)S(1)} %copy.17.ids_ref, bf16[128,1024]{1,0:T(8,128)(2,1)S(1)} %copy-done.9, f32[49,1024]{1,0:T(8,128)S(1)} %copy-done.11, f32[1,1024]{1,0:T(1,128)S(1)} %bitcast.28, f32[1,1024]{1,0:T(1,128)S(1)} %bitcast.26, ...), custom_call_target="tpu_custom_call" | custom-call | flops 262144000 | bytes 2097152 | tf_op jit(solution)/shard_map/front/pallas_call | solution.py:233
  20.3 0.8 copy-done.7
  21.7 11.7 %all-to-all-start = ((bf16[32,16,1024]{2,1,0:T(8,128)(2,1)}), bf16[32,16,1024]{2,1,0:T(8,128)(2,1)S(1)}, u32[]{:S(2)}, u32[]{:S(2)}) async-start(bf16[32,16,1024]{2,1,0:T(8,128)(2,1)} %bitcast.3), calls=%async_computation | async-start | bytes 2097152 | tf_op jit(solution)/shard_map/all_to_all | solution.py:350
  34.3 0.9 copy-done.5
  35.2 1.0 send_grads.1
  36.2 26.4 %all-to-all-done = bf16[32,16,1024]{2,1,0:T(8,128)(2,1)S(1)} async-done(((bf16[32,16,1024]{2,1,0:T(8,128)(2,1)}), bf16[32,16,1024]{2,1,0:T(8,128)(2,1)S(1)}, u32[]{:S(2)}, u32[]{:S(2)}) %all-to-all-start) | async-done | bytes 1048608 | tf_op jit(solution)/shard_map/all_to_all | solution.py:350
  62.6 46.3 %all_to_all.20 = bf16[32,16,1024]{2,1,0:T(8,128)(2,1)S(1)} all-to-all(bf16[32,16,1024]{2,1,0:T(8,128)(2,1)S(1)} %bitcast.20), channel_id=1, replica_groups=mesh['x'=4,'yh'=4,'z'=8,'yl'=2,'core'=2] {'z','yl','core'}, dimensions={0} | all-to-all | bytes 2097152 | tf_op jit(solution)/shard_map/all_to_all | solution.py:350
  108.9 2.2 copy-done.1
  111.1 7.5 %expert.1 = (bf16[512,1024]{1,0:T(8,128)(2,1)}, bf16[512,1024]{1,0:T(8,128)(2,1)S(1)}, bf16[512,1024]{1,0:T(8,128)(2,1)S(1)}) custom-call(bf16[512,1024]{1,0:T(8,128)(2,1)S(1)} %bitcast.22, bf16[512,1024]{1,0:T(8,128)(2,1)S(1)} %bitcast.24, bf16[1024,2048]{1,0:T(8,128)(2,1)S(1)} %bitcast.16, bf16[1024,2048]{1,0:T(8,128)(2,1)S(1)} %bitcast.17), custom_call_target="tpu_custom_call" | custom-call | flops 3221225472 | bytes 4194304 | tf_op jit(solution)/shard_map/expert/pallas_call | solution.py:285
  118.5 3.3 %terms.1 = bf16[1024,2048]{1,0:T(8,128)(2,1)S(1)} custom-call(bf16[512,1024]{1,0:T(8,128)(2,1)S(1)} %bitcast.23, bf16[512,1024]{1,0:T(8,128)(2,1)S(1)} %bitcast.25, bf16[512,1024]{1,0:T(8,128)(2,1)S(1)} %get-tuple-element.11.hidden_ref, bf16[512,1024]{1,0:T(8,128)(2,1)S(1)} %get-tuple-element.15.gh_ref), custom_call_target="tpu_custom_call" | custom-call | flops 2147483648 | bytes 4194304 | tf_op jit(solution)/shard_map/terms/pallas_call | solution.py:317
  121.8 2.0 copy-done
  123.8 1.0 copy-done.3
  124.8 10.5 %all-to-all-start.3 = ((bf16[32,16,1024]{2,1,0:T(8,128)(2,1)}), bf16[32,16,1024]{2,1,0:T(8,128)(2,1)S(1)}, u32[]{:S(2)}, u32[]{:S(2)}) async-start(bf16[32,16,1024]{2,1,0:T(8,128)(2,1)} %bitcast.10), calls=%async_computation.3 | async-start | bytes 2097152 | tf_op jit(solution)/shard_map/all_to_all | solution.py:350
  135.3 2.2 copy-done.2
  137.5 3.0 %result.1 = bf16[512,1024]{1,0:T(8,128)(2,1)} custom-call(bf16[512,1024]{1,0:T(8,128)(2,1)S(1)} %copy-done.4, bf16[1024,2048]{1,0:T(8,128)(2,1)S(1)} %bitcast.18), custom_call_target="tpu_custom_call" | custom-call | flops 1073741824 | bytes 4194304 | tf_op jit(solution)/shard_map/result/pallas_call | solution.py:333
  140.5 23.4 %all-to-all-done.3 = bf16[32,16,1024]{2,1,0:T(8,128)(2,1)S(1)} async-done(((bf16[32,16,1024]{2,1,0:T(8,128)(2,1)}), bf16[32,16,1024]{2,1,0:T(8,128)(2,1)S(1)}, u32[]{:S(2)}, u32[]{:S(2)}) %all-to-all-start.3) | async-done | bytes 1048608 | tf_op jit(solution)/shard_map/all_to_all | solution.py:350
  163.9 3.9 %all-to-all-start.2 = ((bf16[32,16,1024]{2,1,0:T(8,128)(2,1)}), bf16[32,16,1024]{2,1,0:T(8,128)(2,1)S(1)}, u32[]{:S(2)}, u32[]{:S(2)}) async-start(bf16[32,16,1024]{2,1,0:T(8,128)(2,1)} %bitcast.8), calls=%async_computation.2 | async-start | bytes 2097152 | tf_op jit(solution)/shard_map/all_to_all | solution.py:350
  167.9 10.0 %reduce-scatter.2.cloned.1.call-done = bf16[256,2048]{1,0:T(8,128)(2,1)} async-done(((bf16[1024,2048]{1,0:T(8,128)(2,1)}), bf16[256,2048]{1,0:T(8,128)(2,1)}) %reduce-scatter.2.cloned.1.call-update) | async-done | bytes 1048592 | tf_op jit(solution)/shard_map/reduce_scatter | solution.py:357
  177.9 2.0 constant_dynamic-slice_fusion.2
  179.9 2.4 %collective-permute-start.2 = (bf16[64,2048]{1,0:T(8,128)(2,1)}, bf16[64,2048]{1,0:T(8,128)(2,1)}, u32[]{:S(2)}, u32[]{:S(2)}) collective-permute-start(bf16[64,2048]{1,0:T(8,128)(2,1)} %get-tuple-element.17), channel_id=1, source_target_pairs={{0,96},{32,0},{64,32},{96,64},{1,97},{33,1},{65,33},{97,65},{2,98}... | collective-permute-start | bytes 786440 | tf_op jit(solution)/shard_map/ppermute | solution.py:367
  182.3 5.5 %collective-permute-start.1 = (bf16[64,2048]{1,0:T(8,128)(2,1)}, bf16[64,2048]{1,0:T(8,128)(2,1)}, u32[]{:S(2)}, u32[]{:S(2)}) collective-permute-start(bf16[64,2048]{1,0:T(8,128)(2,1)} %get-tuple-element.18), channel_id=1, source_target_pairs={{0,32},{32,64},{64,96},{96,0},{1,33},{33,65},{65,97},{97,1},{2,34}... | collective-permute-start | bytes 786440 | tf_op jit(solution)/shard_map/ppermute | solution.py:367
  187.9 5.6 %collective-permute-start = (bf16[64,2048]{1,0:T(8,128)(2,1)}, bf16[64,2048]{1,0:T(8,128)(2,1)}, u32[]{:S(2)}, u32[]{:S(2)}) collective-permute-start(bf16[64,2048]{1,0:T(8,128)(2,1)} %get-tuple-element.16), channel_id=1, source_target_pairs={{0,64},{32,96},{64,0},{96,32},{1,65},{33,97},{65,1},{97,33},{2,66}... | collective-permute-start | bytes 786440 | tf_op jit(solution)/shard_map/ppermute | solution.py:367
  193.5 0.8 copy-done.14
  194.3 6.4 %back.1 = f32[128,1024]{1,0:T(8,128)} custom-call(s32[128,2]{1,0:T(8,128)S(1)} %copy.17.ids_ref, bf16[512,1024]{1,0:T(8,128)(2,1)S(1)} %bitcast.19, f32[128,1024]{1,0:T(8,128)S(1)} %copy-done.8, f32[128,128]{1,0:T(8,128)S(1)} %copy-done.14, f32[1,1024]{1,0:T(1,128)S(1)} %bitcast.27, f32[49,1024]{1,0:T(8,128)S(1)} %copy-done.12, bf16[128,1024]{1,0:T(8,128)(2,1)S(1)} %copy-done.6), custom_call_target="tpu_custom_call" | custom-call | flops 262144000 | bytes 2097152 | tf_op jit(solution)/shard_map/back/pallas_call | solution.py:254
  200.8 1.5 mix.1
  202.3 2.9 %collective-permute-done.1 = bf16[64,2048]{1,0:T(8,128)(2,1)} collective-permute-done((bf16[64,2048]{1,0:T(8,128)(2,1)}, bf16[64,2048]{1,0:T(8,128)(2,1)}, u32[]{:S(2)}, u32[]{:S(2)}) %collective-permute-start.1) | collective-permute-done | bytes 262176 | tf_op jit(solution)/shard_map/ppermute | solution.py:367
  205.2 8.9 %collective-permute-done = bf16[64,2048]{1,0:T(8,128)(2,1)} collective-permute-done((bf16[64,2048]{1,0:T(8,128)(2,1)}, bf16[64,2048]{1,0:T(8,128)(2,1)}, u32[]{:S(2)}, u32[]{:S(2)}) %collective-permute-start) | collective-permute-done | bytes 262176 | tf_op jit(solution)/shard_map/ppermute | solution.py:367
  214.1 1.3 convert_add_fusion
  215.4 0.8 slice_bitcast_fusion
  (38 shorter events, 4.4 us)
Async XLA Ops:
  7.2 101.7 %all-gather.2.cloned.1.call-start = ((), (), s32[]{:S(2)}) async-start(), calls=%async_computation.5 | async-start | bytes 4456448 | tf_op jit(solution)/shard_map/all_gather | solution.py:387
  9.7 0.9 copy-start.9
  10.7 0.9 copy-start.11
  11.6 0.7 copy-start.15
  12.3 0.7 copy-start.17
  13.0 0.7 copy-start.18
  20.3 0.8 copy-start.7
  21.1 0.6 copy-start.13
  21.7 40.9 %all-to-all-start = ((bf16[32,16,1024]{2,1,0:T(8,128)(2,1)}), bf16[32,16,1024]{2,1,0:T(8,128)(2,1)S(1)}, u32[]{:S(2)}, u32[]{:S(2)}) async-start(bf16[32,16,1024]{2,1,0:T(8,128)(2,1)} %bitcast.3), calls=%async_computation | async-start | bytes 2097152 | tf_op jit(solution)/shard_map/all_to_all | solution.py:350
  33.4 144.5 %reduce-scatter.2.cloned.1.call-start = ((), (), s32[]{:S(2)}) async-start(), calls=%async_computation.6 | async-start | bytes 5242880 | tf_op jit(solution)/shard_map/reduce_scatter | solution.py:357
  34.3 0.9 copy-start.5
  108.9 2.2 copy-start.1
  121.8 2.0 copy-start
  123.8 1.0 copy-start.3
  124.8 10.5 %copy-start.4 = (bf16[512,1024]{1,0:T(8,128)(2,1)S(1)}, bf16[512,1024]{1,0:T(8,128)(2,1)}, u32[]{:S(2)}) copy-start(bf16[512,1024]{1,0:T(8,128)(2,1)} %copy-done.3) | copy-start | bytes 3145732
  124.8 39.1 %all-to-all-start.3 = ((bf16[32,16,1024]{2,1,0:T(8,128)(2,1)}), bf16[32,16,1024]{2,1,0:T(8,128)(2,1)S(1)}, u32[]{:S(2)}, u32[]{:S(2)}) async-start(bf16[32,16,1024]{2,1,0:T(8,128)(2,1)} %bitcast.10), calls=%async_computation.3 | async-start | bytes 2097152 | tf_op jit(solution)/shard_map/all_to_all | solution.py:350
  135.3 2.2 copy-start.2
  137.5 56.0 %copy-start.6 = (bf16[128,1024]{1,0:T(8,128)(2,1)S(1)}, bf16[128,1024]{1,0:T(8,128)(2,1)}, u32[]{:S(2)}) copy-start(bf16[128,1024]{1,0:T(8,128)(2,1)} %cot_ref.3) | copy-start | bytes 786436
  137.5 56.0 %copy-start.8 = (f32[128,1024]{1,0:T(8,128)S(1)}, f32[128,1024]{1,0:T(8,128)}, u32[]{:S(2)}) copy-start(f32[128,1024]{1,0:T(8,128)} %copy-done.7) | copy-start | bytes 1572868
  137.5 56.0 %copy-start.12 = (f32[49,1024]{1,0:T(8,128)S(1)}, f32[49,1024]{1,0:T(8,128)}, u32[]{:S(2)}) copy-start(f32[49,1024]{1,0:T(8,128)} %taps_ref.3) | copy-start | bytes 602116
  137.5 56.0 %copy-start.16 = (f32[1024]{0:T(1024)S(1)}, f32[1024]{0:T(1024)}, u32[]{:S(2)}) copy-start(f32[1024]{0:T(1024)} %param.15) | copy-start | bytes 12292
  140.5 60.3 %copy-start.10 = (bf16[128,1024]{1,0:T(8,128)(2,1)S(1)}, bf16[128,1024]{1,0:T(8,128)(2,1)}, u32[]{:S(2)}) copy-start(bf16[128,1024]{1,0:T(8,128)(2,1)} %x_ref.3) | copy-start | bytes 786436
  163.9 36.9 %all-to-all-start.2 = ((bf16[32,16,1024]{2,1,0:T(8,128)(2,1)}), bf16[32,16,1024]{2,1,0:T(8,128)(2,1)S(1)}, u32[]{:S(2)}, u32[]{:S(2)}) async-start(bf16[32,16,1024]{2,1,0:T(8,128)(2,1)} %bitcast.8), calls=%async_computation.2 | async-start | bytes 2097152 | tf_op jit(solution)/shard_map/all_to_all | solution.py:350
  179.9 22.4 %collective-permute-start.2 = (bf16[64,2048]{1,0:T(8,128)(2,1)}, bf16[64,2048]{1,0:T(8,128)(2,1)}, u32[]{:S(2)}, u32[]{:S(2)}) collective-permute-start(bf16[64,2048]{1,0:T(8,128)(2,1)} %get-tuple-element.17), channel_id=1, source_target_pairs={{0,96},{32,0},{64,32},{96,64},{1,97},{33,1},{65,33},{97,65},{2,98}... | collective-permute-start | bytes 786440 | tf_op jit(solution)/shard_map/ppermute | solution.py:367
  182.3 22.8 %collective-permute-start.1 = (bf16[64,2048]{1,0:T(8,128)(2,1)}, bf16[64,2048]{1,0:T(8,128)(2,1)}, u32[]{:S(2)}, u32[]{:S(2)}) collective-permute-start(bf16[64,2048]{1,0:T(8,128)(2,1)} %get-tuple-element.18), channel_id=1, source_target_pairs={{0,32},{32,64},{64,96},{96,0},{1,33},{33,65},{65,97},{97,1},{2,34}... | collective-permute-start | bytes 786440 | tf_op jit(solution)/shard_map/ppermute | solution.py:367
  187.9 26.3 %collective-permute-start = (bf16[64,2048]{1,0:T(8,128)(2,1)}, bf16[64,2048]{1,0:T(8,128)(2,1)}, u32[]{:S(2)}, u32[]{:S(2)}) collective-permute-start(bf16[64,2048]{1,0:T(8,128)(2,1)} %get-tuple-element.16), channel_id=1, source_target_pairs={{0,64},{32,96},{64,0},{96,32},{1,65},{33,97},{65,1},{97,33},{2,66}... | collective-permute-start | bytes 786440 | tf_op jit(solution)/shard_map/ppermute | solution.py:367
  193.5 0.8 copy-start.14
Sparse Core Ops, SparseCore 0:
  11.6 96.5 all-gather.1
  124.9 52.9 reduce-scatter.1

commit v2 on v1

v2 whole, which is shorter than its diff:
```python
import jax
import jax.numpy as jnp
from jax import lax
from jax.experimental import pallas as pl
from jax.experimental.pallas import tpu as pltpu
from jax.sharding import Mesh, PartitionSpec as P


KSIZE = 7
TOP = 2
IMG_W = 16
IMG_H = 8
EPS = 1e-06
EXPERTS = 32
CAP = 16
TOK = 128
SLOTS = EXPERTS * CAP
LANES = 128
F32 = jnp.float32
BF16 = jnp.bfloat16
MIB = 1 << 20

VMEM = pl.BlockSpec(memory_space=pltpu.VMEM)


def dot(a, b):
    return jnp.dot(a, b, preferred_element_type=F32)


def iota(shape, dim):
    return lax.broadcasted_iota(jnp.int32, shape, dim)


def slot_selects(ids_ref):
    turned = [
        jnp.broadcast_to(ids_ref[:, k : k + 1].astype(F32), (TOK, TOK)).T.astype(jnp.int32)
        for k in range(TOP)
    ]
    hot = [row[:EXPERTS] == iota((EXPERTS, TOK), 0) for row in turned]
    table = (hot[0] | hot[1]).astype(F32).astype(BF16)
    before = (iota((TOK, TOK), 0) < iota((TOK, TOK), 1)).astype(F32).astype(BF16)
    earlier = dot(table, before)
    out = []
    for k in range(TOP):
        slot = jnp.sum(jnp.where(hot[k], earlier, 0.0), axis=0, keepdims=True)
        position = turned[k][:1] * CAP + slot.astype(jnp.int32)
        out.append(iota((SLOTS, TOK), 0) == position)
    return out


def patch_selects(ids_ref):
    hot = [ids_ref[:, k : k + 1] == iota((TOK, EXPERTS), 1) for k in range(TOP)]
    table = (hot[0] | hot[1]).astype(F32).astype(BF16)
    before = (iota((TOK, TOK), 1) < iota((TOK, TOK), 0)).astype(F32).astype(BF16)
    earlier = dot(before, table)
    out = []
    for k in range(TOP):
        slot = jnp.sum(jnp.where(hot[k], earlier, 0.0), axis=1, keepdims=True)
        position = ids_ref[:, k : k + 1] * CAP + slot.astype(jnp.int32)
        out.append(iota((TOK, SLOTS), 1) == position)
    return out


def as_bf16(mask):
    return mask.astype(F32).astype(BF16)


def depthwise(padded, taps_ref, flip, start, put):
    half = KSIZE // 2

    def chunk(c, _):
        lanes = pl.ds(pl.multiple_of(c * LANES, LANES), LANES)
        total = start(lanes)
        for col in range(KSIZE):
            begin = 8 + col - half
            shifted = padded[:, begin : begin + IMG_W, lanes]
            for row in range(KSIZE):
                tap = (KSIZE - 1 - row) * KSIZE + KSIZE - 1 - col if flip else row * KSIZE + col
                weight = taps_ref[tap : tap + 1, lanes]
                total = total + shifted[row : row + IMG_H] * weight[None]
        put(lanes, total)
        return 0

    lax.fori_loop(0, padded.shape[2] // LANES, chunk, 0)


def send_kernel(
    ids_ref,
    gates_ref,
    cot_ref,
    x_ref,
    taps_ref,
    bias_ref,
    gain_ref,
    shift_ref,
    sent_ref,
    xhat_ref,
    rstd_ref,
    padded,
    total,
):
    width = x_ref.shape[1]
    half = KSIZE // 2
    padded[...] = jnp.zeros_like(padded)
    padded[half : half + IMG_H, 8 : 8 + IMG_W, :] = (
        x_ref[...].astype(F32).reshape(IMG_H, IMG_W, width)
    )

    def start(lanes):
        return jnp.broadcast_to(bias_ref[:, lanes][None], (IMG_H, IMG_W, LANES))

    def put(lanes, value):
        total[:, lanes] = value.reshape(TOK, LANES)

    depthwise(padded, taps_ref, False, start, put)
    conv = total[...]
    mean = jnp.sum(conv, axis=1, keepdims=True) * (1.0 / width)
    centred = conv - mean
    spread = jnp.sum(centred * centred, axis=1, keepdims=True) * (1.0 / width)
    rstd = lax.rsqrt(spread + EPS)
    xhat = centred * rstd
    xhat_ref[...] = xhat
    rstd_ref[...] = jnp.broadcast_to(rstd, (TOK, LANES))
    normed = (xhat * gain_ref[...] + shift_ref[...]).astype(BF16)
    select = slot_selects(ids_ref)
    sent = dot(as_bf16(select[0] | select[1]), normed).astype(BF16)
    sent_ref[:, 0] = sent.reshape(EXPERTS, CAP, width)
    cot = cot_ref[...].astype(F32)
    first = (gates_ref[:, 0:1] * cot).astype(BF16)
    second = (gates_ref[:, 1:2] * cot).astype(BF16)
    sent = (dot(as_bf16(select[0]), first) + dot(as_bf16(select[1]), second)).astype(BF16)
    sent_ref[:, 1] = sent.reshape(EXPERTS, CAP, width)


def finish_kernel(
    ids_ref,
    gates_ref,
    back_ref,
    xhat_ref,
    rstd_ref,
    gain_ref,
    taps_ref,
    cot_ref,
    x_ref,
    mixed_ref,
    out_ref,
    padded,
):
    width = xhat_ref.shape[1]
    half = KSIZE // 2
    select = [as_bf16(mask) for mask in patch_selects(ids_ref)]
    rows = back_ref[:, 1].reshape(SLOTS, width)
    combined = gates_ref[:, 0:1] * dot(select[0], rows)
    combined = combined + gates_ref[:, 1:2] * dot(select[1], rows)
    mixed_ref[...] = (x_ref[...].astype(F32) + combined).astype(BF16)

    grad = dot(select[0] + select[1], back_ref[:, 0].reshape(SLOTS, width))
    grad = grad * gain_ref[...]
    xhat = xhat_ref[...]
    mean = jnp.sum(grad, axis=1, keepdims=True) * (1.0 / width)
    along = jnp.sum(grad * xhat, axis=1, keepdims=True) * (1.0 / width)
    grad = rstd_ref[:, 0:1] * (grad - mean - xhat * along)
    padded[...] = jnp.zeros_like(padded)
    padded[half : half + IMG_H, 8 : 8 + IMG_W, :] = grad.reshape(IMG_H, IMG_W, width)

    def start(lanes):
        return jnp.zeros((IMG_H, IMG_W, LANES), F32)

    def put(lanes, value):
        out_ref[:, lanes] = cot_ref[:, lanes].astype(F32) + value.reshape(TOK, LANES)

    depthwise(padded, taps_ref, True, start, put)


def contract_last(left, right):
    return lax.dot_general(left, right, (((1,), (1,)), ((), ())), preferred_element_type=F32)


def contract_first(left, right):
    return lax.dot_general(left, right, (((0,), (0,)), ((), ())), preferred_element_type=F32)


SQRT_2_OVER_PI = 0.7978845608028654


def expert_kernel(
    moved_ref,
    w_in_ref,
    w_out_ref,
    back_ref,
    terms_ref,
    hidden_s,
    gh_s,
    grad_total,
    out_total,
):
    step = pl.program_id(0)
    steps = pl.num_programs(0) // 2
    sources, _, count, width = moved_ref.shape
    flat = sources * count
    block = w_in_ref.shape[1]
    hid = hidden_s.shape[0] * block

    @pl.when(step < steps)
    def _():
        pre = dot(moved_ref[:, 0].reshape(flat, width), w_in_ref[...])
        raw = dot(moved_ref[:, 1].reshape(flat, width), w_out_ref[...])
        square = pre * pre
        t = jnp.tanh(SQRT_2_OVER_PI * (pre + 0.044715 * (pre * square)))
        cdf = 0.5 * (1.0 + t)
        hidden = (pre * cdf).astype(BF16)
        slope = cdf + pre * (0.5 * (1.0 - t * t)) * (
            SQRT_2_OVER_PI * (1.0 + (3 * 0.044715) * square)
        )
        gh = (raw * slope).astype(BF16)
        hidden_s[step] = hidden
        gh_s[step] = gh
        grad_part = contract_last(gh, w_in_ref[...])
        out_part = contract_last(hidden, w_out_ref[...])

        @pl.when(step == 0)
        def _():
            grad_total[...] = grad_part
            out_total[...] = out_part

        @pl.when(step > 0)
        def _():
            grad_total[...] += grad_part
            out_total[...] += out_part

    @pl.when(step == steps - 1)
    def _():
        back_ref[:, 0] = grad_total[...].astype(BF16).reshape(sources, count, width)
        back_ref[:, 1] = out_total[...].astype(BF16).reshape(sources, count, width)

    @pl.when(step >= steps)
    def _():
        lanes = pl.ds(pl.multiple_of((step - steps) * block, block), block)
        rows = moved_ref[:, 0, :, lanes].reshape(flat, block)
        grads = moved_ref[:, 1, :, lanes].reshape(flat, block)
        for j in range(hidden_s.shape[0]):
            at = slice(j * block, (j + 1) * block)
            terms_ref[:, at] = contract_first(rows, gh_s[j]).astype(BF16)
            at = slice(hid + j * block, hid + (j + 1) * block)
            terms_ref[:, at] = contract_first(grads, hidden_s[j]).astype(BF16)


def place_kernel(where_ref, *refs):
    pieces, out_ref = refs[:-1], refs[-1]
    for k, piece in enumerate(pieces):
        at = lax.rem(where_ref[0] + len(pieces) - k, len(pieces))
        out_ref[at] = piece[...]


def cut_kernel(where_ref, block_ref, *out_refs):
    parts = block_ref.shape[0]
    for k, out_ref in enumerate(out_refs):
        out_ref[...] = block_ref[lax.rem(where_ref[0] + k + 1, parts)]


def add_kernel(where_ref, block_ref, first_ref, second_ref, third_ref, in_ref, out_ref):
    hid = in_ref.shape[1]
    total = block_ref[where_ref[0]].astype(F32) + first_ref[...].astype(F32)
    total = total + second_ref[...].astype(F32) + third_ref[...].astype(F32)
    in_ref[...] = total[:, :hid]
    out_ref[...] = total[:, hid:]


def params(mib=16):
    return pltpu.CompilerParams(vmem_limit_bytes=mib * MIB)


def cost(flops, nbytes):
    return pl.CostEstimate(flops=int(flops), bytes_accessed=int(nbytes), transcendentals=0)


def shape(dims, dtype):
    return jax.ShapeDtypeStruct(dims, dtype)


def send(ids, gates, cot, x, taps, bias, gain, shift):
    width = x.shape[1]
    return pl.pallas_call(
        send_kernel,
        out_shape=(
            shape((EXPERTS, 2, CAP, width), BF16),
            shape((TOK, width), F32),
            shape((TOK, LANES), F32),
        ),
        in_specs=[VMEM] * 8,
        out_specs=[VMEM] * 3,
        scratch_shapes=[
            pltpu.VMEM((IMG_H + KSIZE - 1, IMG_W + 16, width), F32),
            pltpu.VMEM((TOK, width), F32),
        ],
        compiler_params=params(),
        cost_estimate=cost(100 * TOK * width * 20, 4 * SLOTS * width),
        name="send",
    )(ids, gates, cot, x, taps, bias.reshape(1, width), gain.reshape(1, width), shift.reshape(1, width))


def finish(ids, gates, back, xhat, rstd, gain, taps, cot, x):
    width = cot.shape[1]
    return pl.pallas_call(
        finish_kernel,
        out_shape=(shape((TOK, width), BF16), shape((TOK, width), F32)),
        in_specs=[VMEM] * 9,
        out_specs=[VMEM] * 2,
        scratch_shapes=[pltpu.VMEM((IMG_H + KSIZE - 1, IMG_W + 16, width), F32)],
        compiler_params=params(),
        cost_estimate=cost(100 * TOK * width * 20, 4 * SLOTS * width),
        name="finish",
    )(ids, gates, back, xhat, rstd, gain.reshape(1, width), taps, cot, x)


def expert(moved, w_in, w_out):
    sources, _, count, width = moved.shape
    flat = sources * count
    hid = w_in.shape[1]
    block = 256
    steps = hid // block
    whole = pl.BlockSpec(
        (sources, 2, count, width), lambda j: (0, 0, 0, 0), pipeline_mode=pl.Buffered(1)
    )
    weight = pl.BlockSpec((width, block), lambda j: (0, jnp.minimum(j, steps - 1)))
    return pl.pallas_call(
        expert_kernel,
        grid=(2 * steps,),
        out_shape=(
            pltpu.HBM((sources, 2, count, width), BF16),
            pltpu.HBM((width, 2 * hid), BF16),
        ),
        in_specs=[whole, weight, weight],
        out_specs=[
            pl.BlockSpec((sources, 2, count, width), lambda j: (0, 0, 0, 0)),
            pl.BlockSpec((block, 2 * hid), lambda j: (jnp.maximum(j - steps, 0), 0)),
        ],
        scratch_shapes=[
            pltpu.VMEM((steps, flat, block), BF16),
            pltpu.VMEM((steps, flat, block), BF16),
            pltpu.VMEM((flat, width), F32),
            pltpu.VMEM((flat, width), F32),
        ],
        compiler_params=params(32),
        cost_estimate=cost(12 * flat * width * hid, 12 * MIB),
        name="expert",
    )(moved, *(pltpu.with_memory_space_constraint(w, pltpu.HBM) for w in (w_in, w_out)))


SMEM = pl.BlockSpec(memory_space=pltpu.SMEM)


def place(where, pieces):
    dims = pieces[0].shape
    return pl.pallas_call(
        place_kernel,
        out_shape=shape((len(pieces),) + dims, BF16),
        in_specs=[SMEM] + [VMEM] * len(pieces),
        out_specs=VMEM,
        compiler_params=params(8),
        cost_estimate=cost(0, 4 * MIB),
        name="place",
    )(where, *pieces)


def exchange(rows, axes):
    return lax.all_to_all(rows, axes, split_axis=0, concat_axis=0, tiled=True)


def shifted(value, axis, k):
    n = lax.axis_size(axis)
    return lax.ppermute(value, axis, [(i, (i + k) % n) for i in range(n)])


def where_on(axis):
    return lax.axis_index(axis).astype(jnp.int32).reshape(1)


def gather_by(axis, piece):
    far, after, before = (shifted(piece, axis, k) for k in (2, 1, 3))
    return place(where_on(axis), [piece, after, far, before])


def sum_over_y(block):
    where = where_on("yh")
    parts, rows, columns = block.shape
    cuts = pl.pallas_call(
        cut_kernel,
        out_shape=[shape((rows, columns), BF16)] * (parts - 1),
        in_specs=[SMEM, VMEM],
        out_specs=[VMEM] * (parts - 1),
        compiler_params=params(8),
        cost_estimate=cost(0, 2 * MIB),
        name="cut",
    )(where, block)
    got = {k: shifted(cuts[k - 1], "yh", k) for k in (2, 1, 3)}
    hid = columns // 2
    return pl.pallas_call(
        add_kernel,
        out_shape=[shape((rows, hid), F32)] * 2,
        in_specs=[SMEM] + [VMEM] * parts,
        out_specs=[VMEM] * 2,
        compiler_params=params(8),
        cost_estimate=cost(0, 2 * MIB),
        name="add",
    )(where, block, got[1], got[2], got[3])


def local(
    patches,
    expert_ids,
    gate_weights,
    conv_weight,
    conv_bias,
    ln_gain,
    ln_shift,
    w_in,
    w_out,
    grad_mixed,
):
    hid = w_in.shape[2]
    dp = ("x", "yh")
    ep = ("z", "yl", "core")
    full_in = lax.all_gather(w_in, dp, axis=1, tiled=True)[0]
    sent, xhat, rstd = send(
        expert_ids,
        gate_weights,
        grad_mixed,
        patches,
        conv_weight,
        conv_bias,
        ln_gain,
        ln_shift,
    )
    moved = exchange(sent, ep)
    along_y = gather_by("yh", w_out[0])
    full_out = gather_by("x", along_y.reshape(-1, hid)).reshape(-1, hid)
    back, partial = expert(moved, full_in, full_out)
    over_x = lax.psum_scatter(partial, "x", scatter_dimension=0, tiled=True)
    returned = exchange(back, ep)
    grad_in, grad_out = sum_over_y(over_x.reshape(4, -1, 2 * hid))
    mixed, grad_input = finish(
        expert_ids,
        gate_weights,
        returned,
        xhat,
        rstd,
        ln_gain,
        conv_weight,
        grad_mixed,
        patches,
    )
    return (mixed, grad_input, grad_in[None], grad_out[None])


def solution(mesh):
    fine = Mesh(mesh.devices.reshape(4, 4, 8, 2, 2), ("x", "yh", "z", "yl", "core"))
    dp = ("x", "yh")
    ep = ("z", "yl", "core")
    rows = P(dp + ep, None)
    weight = P(ep, dp, None)
    return jax.shard_map(
        local,
        mesh=fine,
        in_specs=(rows, rows, rows, P(), P(), P(), P(), weight, weight, rows),
        out_specs=(rows, rows, weight, weight),
        check_vma=False,
    )
```

time: 224 us -> 235 us (1.049)
  the two profiles are of different devices: /device:TPU:16 before, /device:TPU:1 now
where the time goes in v2:
time: 235 us; the launch traced here: 234 us
  waiting for transfers between devices  112 us (48%)
  starting transfers between devices  59.9 us (25%)
  Pallas kernels  31.3 us (13%)
  local copies, waits for them, and re-layouts  16.5 us (7%)
  between operations  14.2 us (6%)
    ppermute x9, waiting for transfers between devices, shifted(): return lax.ppermute(value, axis, [(i, (i + k) % n) for i in range(n)])  70.9 us
    reduce_scatter x1, waiting for transfers between devices, local(): over_x = lax.psum_scatter(partial, 'x', scatter_dimension=0, tiled=True)  40.8 us
    ppermute x9, starting transfers between devices, shifted(): return lax.ppermute(value, axis, [(i, (i + k) % n) for i in range(n)])  36.1 us
    all_to_all x2, starting transfers between devices, exchange(): return lax.all_to_all(rows, axes, split_axis=0, concat_axis=0, tiled=True)  23.7 us
    unnamed x40, local copies, waits for them, and re-layouts  16.5 us
    pallas_call x1, Pallas kernels, expert(): pl.pallas_call(expert_kernel, grid=(2 * steps,), out_shape=(pltpu.HBM((so...  14.2 us
    pallas_call x1, Pallas kernels, finish(): pl.pallas_call(finish_kernel, out_shape=(shape((TOK, width), BF16), shape...  6.75 us
    pallas_call x1, Pallas kernels, send(): pl.pallas_call(send_kernel, out_shape=(shape((EXPERTS, 2, CAP, width), BF...  6.18 us
  transfers between devices with their start and end apart: 13, of which 7 were waited for; matrix products, arithmetic and copies ran while one was open for 0% of the time, Pallas kernels for 4%

profile of v2, /device:TPU:1, one launch (start us, length us, event | category | flops | bytes accessed | tf_op | source)
XLA Modules:
  0.0 234.4 jit_solution(11204110581835381068)
XLA Ops:
  8.7 0.9 copy-done.6
  9.7 0.9 copy-done.8
  10.6 0.9 copy-done.10
  13.6 6.2 %send.1 = (bf16[32,2,16,1024]{3,2,1,0:T(8,128)(2,1)S(1)}, f32[128,1024]{1,0:T(8,128)S(1)}, f32[128,128]{1,0:T(8,128)S(1)}) custom-call(s32[128,2]{1,0:T(8,128)S(1)} %copy.16.ids_ref, f32[128,2]{1,0:T(8,128)S(1)} %copy.17.gates_ref, bf16[128,1024]{1,0:T(8,128)(2,1)S(1)} %copy-done.6, bf16[128,1024]{1,0:T(8,128)(2,1)S(1)} %copy-done.8, ...), custom_call_target="tpu_custom_call" | custom-call | flops 262144000 | bytes 2097152 | tf_op jit(solution)/shard_map/send/pallas_call | solution.py:283
  19.8 1.3 copy-done.2
  22.6 13.1 %all-to-all-start = ((bf16[32,2,16,1024]{3,2,1,0:T(8,128)(2,1)}), bf16[32,2,16,1024]{3,2,1,0:T(8,128)(2,1)S(1)}, u32[]{:S(2)}, u32[]{:S(2)}) async-start(bf16[32,2,16,1024]{3,2,1,0:T(8,128)(2,1)} %copy-done.2), calls=%async_computation | async-start | bytes 4194304 | tf_op jit(solution)/shard_map/all_to_all | solution.py:367
  36.5 5.0 %collective-permute-start.2 = (bf16[64,1024]{1,0:T(8,128)(2,1)S(1)}, bf16[64,1024]{1,0:T(8,128)(2,1)S(1)}, u32[]{:S(2)}, u32[]{:S(2)}) collective-permute-start(bf16[64,1024]{1,0:T(8,128)(2,1)S(1)} %bitcast.19), channel_id=1, source_target_pairs={{0,96},{32,0},{64,32},{96,64},{1,97},{33,1},{65,33},{97,65},{2,98}... | collective-permute-start | bytes 393224 | tf_op jit(solution)/shard_map/ppermute | solution.py:372
  41.5 4.4 %collective-permute-start.1 = (bf16[64,1024]{1,0:T(8,128)(2,1)S(1)}, bf16[64,1024]{1,0:T(8,128)(2,1)S(1)}, u32[]{:S(2)}, u32[]{:S(2)}) collective-permute-start(bf16[64,1024]{1,0:T(8,128)(2,1)S(1)} %bitcast.20), channel_id=1, source_target_pairs={{0,64},{32,96},{64,0},{96,32},{1,65},{33,97},{65,1},{97,33},{2,66}... | collective-permute-start | bytes 393224 | tf_op jit(solution)/shard_map/ppermute | solution.py:372
  45.9 3.3 %collective-permute-start = (bf16[64,1024]{1,0:T(8,128)(2,1)S(1)}, bf16[64,1024]{1,0:T(8,128)(2,1)S(1)}, u32[]{:S(2)}, u32[]{:S(2)}) collective-permute-start(bf16[64,1024]{1,0:T(8,128)(2,1)S(1)} %bitcast.21), channel_id=1, source_target_pairs={{0,32},{32,64},{64,96},{96,0},{1,33},{33,65},{65,97},{97,1},{2,34}... | collective-permute-start | bytes 393224 | tf_op jit(solution)/shard_map/ppermute | solution.py:372
  49.3 30.5 %collective-permute-done.1.refs_2_ = bf16[64,1024]{1,0:T(8,128)(2,1)S(1)} collective-permute-done((bf16[64,1024]{1,0:T(8,128)(2,1)S(1)}, bf16[64,1024]{1,0:T(8,128)(2,1)S(1)}, u32[]{:S(2)}, u32[]{:S(2)}) %collective-permute-start.1) | collective-permute-done | bytes 131104 | tf_op jit(solution)/shard_map/ppermute | solution.py:372
  79.8 3.0 %collective-permute-done.refs_1_ = bf16[64,1024]{1,0:T(8,128)(2,1)S(1)} collective-permute-done((bf16[64,1024]{1,0:T(8,128)(2,1)S(1)}, bf16[64,1024]{1,0:T(8,128)(2,1)S(1)}, u32[]{:S(2)}, u32[]{:S(2)}) %collective-permute-start) | collective-permute-done | bytes 131104 | tf_op jit(solution)/shard_map/ppermute | solution.py:372
  82.8 3.9 %collective-permute-start.5 = (bf16[256,1024]{1,0:T(8,128)(2,1)S(1)}, bf16[256,1024]{1,0:T(8,128)(2,1)S(1)}, u32[]{:S(2)}, u32[]{:S(2)}) collective-permute-start(bf16[256,1024]{1,0:T(8,128)(2,1)S(1)} %bitcast.14), channel_id=1, source_target_pairs={{0,384},{128,0},{256,128},{384,256},{1,385},{129,1},{257,129},{385... | collective-permute-start | bytes 1572872 | tf_op jit(solution)/shard_map/ppermute | solution.py:372
  86.8 2.4 %collective-permute-start.4 = (bf16[256,1024]{1,0:T(8,128)(2,1)S(1)}, bf16[256,1024]{1,0:T(8,128)(2,1)}, u32[]{:S(2)}, u32[]{:S(2)}) collective-permute-start(bf16[256,1024]{1,0:T(8,128)(2,1)S(1)} %bitcast.15), channel_id=1, source_target_pairs={{0,256},{128,384},{256,0},{384,128},{1,257},{129,385},{257,1},{385... | collective-permute-start | bytes 1572872 | tf_op jit(solution)/shard_map/ppermute | solution.py:372
  89.2 2.6 %collective-permute-start.3 = (bf16[256,1024]{1,0:T(8,128)(2,1)S(1)}, bf16[256,1024]{1,0:T(8,128)(2,1)}, u32[]{:S(2)}, u32[]{:S(2)}) collective-permute-start(bf16[256,1024]{1,0:T(8,128)(2,1)S(1)} %bitcast.16), channel_id=1, source_target_pairs={{0,128},{128,256},{256,384},{384,0},{1,129},{129,257},{257,385},{3... | collective-permute-start | bytes 1572872 | tf_op jit(solution)/shard_map/ppermute | solution.py:372
  91.8 13.7 %collective-permute-done.5.refs_3_ = bf16[256,1024]{1,0:T(8,128)(2,1)S(1)} collective-permute-done((bf16[256,1024]{1,0:T(8,128)(2,1)S(1)}, bf16[256,1024]{1,0:T(8,128)(2,1)S(1)}, u32[]{:S(2)}, u32[]{:S(2)}) %collective-permute-start.5) | collective-permute-done | bytes 524320 | tf_op jit(solution)/shard_map/ppermute | solution.py:372
  105.5 2.9 %collective-permute-done.4.refs_2_ = bf16[256,1024]{1,0:T(8,128)(2,1)} collective-permute-done((bf16[256,1024]{1,0:T(8,128)(2,1)S(1)}, bf16[256,1024]{1,0:T(8,128)(2,1)}, u32[]{:S(2)}, u32[]{:S(2)}) %collective-permute-start.4) | collective-permute-done | bytes 524320 | tf_op jit(solution)/shard_map/ppermute | solution.py:372
  108.4 12.4 %collective-permute-done.3.refs_1_ = bf16[256,1024]{1,0:T(8,128)(2,1)} collective-permute-done((bf16[256,1024]{1,0:T(8,128)(2,1)S(1)}, bf16[256,1024]{1,0:T(8,128)(2,1)}, u32[]{:S(2)}, u32[]{:S(2)}) %collective-permute-start.3) | collective-permute-done | bytes 524320 | tf_op jit(solution)/shard_map/ppermute | solution.py:372
  120.8 1.3 place.3
  122.2 1.4 copy-done.3
  123.5 14.2 %expert.1 = (bf16[32,2,16,1024]{3,2,1,0:T(8,128)(2,1)}, bf16[1024,2048]{1,0:T(8,128)(2,1)}) custom-call(bf16[32,2,16,1024]{3,2,1,0:T(8,128)(2,1)S(1)} %all-to-all-done.moved_ref, bf16[1024,1024]{1,0:T(8,128)(2,1)} %bitcast.27, bf16[1024,1024]{1,0:T(8,128)(2,1)} %bitcast.18), custom_call_target="tpu_custom_call" | custom-call | flops 6442450944 | bytes 12582912 | tf_op jit(solution)/shard_map/expert/pallas_call | solution.py:326
  137.7 10.6 %all-to-all-start.1 = ((bf16[32,2,16,1024]{3,2,1,0:T(8,128)(2,1)}), bf16[32,2,16,1024]{3,2,1,0:T(8,128)(2,1)S(1)}, u32[]{:S(2)}, u32[]{:S(2)}) async-start(bf16[32,2,16,1024]{3,2,1,0:T(8,128)(2,1)} %get-tuple-element.17), calls=%async_computation.1 | async-start | bytes 4194304 | tf_op jit(solution)/shard_map/all_to_all | solution.py:367
  148.3 40.8 %reduce-scatter.2.cloned.1.call-done = bf16[256,2048]{1,0:T(8,128)(2,1)} async-done(((bf16[1024,2048]{1,0:T(8,128)(2,1)}), bf16[256,2048]{1,0:T(8,128)(2,1)}) %reduce-scatter.2.cloned.1.call-update) | async-done | bytes 1048592 | tf_op jit(solution)/shard_map/reduce_scatter | solution.py:439
  189.1 1.2 copy-done
  191.3 4.0 %collective-permute-start.6 = (bf16[64,2048]{1,0:T(8,128)(2,1)}, bf16[64,2048]{1,0:T(8,128)(2,1)S(1)}, u32[]{:S(2)}, u32[]{:S(2)}) collective-permute-start(bf16[64,2048]{1,0:T(8,128)(2,1)} %get-tuple-element.23), channel_id=1, source_target_pairs={{0,32},{32,64},{64,96},{96,0},{1,33},{33,65},{65,97},{97,1},{2,34}... | collective-permute-start | bytes 786440 | tf_op jit(solution)/shard_map/ppermute | solution.py:372
  195.3 5.3 %collective-permute-start.7 = (bf16[64,2048]{1,0:T(8,128)(2,1)}, bf16[64,2048]{1,0:T(8,128)(2,1)}, u32[]{:S(2)}, u32[]{:S(2)}) collective-permute-start(bf16[64,2048]{1,0:T(8,128)(2,1)} %get-tuple-element.24), channel_id=1, source_target_pairs={{0,64},{32,96},{64,0},{96,32},{1,65},{33,97},{65,1},{97,33},{2,66}... | collective-permute-start | bytes 786440 | tf_op jit(solution)/shard_map/ppermute | solution.py:372
  200.6 5.2 %collective-permute-start.8 = (bf16[64,2048]{1,0:T(8,128)(2,1)}, bf16[64,2048]{1,0:T(8,128)(2,1)}, u32[]{:S(2)}, u32[]{:S(2)}) collective-permute-start(bf16[64,2048]{1,0:T(8,128)(2,1)} %get-tuple-element.25), channel_id=1, source_target_pairs={{0,96},{32,0},{64,32},{96,64},{1,97},{33,1},{65,33},{97,65},{2,98}... | collective-permute-start | bytes 786440 | tf_op jit(solution)/shard_map/ppermute | solution.py:372
  205.8 1.0 copy-done.5
  206.8 0.9 copy-done.7
  207.8 0.9 copy-done.9
  210.5 6.8 %finish.1 = (bf16[128,1024]{1,0:T(8,128)(2,1)}, f32[128,1024]{1,0:T(8,128)}) custom-call(s32[128,2]{1,0:T(8,128)S(1)} %copy.16.ids_ref, f32[128,2]{1,0:T(8,128)S(1)} %copy.17.gates_ref, bf16[32,2,16,1024]{3,2,1,0:T(8,128)(2,1)S(1)} %all-to-all-done.1.back_ref, f32[128,1024]{1,0:T(8,128)S(1)} %copy-done.5, f32[128,128]{1,0:T(8,128)S(1)} %copy-done.14, ...), custom_call_target="tpu_custom_call" | custom-call | flops 262144000 | bytes 2097152 | tf_op jit(solution)/shard_map/finish/pallas_call | solution.py:304
  217.3 8.4 %collective-permute-done.8.third_ref = bf16[64,2048]{1,0:T(8,128)(2,1)} collective-permute-done((bf16[64,2048]{1,0:T(8,128)(2,1)}, bf16[64,2048]{1,0:T(8,128)(2,1)}, u32[]{:S(2)}, u32[]{:S(2)}) %collective-permute-start.8) | collective-permute-done | bytes 262176 | tf_op jit(solution)/shard_map/ppermute | solution.py:372
  225.6 1.9 add.4
  (43 shorter events, 8.6 us)
Async XLA Ops:
  8.7 0.9 copy-start.6
  9.7 0.9 copy-start.8
  10.6 0.9 copy-start.10
  11.6 0.7 copy-start.15
  12.3 0.7 copy-start.17
  12.9 0.7 copy-start.18
  19.8 1.4 copy-start.2
  21.2 0.8 copy-start.4
  22.0 0.6 copy-start.13
  22.6 13.9 %copy-start.12 = (bf16[1,64,1024]{2,1,0:T(8,128)(2,1)S(1)}, bf16[1,64,1024]{2,1,0:T(8,128)(2,1)}, u32[]{:S(2)}) copy-start(bf16[1,64,1024]{2,1,0:T(8,128)(2,1)} %param.18) | copy-start | bytes 393220
  22.6 100.9 %all-to-all-start = ((bf16[32,2,16,1024]{3,2,1,0:T(8,128)(2,1)}), bf16[32,2,16,1024]{3,2,1,0:T(8,128)(2,1)S(1)}, u32[]{:S(2)}, u32[]{:S(2)}) async-start(bf16[32,2,16,1024]{3,2,1,0:T(8,128)(2,1)} %copy-done.2), calls=%async_computation | async-start | bytes 4194304 | tf_op jit(solution)/shard_map/all_to_all | solution.py:367
  35.7 87.8 %all-gather.2.cloned.1.call-start = ((), (), s32[]{:S(2)}) async-start(), calls=%async_computation.3 | async-start | bytes 2228224 | tf_op jit(solution)/shard_map/all_gather | solution.py:424
  36.5 152.7 %reduce-scatter.2.cloned.1.call-start = ((), (), s32[]{:S(2)}) async-start(), calls=%async_computation.4 | async-start | bytes 5242880 | tf_op jit(solution)/shard_map/reduce_scatter | solution.py:439
  36.5 12.8 %collective-permute-start.2 = (bf16[64,1024]{1,0:T(8,128)(2,1)S(1)}, bf16[64,1024]{1,0:T(8,128)(2,1)S(1)}, u32[]{:S(2)}, u32[]{:S(2)}) collective-permute-start(bf16[64,1024]{1,0:T(8,128)(2,1)S(1)} %bitcast.19), channel_id=1, source_target_pairs={{0,96},{32,0},{64,32},{96,64},{1,97},{33,1},{65,33},{97,65},{2,98}... | collective-permute-start | bytes 393224 | tf_op jit(solution)/shard_map/ppermute | solution.py:372
  41.5 38.3 %collective-permute-start.1 = (bf16[64,1024]{1,0:T(8,128)(2,1)S(1)}, bf16[64,1024]{1,0:T(8,128)(2,1)S(1)}, u32[]{:S(2)}, u32[]{:S(2)}) collective-permute-start(bf16[64,1024]{1,0:T(8,128)(2,1)S(1)} %bitcast.20), channel_id=1, source_target_pairs={{0,64},{32,96},{64,0},{96,32},{1,65},{33,97},{65,1},{97,33},{2,66}... | collective-permute-start | bytes 393224 | tf_op jit(solution)/shard_map/ppermute | solution.py:372
  45.9 36.9 %collective-permute-start = (bf16[64,1024]{1,0:T(8,128)(2,1)S(1)}, bf16[64,1024]{1,0:T(8,128)(2,1)S(1)}, u32[]{:S(2)}, u32[]{:S(2)}) collective-permute-start(bf16[64,1024]{1,0:T(8,128)(2,1)S(1)} %bitcast.21), channel_id=1, source_target_pairs={{0,32},{32,64},{64,96},{96,0},{1,33},{33,65},{65,97},{97,1},{2,34}... | collective-permute-start | bytes 393224 | tf_op jit(solution)/shard_map/ppermute | solution.py:372
  82.8 22.7 %collective-permute-start.5 = (bf16[256,1024]{1,0:T(8,128)(2,1)S(1)}, bf16[256,1024]{1,0:T(8,128)(2,1)S(1)}, u32[]{:S(2)}, u32[]{:S(2)}) collective-permute-start(bf16[256,1024]{1,0:T(8,128)(2,1)S(1)} %bitcast.14), channel_id=1, source_target_pairs={{0,384},{128,0},{256,128},{384,256},{1,385},{129,1},{257,129},{385... | collective-permute-start | bytes 1572872 | tf_op jit(solution)/shard_map/ppermute | solution.py:372
  86.8 21.6 %collective-permute-start.4 = (bf16[256,1024]{1,0:T(8,128)(2,1)S(1)}, bf16[256,1024]{1,0:T(8,128)(2,1)}, u32[]{:S(2)}, u32[]{:S(2)}) collective-permute-start(bf16[256,1024]{1,0:T(8,128)(2,1)S(1)} %bitcast.15), channel_id=1, source_target_pairs={{0,256},{128,384},{256,0},{384,128},{1,257},{129,385},{257,1},{385... | collective-permute-start | bytes 1572872 | tf_op jit(solution)/shard_map/ppermute | solution.py:372
  89.2 31.6 %collective-permute-start.3 = (bf16[256,1024]{1,0:T(8,128)(2,1)S(1)}, bf16[256,1024]{1,0:T(8,128)(2,1)}, u32[]{:S(2)}, u32[]{:S(2)}) collective-permute-start(bf16[256,1024]{1,0:T(8,128)(2,1)S(1)} %bitcast.16), channel_id=1, source_target_pairs={{0,128},{128,256},{256,384},{384,0},{1,129},{129,257},{257,385},{3... | collective-permute-start | bytes 1572872 | tf_op jit(solution)/shard_map/ppermute | solution.py:372
  122.1 1.4 copy-start.3
  137.7 68.1 %copy-start.16 = (f32[1024]{0:T(1024)S(1)}, f32[1024]{0:T(1024)}, u32[]{:S(2)}) copy-start(f32[1024]{0:T(1024)} %param.15) | copy-start | bytes 12292
  137.7 68.0 %all-to-all-start.1 = ((bf16[32,2,16,1024]{3,2,1,0:T(8,128)(2,1)}), bf16[32,2,16,1024]{3,2,1,0:T(8,128)(2,1)S(1)}, u32[]{:S(2)}, u32[]{:S(2)}) async-start(bf16[32,2,16,1024]{3,2,1,0:T(8,128)(2,1)} %get-tuple-element.17), calls=%async_computation.1 | async-start | bytes 4194304 | tf_op jit(solution)/shard_map/all_to_all | solution.py:367
  189.1 1.2 copy-start
  190.4 35.3 %copy-start.1 = (bf16[256,2048]{1,0:T(8,128)(2,1)S(1)}, bf16[256,2048]{1,0:T(8,128)(2,1)}, u32[]{:S(2)}) copy-start(bf16[256,2048]{1,0:T(8,128)(2,1)} %reduce-scatter.2.cloned.1.call-done) | copy-start | bytes 3145732
  191.3 26.0 %collective-permute-start.6 = (bf16[64,2048]{1,0:T(8,128)(2,1)}, bf16[64,2048]{1,0:T(8,128)(2,1)S(1)}, u32[]{:S(2)}, u32[]{:S(2)}) collective-permute-start(bf16[64,2048]{1,0:T(8,128)(2,1)} %get-tuple-element.23), channel_id=1, source_target_pairs={{0,32},{32,64},{64,96},{96,0},{1,33},{33,65},{65,97},{97,1},{2,34}... | collective-permute-start | bytes 786440 | tf_op jit(solution)/shard_map/ppermute | solution.py:372
  195.3 22.0 %collective-permute-start.7 = (bf16[64,2048]{1,0:T(8,128)(2,1)}, bf16[64,2048]{1,0:T(8,128)(2,1)}, u32[]{:S(2)}, u32[]{:S(2)}) collective-permute-start(bf16[64,2048]{1,0:T(8,128)(2,1)} %get-tuple-element.24), channel_id=1, source_target_pairs={{0,64},{32,96},{64,0},{96,32},{1,65},{33,97},{65,1},{97,33},{2,66}... | collective-permute-start | bytes 786440 | tf_op jit(solution)/shard_map/ppermute | solution.py:372
  200.6 25.0 %collective-permute-start.8 = (bf16[64,2048]{1,0:T(8,128)(2,1)}, bf16[64,2048]{1,0:T(8,128)(2,1)}, u32[]{:S(2)}, u32[]{:S(2)}) collective-permute-start(bf16[64,2048]{1,0:T(8,128)(2,1)} %get-tuple-element.25), channel_id=1, source_target_pairs={{0,96},{32,0},{64,32},{96,64},{1,97},{33,1},{65,33},{97,65},{2,98}... | collective-permute-start | bytes 786440 | tf_op jit(solution)/shard_map/ppermute | solution.py:372
  205.8 1.0 copy-start.5
  206.8 0.9 copy-start.7
  207.8 0.9 copy-start.9
  208.7 0.9 copy-start.11
  209.7 0.8 copy-start.14
Sparse Core Ops, SparseCore 0:
  39.5 74.7 all-gather.1
  137.8 51.2 reduce-scatter.1

commit v3 on v2

--- a/solution.py
+++ b/solution.py
@@ -250,20 +250,6 @@
     for k, piece in enumerate(pieces):
         at = lax.rem(where_ref[0] + len(pieces) - k, len(pieces))
         out_ref[at] = piece[...]
-
-
-def cut_kernel(where_ref, block_ref, *out_refs):
-    parts = block_ref.shape[0]
-    for k, out_ref in enumerate(out_refs):
-        out_ref[...] = block_ref[lax.rem(where_ref[0] + k + 1, parts)]
-
-
-def add_kernel(where_ref, block_ref, first_ref, second_ref, third_ref, in_ref, out_ref):
-    hid = in_ref.shape[1]
-    total = block_ref[where_ref[0]].astype(F32) + first_ref[...].astype(F32)
-    total = total + second_ref[...].astype(F32) + third_ref[...].astype(F32)
-    in_ref[...] = total[:, :hid]
-    out_ref[...] = total[:, hid:]
 
 
 def params(mib=16):
@@ -381,29 +367,9 @@
     return place(where_on(axis), [piece, after, far, before])
 
 
-def sum_over_y(block):
-    where = where_on("yh")
-    parts, rows, columns = block.shape
-    cuts = pl.pallas_call(
-        cut_kernel,
-        out_shape=[shape((rows, columns), BF16)] * (parts - 1),
-        in_specs=[SMEM, VMEM],
-        out_specs=[VMEM] * (parts - 1),
-        compiler_params=params(8),
-        cost_estimate=cost(0, 2 * MIB),
-        name="cut",
-    )(where, block)
-    got = {k: shifted(cuts[k - 1], "yh", k) for k in (2, 1, 3)}
-    hid = columns // 2
-    return pl.pallas_call(
-        add_kernel,
-        out_shape=[shape((rows, hid), F32)] * 2,
-        in_specs=[SMEM] + [VMEM] * parts,
-        out_specs=[VMEM] * 2,
-        compiler_params=params(8),
-        cost_estimate=cost(0, 2 * MIB),
-        name="add",
-    )(where, block, got[1], got[2], got[3])
+def gather_y(piece):
+    parts = lax.axis_size("yh")
+    return exchange(jnp.broadcast_to(piece[None], (parts,) + piece.shape), "yh")
 
 
 def local(
@@ -433,12 +399,12 @@
         ln_shift,
     )
     moved = exchange(sent, ep)
-    along_y = gather_by("yh", w_out[0])
+    along_y = gather_y(w_out[0])
     full_out = gather_by("x", along_y.reshape(-1, hid)).reshape(-1, hid)
     back, partial = expert(moved, full_in, full_out)
     over_x = lax.psum_scatter(partial, "x", scatter_dimension=0, tiled=True)
     returned = exchange(back, ep)
-    grad_in, grad_out = sum_over_y(over_x.reshape(4, -1, 2 * hid))
+    total = lax.psum_scatter(over_x, "yh", scatter_dimension=0, tiled=True).astype(F32)
     mixed, grad_input = finish(
         expert_ids,
         gate_weights,
@@ -450,7 +416,7 @@
         grad_mixed,
         patches,
     )
-    return (mixed, grad_input, grad_in[None], grad_out[None])
+    return (mixed, grad_input, total[:, :hid][None], total[:, hid:][None])
 
 
 def solution(mesh):

time: 235 us -> 228 us (0.970)
  starting transfers between devices: 59.9 us -> 38.3 us
  waiting for transfers between devices: 112 us -> 132 us
  local copies, waits for them, and re-layouts: 16.5 us -> 12.7 us
    ppermute x9 -> x3, waiting for transfers between devices: 70.9 us -> 25.3 us  [shifted(): return lax.ppermute(value, axis, [(i, (i + k) % n) for i in range(n)])]
    all_gather x1, waiting for transfers between devices: 0.01 us -> 33.4 us  [local(): full_in = lax.all_gather(w_in, dp, axis=1, tiled=True)[0]]
    ppermute x9 -> x3, starting transfers between devices: 36.1 us -> 9.33 us  [shifted(): return lax.ppermute(value, axis, [(i, (i + k) % n) for i in range(n)])]
    reduce_scatter x0 -> x1, waiting for transfers between devices: none -> 17.7 us  [local(): lax.psum_scatter(over_x, 'yh', scatter_dimension=0, tiled=True).astype(F32)]
    all_to_all x2 -> x3, waiting for transfers between devices: 0.01 us -> 13.2 us  [exchange(): return lax.all_to_all(rows, axes, split_axis=0, concat_axis=0, tiled=True)]
    unnamed x40 -> x32, local copies, waits for them, and re-layouts: 16.5 us -> 10.1 us
    all_to_all x2 -> x3, starting transfers between devices: 23.7 us -> 28.9 us  [exchange(): return lax.all_to_all(rows, axes, split_axis=0, concat_axis=0, tiled=True)]
    pallas_call x2 -> x0, Pallas kernels: 2.8 us -> none  [the longest x1 1.88 us: sum_over_y(): pl.pallas_call(add_kernel, out_shape=[shape((rows, hid), F32)] * 2, in_sp...]
  transfers between devices with their start and end apart: 13 -> 9, of which waited for: 7 -> 6; matrix products, arithmetic and copies ran while one was open for 0% -> 1% of each run, Pallas kernels for 4% -> 4%
where the time goes in v3:
time: 228 us
  waiting for transfers between devices  132 us (58%)
  starting transfers between devices  38.3 us (17%)
  Pallas kernels  29.7 us (13%)
  between operations  13.9 us (6%)
  local copies, waits for them, and re-layouts  12.7 us (6%)
    reduce_scatter x1, waiting for transfers between devices, local(): over_x = lax.psum_scatter(partial, 'x', scatter_dimension=0, tiled=True)  41.6 us
    all_gather x1, waiting for transfers between devices, local(): full_in = lax.all_gather(w_in, dp, axis=1, tiled=True)[0]  33.4 us
    all_to_all x3, starting transfers between devices, exchange(): return lax.all_to_all(rows, axes, split_axis=0, concat_axis=0, tiled=True)  28.9 us
    ppermute x3, waiting for transfers between devices, shifted(): return lax.ppermute(value, axis, [(i, (i + k) % n) for i in range(n)])  25.3 us
    reduce_scatter x1, waiting for transfers between devices, local(): lax.psum_scatter(over_x, 'yh', scatter_dimension=0, tiled=True).astype(F32)  17.7 us
    pallas_call x1, Pallas kernels, expert(): pl.pallas_call(expert_kernel, grid=(2 * steps,), out_shape=(pltpu.HBM((so...  14.1 us
    all_to_all x3, waiting for transfers between devices, exchange(): return lax.all_to_all(rows, axes, split_axis=0, concat_axis=0, tiled=True)  13.2 us
    unnamed x32, local copies, waits for them, and re-layouts  10.1 us
  transfers between devices with their start and end apart: 9, of which 6 were waited for; matrix products, arithmetic and copies ran while one was open for 1% of the time, Pallas kernels for 4%

profile of v3, /device:TPU:1, one launch (start us, length us, event | category | flops | bytes accessed | tf_op | source)
XLA Modules:
  0.0 227.6 jit_solution(11615111427432209239)
XLA Ops:
  7.2 1.8 broadcast_in_dim.14
  8.9 7.6 %all-to-all-start.1 = ((bf16[4,64,1024]{2,1,0:T(8,128)(2,1)}), bf16[4,64,1024]{2,1,0:T(8,128)(2,1)S(1)}, u32[]{:S(2)}, u32[]{:S(2)}) async-start(bf16[4,64,1024]{2,1,0:T(8,128)(2,1)} %broadcast_in_dim.14), calls=%async_computation.1 | async-start | bytes 1048576 | tf_op jit(solution)/shard_map/all_to_all | solution.py:353
  16.6 0.8 copy.16.ids_ref
  17.3 0.8 copy.17.gates_ref
  18.1 0.9 copy-done.3
  19.1 0.9 copy-done.5
  20.0 0.9 copy-done.7
  21.0 0.7 copy-done.11
  21.7 0.7 copy-done.13
  22.3 0.7 copy-done.14
  23.0 7.5 %send.1 = (bf16[32,2,16,1024]{3,2,1,0:T(8,128)(2,1)}, f32[128,1024]{1,0:T(8,128)S(1)}, f32[128,128]{1,0:T(8,128)S(1)}) custom-call(s32[128,2]{1,0:T(8,128)S(1)} %copy.16.ids_ref, f32[128,2]{1,0:T(8,128)S(1)} %copy.17.gates_ref, bf16[128,1024]{1,0:T(8,128)(2,1)S(1)} %copy-done.3, bf16[128,1024]{1,0:T(8,128)(2,1)S(1)} %copy-done.5, f32[49,1024]{1,0:T(8,128)S(1)} %copy-done.7, ...), custom_call_target="tpu_custom_call" | custom-call | flops 262144000 | bytes 2097152 | tf_op jit(solution)/shard_map/send/pallas_call | solution.py:269
  30.6 0.8 copy-done.1
  31.4 0.6 copy-done.9
  32.0 11.5 %all-to-all-start = ((bf16[32,2,16,1024]{3,2,1,0:T(8,128)(2,1)}), bf16[32,2,16,1024]{3,2,1,0:T(8,128)(2,1)S(1)}, u32[]{:S(2)}, u32[]{:S(2)}) async-start(bf16[32,2,16,1024]{3,2,1,0:T(8,128)(2,1)} %get-tuple-element.11), calls=%async_computation | async-start | bytes 4194304 | tf_op jit(solution)/shard_map/all_to_all | solution.py:353
  43.6 0.7 all-gather.2.cloned.1.call-update
  44.3 4.4 %collective-permute-start.2 = (bf16[256,1024]{1,0:T(8,128)(2,1)S(1)}, bf16[256,1024]{1,0:T(8,128)(2,1)S(1)}, u32[]{:S(2)}, u32[]{:S(2)}) collective-permute-start(bf16[256,1024]{1,0:T(8,128)(2,1)S(1)} %bitcast.12), channel_id=1, source_target_pairs={{0,384},{128,0},{256,128},{384,256},{1,385},{129,1},{257,129},{385... | collective-permute-start | bytes 1572872 | tf_op jit(solution)/shard_map/ppermute | solution.py:358
  48.7 2.4 %collective-permute-start.1 = (bf16[256,1024]{1,0:T(8,128)(2,1)S(1)}, bf16[256,1024]{1,0:T(8,128)(2,1)}, u32[]{:S(2)}, u32[]{:S(2)}) collective-permute-start(bf16[256,1024]{1,0:T(8,128)(2,1)S(1)} %bitcast.13), channel_id=1, source_target_pairs={{0,256},{128,384},{256,0},{384,128},{1,257},{129,385},{257,1},{385... | collective-permute-start | bytes 1572872 | tf_op jit(solution)/shard_map/ppermute | solution.py:358
  51.2 2.5 %collective-permute-start = (bf16[256,1024]{1,0:T(8,128)(2,1)S(1)}, bf16[256,1024]{1,0:T(8,128)(2,1)}, u32[]{:S(2)}, u32[]{:S(2)}) collective-permute-start(bf16[256,1024]{1,0:T(8,128)(2,1)S(1)} %bitcast.14), channel_id=1, source_target_pairs={{0,128},{128,256},{256,384},{384,0},{1,129},{129,257},{257,385},{3... | collective-permute-start | bytes 1572872 | tf_op jit(solution)/shard_map/ppermute | solution.py:358
  53.7 12.7 %collective-permute-done.2.refs_3_ = bf16[256,1024]{1,0:T(8,128)(2,1)S(1)} collective-permute-done((bf16[256,1024]{1,0:T(8,128)(2,1)S(1)}, bf16[256,1024]{1,0:T(8,128)(2,1)S(1)}, u32[]{:S(2)}, u32[]{:S(2)}) %collective-permute-start.2) | collective-permute-done | bytes 524320 | tf_op jit(solution)/shard_map/ppermute | solution.py:358
  66.4 12.6 %collective-permute-done.refs_1_ = bf16[256,1024]{1,0:T(8,128)(2,1)} collective-permute-done((bf16[256,1024]{1,0:T(8,128)(2,1)S(1)}, bf16[256,1024]{1,0:T(8,128)(2,1)}, u32[]{:S(2)}, u32[]{:S(2)}) %collective-permute-start) | collective-permute-done | bytes 524320 | tf_op jit(solution)/shard_map/ppermute | solution.py:358
  79.0 1.3 place.1
  80.4 1.4 copy-done
  81.7 33.4 %all-gather.2.cloned.1.call-done = bf16[1,1024,1024]{2,1,0:T(8,128)(2,1)} async-done(((bf16[1,64,1024]{2,1,0:T(8,128)(2,1)}), bf16[1,1024,1024]{2,1,0:T(8,128)(2,1)}) %all-gather.2.cloned.1.call-update) | async-done | bytes 2097168 | tf_op jit(solution)/shard_map/all_gather | solution.py:390
  115.1 14.1 %expert.1 = (bf16[32,2,16,1024]{3,2,1,0:T(8,128)(2,1)}, bf16[1024,2048]{1,0:T(8,128)(2,1)}) custom-call(bf16[32,2,16,1024]{3,2,1,0:T(8,128)(2,1)S(1)} %all-to-all-done.moved_ref, bf16[1024,1024]{1,0:T(8,128)(2,1)} %bitcast.22, bf16[1024,1024]{1,0:T(8,128)(2,1)} %bitcast.16), custom_call_target="tpu_custom_call" | custom-call | flops 6442450944 | bytes 12582912 | tf_op jit(solution)/shard_map/expert/pallas_call | solution.py:312
  129.3 9.7 %all-to-all-start.2 = ((bf16[32,2,16,1024]{3,2,1,0:T(8,128)(2,1)}), bf16[32,2,16,1024]{3,2,1,0:T(8,128)(2,1)S(1)}, u32[]{:S(2)}, u32[]{:S(2)}) async-start(bf16[32,2,16,1024]{3,2,1,0:T(8,128)(2,1)} %get-tuple-element.12), calls=%async_computation.2 | async-start | bytes 4194304 | tf_op jit(solution)/shard_map/all_to_all | solution.py:353
  139.1 41.6 %reduce-scatter.3.cloned.1.call-done = bf16[256,2048]{1,0:T(8,128)(2,1)} async-done(((bf16[1024,2048]{1,0:T(8,128)(2,1)}), bf16[256,2048]{1,0:T(8,128)(2,1)}) %reduce-scatter.3.cloned.1.call-update) | async-done | bytes 1048592 | tf_op jit(solution)/shard_map/reduce_scatter | solution.py:405
  180.7 13.2 %all-to-all-done.2.back_ref = bf16[32,2,16,1024]{3,2,1,0:T(8,128)(2,1)S(1)} async-done(((bf16[32,2,16,1024]{3,2,1,0:T(8,128)(2,1)}), bf16[32,2,16,1024]{3,2,1,0:T(8,128)(2,1)S(1)}, u32[]{:S(2)}, u32[]{:S(2)}) %all-to-all-start.2) | async-done | bytes 2097184 | tf_op jit(solution)/shard_map/all_to_all | solution.py:353
  194.0 0.8 copy-done.10
  194.8 6.8 %finish.1 = (bf16[128,1024]{1,0:T(8,128)(2,1)}, f32[128,1024]{1,0:T(8,128)}) custom-call(s32[128,2]{1,0:T(8,128)S(1)} %copy.16.ids_ref, f32[128,2]{1,0:T(8,128)S(1)} %copy.17.gates_ref, bf16[32,2,16,1024]{3,2,1,0:T(8,128)(2,1)S(1)} %all-to-all-done.2.back_ref, f32[128,1024]{1,0:T(8,128)S(1)} %copy-done.2, f32[128,128]{1,0:T(8,128)S(1)} %copy-done.10, ...), custom_call_target="tpu_custom_call" | custom-call | flops 262144000 | bytes 2097152 | tf_op jit(solution)/shard_map/finish/pallas_call | solution.py:290
  201.6 17.7 %reduce-scatter.5.cloned.1.call-done = bf16[64,2048]{1,0:T(8,128)(2,1)} async-done(((bf16[256,2048]{1,0:T(8,128)(2,1)}), bf16[64,2048]{1,0:T(8,128)(2,1)}) %reduce-scatter.5.cloned.1.call-update) | async-done | bytes 262160 | tf_op jit(solution)/shard_map/reduce_scatter | solution.py:407
  219.3 1.0 convert_element_type.3
  220.3 0.8 slice_bitcast_fusion
  (28 shorter events, 0.2 us)
Async XLA Ops:
  8.9 23.1 %all-to-all-start.1 = ((bf16[4,64,1024]{2,1,0:T(8,128)(2,1)}), bf16[4,64,1024]{2,1,0:T(8,128)(2,1)S(1)}, u32[]{:S(2)}, u32[]{:S(2)}) async-start(bf16[4,64,1024]{2,1,0:T(8,128)(2,1)} %broadcast_in_dim.14), calls=%async_computation.1 | async-start | bytes 1048576 | tf_op jit(solution)/shard_map/all_to_all | solution.py:353
  18.1 0.9 copy-start.3
  19.1 0.9 copy-start.5
  20.0 0.9 copy-start.7
  21.0 0.7 copy-start.11
  21.7 0.7 copy-start.13
  22.3 0.7 copy-start.14
  30.6 0.8 copy-start.1
  31.4 0.6 copy-start.9
  32.0 83.1 %all-to-all-start = ((bf16[32,2,16,1024]{3,2,1,0:T(8,128)(2,1)}), bf16[32,2,16,1024]{3,2,1,0:T(8,128)(2,1)S(1)}, u32[]{:S(2)}, u32[]{:S(2)}) async-start(bf16[32,2,16,1024]{3,2,1,0:T(8,128)(2,1)} %get-tuple-element.11), calls=%async_computation | async-start | bytes 4194304 | tf_op jit(solution)/shard_map/all_to_all | solution.py:353
  43.5 71.6 %all-gather.2.cloned.1.call-start = ((), (), s32[]{:S(2)}) async-start(), calls=%async_computation.5 | async-start | bytes 2228224 | tf_op jit(solution)/shard_map/all_gather | solution.py:390
  44.3 136.4 %reduce-scatter.3.cloned.1.call-start = ((), (), s32[]{:S(2)}) async-start(), calls=%async_computation.6 | async-start | bytes 5242880 | tf_op jit(solution)/shard_map/reduce_scatter | solution.py:405
  44.3 22.0 %collective-permute-start.2 = (bf16[256,1024]{1,0:T(8,128)(2,1)S(1)}, bf16[256,1024]{1,0:T(8,128)(2,1)S(1)}, u32[]{:S(2)}, u32[]{:S(2)}) collective-permute-start(bf16[256,1024]{1,0:T(8,128)(2,1)S(1)} %bitcast.12), channel_id=1, source_target_pairs={{0,384},{128,0},{256,128},{384,256},{1,385},{129,1},{257,129},{385... | collective-permute-start | bytes 1572872 | tf_op jit(solution)/shard_map/ppermute | solution.py:358
  48.7 17.6 %collective-permute-start.1 = (bf16[256,1024]{1,0:T(8,128)(2,1)S(1)}, bf16[256,1024]{1,0:T(8,128)(2,1)}, u32[]{:S(2)}, u32[]{:S(2)}) collective-permute-start(bf16[256,1024]{1,0:T(8,128)(2,1)S(1)} %bitcast.13), channel_id=1, source_target_pairs={{0,256},{128,384},{256,0},{384,128},{1,257},{129,385},{257,1},{385... | collective-permute-start | bytes 1572872 | tf_op jit(solution)/shard_map/ppermute | solution.py:358
  51.2 27.8 %collective-permute-start = (bf16[256,1024]{1,0:T(8,128)(2,1)S(1)}, bf16[256,1024]{1,0:T(8,128)(2,1)}, u32[]{:S(2)}, u32[]{:S(2)}) collective-permute-start(bf16[256,1024]{1,0:T(8,128)(2,1)S(1)} %bitcast.14), channel_id=1, source_target_pairs={{0,128},{128,256},{256,384},{384,0},{1,129},{129,257},{257,385},{3... | collective-permute-start | bytes 1572872 | tf_op jit(solution)/shard_map/ppermute | solution.py:358
  80.3 1.4 copy-start
  129.3 64.7 %copy-start.2 = (f32[128,1024]{1,0:T(8,128)S(1)}, f32[128,1024]{1,0:T(8,128)}, u32[]{:S(2)}) copy-start(f32[128,1024]{1,0:T(8,128)} %copy-done.1) | copy-start | bytes 1572868
  129.3 64.7 %copy-start.4 = (bf16[128,1024]{1,0:T(8,128)(2,1)S(1)}, bf16[128,1024]{1,0:T(8,128)(2,1)}, u32[]{:S(2)}) copy-start(bf16[128,1024]{1,0:T(8,128)(2,1)} %cot_ref.3) | copy-start | bytes 786436
  129.3 64.7 %copy-start.6 = (bf16[128,1024]{1,0:T(8,128)(2,1)S(1)}, bf16[128,1024]{1,0:T(8,128)(2,1)}, u32[]{:S(2)}) copy-start(bf16[128,1024]{1,0:T(8,128)(2,1)} %x_ref.3) | copy-start | bytes 786436
  129.3 64.7 %copy-start.8 = (f32[49,1024]{1,0:T(8,128)S(1)}, f32[49,1024]{1,0:T(8,128)}, u32[]{:S(2)}) copy-start(f32[49,1024]{1,0:T(8,128)} %taps_ref.3) | copy-start | bytes 602116
  129.3 64.7 %copy-start.12 = (f32[1024]{0:T(1024)S(1)}, f32[1024]{0:T(1024)}, u32[]{:S(2)}) copy-start(f32[1024]{0:T(1024)} %param.15) | copy-start | bytes 12292
  129.3 64.6 %all-to-all-start.2 = ((bf16[32,2,16,1024]{3,2,1,0:T(8,128)(2,1)}), bf16[32,2,16,1024]{3,2,1,0:T(8,128)(2,1)S(1)}, u32[]{:S(2)}, u32[]{:S(2)}) async-start(bf16[32,2,16,1024]{3,2,1,0:T(8,128)(2,1)} %get-tuple-element.12), calls=%async_computation.2 | async-start | bytes 4194304 | tf_op jit(solution)/shard_map/all_to_all | solution.py:353
  139.0 80.3 %reduce-scatter.5.cloned.1.call-start = ((), (), s32[]{:S(2)}) async-start(), calls=%async_computation.7 | async-start | bytes 1310720 | tf_op jit(solution)/shard_map/reduce_scatter | solution.py:407
  194.0 0.8 copy-start.10
Sparse Core Ops, SparseCore 0:
  47.4 67.7 all-gather.1
  129.4 51.2 reduce-scatter.2
  183.5 35.7 reduce-scatter.4

commit v4 on v3

--- a/solution.py
+++ b/solution.py
@@ -183,23 +183,13 @@
 SQRT_2_OVER_PI = 0.7978845608028654
 
 
-def expert_kernel(
-    moved_ref,
-    w_in_ref,
-    w_out_ref,
-    back_ref,
-    terms_ref,
-    hidden_s,
-    gh_s,
-    grad_total,
-    out_total,
-):
+def expert_kernel(moved_ref, w_in_ref, w_out_ref, terms_ref, hidden_ref, gh_ref):
     step = pl.program_id(0)
     steps = pl.num_programs(0) // 2
     sources, _, count, width = moved_ref.shape
     flat = sources * count
     block = w_in_ref.shape[1]
-    hid = hidden_s.shape[0] * block
+    hid = hidden_ref.shape[1]
 
     @pl.when(step < steps)
     def _():
@@ -208,41 +198,28 @@
         square = pre * pre
         t = jnp.tanh(SQRT_2_OVER_PI * (pre + 0.044715 * (pre * square)))
         cdf = 0.5 * (1.0 + t)
-        hidden = (pre * cdf).astype(BF16)
         slope = cdf + pre * (0.5 * (1.0 - t * t)) * (
             SQRT_2_OVER_PI * (1.0 + (3 * 0.044715) * square)
         )
-        gh = (raw * slope).astype(BF16)
-        hidden_s[step] = hidden
-        gh_s[step] = gh
-        grad_part = contract_last(gh, w_in_ref[...])
-        out_part = contract_last(hidden, w_out_ref[...])
-
-        @pl.when(step == 0)
-        def _():
-            grad_total[...] = grad_part
-            out_total[...] = out_part
-
-        @pl.when(step > 0)
-        def _():
-            grad_total[...] += grad_part
-            out_total[...] += out_part
-
-    @pl.when(step == steps - 1)
-    def _():
-        back_ref[:, 0] = grad_total[...].astype(BF16).reshape(sources, count, width)
-        back_ref[:, 1] = out_total[...].astype(BF16).reshape(sources, count, width)
+        lanes = pl.ds(pl.multiple_of(step * block, block), block)
+        hidden_ref[:, lanes] = (pre * cdf).astype(BF16)
+        gh_ref[:, lanes] = (raw * slope).astype(BF16)
 
     @pl.when(step >= steps)
     def _():
         lanes = pl.ds(pl.multiple_of((step - steps) * block, block), block)
         rows = moved_ref[:, 0, :, lanes].reshape(flat, block)
         grads = moved_ref[:, 1, :, lanes].reshape(flat, block)
-        for j in range(hidden_s.shape[0]):
-            at = slice(j * block, (j + 1) * block)
-            terms_ref[:, at] = contract_first(rows, gh_s[j]).astype(BF16)
-            at = slice(hid + j * block, hid + (j + 1) * block)
-            terms_ref[:, at] = contract_first(grads, hidden_s[j]).astype(BF16)
+        terms_ref[:, :hid] = contract_first(rows, gh_ref[...]).astype(BF16)
+        terms_ref[:, hid:] = contract_first(grads, hidden_ref[...]).astype(BF16)
+
+
+def return_kernel(hidden_ref, gh_ref, w_in_ref, w_out_ref, back_ref):
+    sources, _, count, block = back_ref.shape
+    grad = contract_last(gh_ref[...], w_in_ref[...]).astype(BF16)
+    back_ref[:, 0] = grad.reshape(sources, count, block)
+    out = contract_last(hidden_ref[...], w_out_ref[...]).astype(BF16)
+    back_ref[:, 1] = out.reshape(sources, count, block)
 
 
 def place_kernel(where_ref, *refs):
@@ -299,38 +276,62 @@
     )(ids, gates, back, xhat, rstd, gain.reshape(1, width), taps, cot, x)
 
 
+def in_hbm(array):
+    return pltpu.with_memory_space_constraint(array, pltpu.HBM)
+
+
 def expert(moved, w_in, w_out):
     sources, _, count, width = moved.shape
     flat = sources * count
     hid = w_in.shape[1]
     block = 256
     steps = hid // block
-    whole = pl.BlockSpec(
-        (sources, 2, count, width), lambda j: (0, 0, 0, 0), pipeline_mode=pl.Buffered(1)
-    )
+    once = pl.Buffered(1)
     weight = pl.BlockSpec((width, block), lambda j: (0, jnp.minimum(j, steps - 1)))
+    whole = pl.BlockSpec((flat, hid), lambda j: (0, 0))
     return pl.pallas_call(
         expert_kernel,
         grid=(2 * steps,),
         out_shape=(
-            pltpu.HBM((sources, 2, count, width), BF16),
             pltpu.HBM((width, 2 * hid), BF16),
+            pltpu.HBM((flat, hid), BF16),
+            pltpu.HBM((flat, hid), BF16),
         ),
-        in_specs=[whole, weight, weight],
+        in_specs=[
+            pl.BlockSpec(
+                (sources, 2, count, width), lambda j: (0, 0, 0, 0), pipeline_mode=once
+            ),
+            weight,
+            weight,
+        ],
         out_specs=[
-            pl.BlockSpec((sources, 2, count, width), lambda j: (0, 0, 0, 0)),
             pl.BlockSpec((block, 2 * hid), lambda j: (jnp.maximum(j - steps, 0), 0)),
+            whole,
+            whole,
         ],
-        scratch_shapes=[
-            pltpu.VMEM((steps, flat, block), BF16),
-            pltpu.VMEM((steps, flat, block), BF16),
-            pltpu.VMEM((flat, width), F32),
-            pltpu.VMEM((flat, width), F32),
-        ],
-        compiler_params=params(32),
-        cost_estimate=cost(12 * flat * width * hid, 12 * MIB),
+        compiler_params=params(20),
+        cost_estimate=cost(8 * flat * width * hid, 12 * MIB),
         name="expert",
-    )(moved, *(pltpu.with_memory_space_constraint(w, pltpu.HBM) for w in (w_in, w_out)))
+    )(moved, in_hbm(w_in), in_hbm(w_out))
+
+
+def return_rows(hidden, gh, w_in, w_out, sources):
+    flat, hid = hidden.shape
+    width = w_in.shape[0]
+    block = 256
+    count = flat // sources
+    whole = pl.BlockSpec((flat, hid), lambda j: (0, 0), pipeline_mode=pl.Buffered(1))
+    weight = pl.BlockSpec((block, hid), lambda j: (j, 0))
+    return pl.pallas_call(
+        return_kernel,
+        grid=(width // block,),
+        out_shape=pltpu.HBM((sources, 2, count, width), BF16),
+        in_specs=[whole, whole, weight, weight],
+        out_specs=pl.BlockSpec((sources, 2, count, block), lambda j: (0, 0, 0, j)),
+        compiler_params=params(16),
+        cost_estimate=cost(4 * flat * width * hid, 8 * MIB),
+        name="return_rows",
+    )(*(in_hbm(v) for v in (hidden, gh, w_in, w_out)))
 
 
 SMEM = pl.BlockSpec(memory_space=pltpu.SMEM)
@@ -401,10 +402,10 @@
     moved = exchange(sent, ep)
     along_y = gather_y(w_out[0])
     full_out = gather_by("x", along_y.reshape(-1, hid)).reshape(-1, hid)
-    back, partial = expert(moved, full_in, full_out)
-    over_x = lax.psum_scatter(partial, "x", scatter_dimension=0, tiled=True)
+    partial, hidden, gh = expert(moved, full_in, full_out)
+    total = lax.psum_scatter(partial, dp, scatter_dimension=0, tiled=True).astype(F32)
+    back = return_rows(hidden, gh, full_in, full_out, moved.shape[0])
     returned = exchange(back, ep)
-    total = lax.psum_scatter(over_x, "yh", scatter_dimension=0, tiled=True).astype(F32)
     mixed, grad_input = finish(
         expert_ids,
         gate_weights,

time: 228 us -> 238 us (1.044)
  blocking collectives: 0 us -> 67.7 us
  waiting for transfers between devices: 132 us -> 81.2 us
  starting transfers between devices: 38.3 us -> 29.1 us
  Pallas kernels: 29.7 us -> 32.4 us
    all_to_all x0 -> x1, blocking collectives: none -> 67.7 us  [exchange(): return lax.all_to_all(rows, axes, split_axis=0, concat_axis=0, tiled=True)]
    reduce_scatter x2 -> x1, waiting for transfers between devices: 59.3 us -> 22.2 us  [local(): lax.psum_scatter(partial, dp, scatter_dimension=0, tiled=True).astype(F32)]
    all_to_all x3 -> x2, waiting for transfers between devices: 13.2 us -> 0.01 us  [exchange(): return lax.all_to_all(rows, axes, split_axis=0, concat_axis=0, tiled=True)]
    all_to_all x3 -> x2, starting transfers between devices: 28.9 us -> 19.7 us  [exchange(): return lax.all_to_all(rows, axes, split_axis=0, concat_axis=0, tiled=True)]
    pallas_call x1 -> x2, Pallas kernels: 14.1 us -> 16.8 us  [the longest x1 10.3 us: expert(): pl.pallas_call(expert_kernel, grid=(2 * steps,), out_shape=(pltpu.HBM((wi...]
    unnamed x32 -> x28, local copies, waits for them, and re-layouts: 10.1 us -> 8.71 us
  transfers between devices with their start and end apart: 9 -> 7, of which waited for: 6 -> 4; matrix products, arithmetic and copies ran while one was open for 1% -> 1% of each run, Pallas kernels for 4% -> 6%
where the time goes in v4:
time: 238 us; the launch traced here: 237 us
  waiting for transfers between devices  81.2 us (34%)
  blocking collectives  67.7 us (28%)
  Pallas kernels  32.4 us (14%)
  starting transfers between devices  29.1 us (12%)
  between operations  14.1 us (6%)
  local copies, waits for them, and re-layouts  11.3 us (5%)
    all_to_all x1, blocking collectives, exchange(): return lax.all_to_all(rows, axes, split_axis=0, concat_axis=0, tiled=True)  67.7 us
    all_gather x1, waiting for transfers between devices, local(): full_in = lax.all_gather(w_in, dp, axis=1, tiled=True)[0]  32.9 us
    ppermute x3, waiting for transfers between devices, shifted(): return lax.ppermute(value, axis, [(i, (i + k) % n) for i in range(n)])  25.4 us
    reduce_scatter x1, waiting for transfers between devices, local(): lax.psum_scatter(partial, dp, scatter_dimension=0, tiled=True).astype(F32)  22.2 us
    all_to_all x2, starting transfers between devices, exchange(): return lax.all_to_all(rows, axes, split_axis=0, concat_axis=0, tiled=True)  19.7 us
    pallas_call x1, Pallas kernels, expert(): pl.pallas_call(expert_kernel, grid=(2 * steps,), out_shape=(pltpu.HBM((wi...  10.3 us
    ppermute x3, starting transfers between devices, shifted(): return lax.ppermute(value, axis, [(i, (i + k) % n) for i in range(n)])  9.33 us
    unnamed x28, local copies, waits for them, and re-layouts  8.71 us
  transfers between devices with their start and end apart: 7, of which 4 were waited for; matrix products, arithmetic and copies ran while one was open for 1% of the time, Pallas kernels for 6%

profile of v4, /device:TPU:1, one launch (start us, length us, event | category | flops | bytes accessed | tf_op | source)
XLA Modules:
  0.0 236.8 jit_solution(12658550454900055388)
XLA Ops:
  7.2 1.8 broadcast_in_dim.14
  8.9 7.6 %all-to-all-start.1 = ((bf16[4,64,1024]{2,1,0:T(8,128)(2,1)}), bf16[4,64,1024]{2,1,0:T(8,128)(2,1)S(1)}, u32[]{:S(2)}, u32[]{:S(2)}) async-start(bf16[4,64,1024]{2,1,0:T(8,128)(2,1)} %broadcast_in_dim.14), calls=%async_computation.1 | async-start | bytes 1048576 | tf_op jit(solution)/shard_map/all_to_all | solution.py:354
  16.6 0.8 copy.16.ids_ref
  17.3 0.8 copy.17.gates_ref
  18.1 0.9 copy-done.3
  19.1 0.9 copy-done.5
  20.0 0.9 copy-done.7
  21.0 0.7 copy-done.9
  21.7 0.7 copy-done.11
  22.3 0.7 copy-done.12
  23.0 7.5 %send.1 = (bf16[32,2,16,1024]{3,2,1,0:T(8,128)(2,1)}, f32[128,1024]{1,0:T(8,128)S(1)}, f32[128,128]{1,0:T(8,128)S(1)}) custom-call(s32[128,2]{1,0:T(8,128)S(1)} %copy.16.ids_ref, f32[128,2]{1,0:T(8,128)S(1)} %copy.17.gates_ref, bf16[128,1024]{1,0:T(8,128)(2,1)S(1)} %copy-done.3, bf16[128,1024]{1,0:T(8,128)(2,1)S(1)} %copy-done.5, f32[49,1024]{1,0:T(8,128)S(1)} %copy-done.7, ...), custom_call_target="tpu_custom_call" | custom-call | flops 262144000 | bytes 2097152 | tf_op jit(solution)/shard_map/send/pallas_call | solution.py:246
  30.5 0.8 copy-done.1
  31.4 12.0 %all-to-all-start = ((bf16[32,2,16,1024]{3,2,1,0:T(8,128)(2,1)}), bf16[32,2,16,1024]{3,2,1,0:T(8,128)(2,1)S(1)}, u32[]{:S(2)}, u32[]{:S(2)}) async-start(bf16[32,2,16,1024]{3,2,1,0:T(8,128)(2,1)} %get-tuple-element.12), calls=%async_computation | async-start | bytes 4194304 | tf_op jit(solution)/shard_map/all_to_all | solution.py:354
  43.4 0.0 all-gather.2.cloned.1.call-start
  43.5 0.7 all-gather.2.cloned.1.call-update
  44.2 0.0 reduce-scatter.2.cloned.1.call-start
  44.2 4.4 %collective-permute-start.2 = (bf16[256,1024]{1,0:T(8,128)(2,1)S(1)}, bf16[256,1024]{1,0:T(8,128)(2,1)S(1)}, u32[]{:S(2)}, u32[]{:S(2)}) collective-permute-start(bf16[256,1024]{1,0:T(8,128)(2,1)S(1)} %bitcast.14), channel_id=1, source_target_pairs={{0,384},{128,0},{256,128},{384,256},{1,385},{129,1},{257,129},{385... | collective-permute-start | bytes 1572872 | tf_op jit(solution)/shard_map/ppermute | solution.py:359
  48.6 2.4 %collective-permute-start.1 = (bf16[256,1024]{1,0:T(8,128)(2,1)S(1)}, bf16[256,1024]{1,0:T(8,128)(2,1)}, u32[]{:S(2)}, u32[]{:S(2)}) collective-permute-start(bf16[256,1024]{1,0:T(8,128)(2,1)S(1)} %bitcast.15), channel_id=1, source_target_pairs={{0,256},{128,384},{256,0},{384,128},{1,257},{129,385},{257,1},{385... | collective-permute-start | bytes 1572872 | tf_op jit(solution)/shard_map/ppermute | solution.py:359
  51.1 2.5 %collective-permute-start = (bf16[256,1024]{1,0:T(8,128)(2,1)S(1)}, bf16[256,1024]{1,0:T(8,128)(2,1)}, u32[]{:S(2)}, u32[]{:S(2)}) collective-permute-start(bf16[256,1024]{1,0:T(8,128)(2,1)S(1)} %bitcast.16), channel_id=1, source_target_pairs={{0,128},{128,256},{256,384},{384,0},{1,129},{129,257},{257,385},{3... | collective-permute-start | bytes 1572872 | tf_op jit(solution)/shard_map/ppermute | solution.py:359
  53.6 12.2 %collective-permute-done.2.refs_3_ = bf16[256,1024]{1,0:T(8,128)(2,1)S(1)} collective-permute-done((bf16[256,1024]{1,0:T(8,128)(2,1)S(1)}, bf16[256,1024]{1,0:T(8,128)(2,1)S(1)}, u32[]{:S(2)}, u32[]{:S(2)}) %collective-permute-start.2) | collective-permute-done | bytes 524320 | tf_op jit(solution)/shard_map/ppermute | solution.py:359
  65.8 13.2 %collective-permute-done.refs_1_ = bf16[256,1024]{1,0:T(8,128)(2,1)} collective-permute-done((bf16[256,1024]{1,0:T(8,128)(2,1)S(1)}, bf16[256,1024]{1,0:T(8,128)(2,1)}, u32[]{:S(2)}, u32[]{:S(2)}) %collective-permute-start) | collective-permute-done | bytes 524320 | tf_op jit(solution)/shard_map/ppermute | solution.py:359
  79.0 1.3 place.1
  80.3 1.4 copy-done
  81.7 32.9 %all-gather.2.cloned.1.call-done = bf16[1,1024,1024]{2,1,0:T(8,128)(2,1)} async-done(((bf16[1,64,1024]{2,1,0:T(8,128)(2,1)}), bf16[1,1024,1024]{2,1,0:T(8,128)(2,1)}) %all-gather.2.cloned.1.call-update) | async-done | bytes 2097168 | tf_op jit(solution)/shard_map/all_gather | solution.py:391
  114.6 10.3 %expert.1 = (bf16[1024,2048]{1,0:T(8,128)(2,1)}, bf16[512,1024]{1,0:T(8,128)(2,1)}, bf16[512,1024]{1,0:T(8,128)(2,1)}) custom-call(bf16[32,2,16,1024]{3,2,1,0:T(8,128)(2,1)S(1)} %all-to-all-done.moved_ref, bf16[1024,1024]{1,0:T(8,128)(2,1)} %bitcast.22, bf16[1024,1024]{1,0:T(8,128)(2,1)} %bitcast.12), custom_call_target="tpu_custom_call" | custom-call | flops 4294967296 | bytes 12582912 | tf_op jit(solution)/shard_map/expert/pallas_call | solution.py:292
  124.9 0.0 reduce-scatter.2.cloned.1.call-update
  124.9 6.5 %return_rows.1 = bf16[32,2,16,1024]{3,2,1,0:T(8,128)(2,1)} custom-call(bf16[512,1024]{1,0:T(8,128)(2,1)} %get-tuple-element.13.hidden_ref, bf16[512,1024]{1,0:T(8,128)(2,1)} %get-tuple-element.14.gh_ref, bf16[1024,1024]{1,0:T(8,128)(2,1)} %bitcast.23, bf16[1024,1024]{1,0:T(8,128)(2,1)} %bitcast.13), custom_call_target="tpu_custom_call" | custom-call | flops 2147483648 | bytes 8388608 | tf_op jit(solution)/shard_map/return_rows/pallas_call | solution.py:325
  131.4 67.7 %all_to_all.15.back_ref = bf16[32,2,16,1024]{3,2,1,0:T(8,128)(2,1)S(1)} all-to-all(bf16[32,2,16,1024]{3,2,1,0:T(8,128)(2,1)} %return_rows.1), channel_id=1, replica_groups=mesh['x'=4,'yh'=4,'z'=8,'yl'=2,'core'=2] {'z','yl','core'}, dimensions={0} | all-to-all | bytes 4194304 | tf_op jit(solution)/shard_map/all_to_all | solution.py:354
  199.2 6.7 %finish.1 = (bf16[128,1024]{1,0:T(8,128)(2,1)}, f32[128,1024]{1,0:T(8,128)}) custom-call(s32[128,2]{1,0:T(8,128)S(1)} %copy.16.ids_ref, f32[128,2]{1,0:T(8,128)S(1)} %copy.17.gates_ref, bf16[32,2,16,1024]{3,2,1,0:T(8,128)(2,1)S(1)} %all_to_all.15.back_ref, f32[128,1024]{1,0:T(8,128)S(1)} %copy-done.2, f32[128,128]{1,0:T(8,128)S(1)} %get-tuple-element.16.rstd_ref, ...), custom_call_target="tpu_custom_call" | custom-call | flops 262144000 | bytes 2097152 | tf_op jit(solution)/shard_map/finish/pallas_call | solution.py:267
  205.9 22.2 %reduce-scatter.2.cloned.1.call-done = bf16[64,2048]{1,0:T(8,128)(2,1)} async-done(((bf16[1024,2048]{1,0:T(8,128)(2,1)}), bf16[64,2048]{1,0:T(8,128)(2,1)}) %reduce-scatter.2.cloned.1.call-update) | async-done | bytes 262160 | tf_op jit(solution)/shard_map/reduce_scatter | solution.py:406
  228.1 1.0 convert_element_type.3
  229.1 0.8 slice_bitcast_fusion
  (21 shorter events, 0.0 us)
Async XLA Ops:
  8.9 22.5 %all-to-all-start.1 = ((bf16[4,64,1024]{2,1,0:T(8,128)(2,1)}), bf16[4,64,1024]{2,1,0:T(8,128)(2,1)S(1)}, u32[]{:S(2)}, u32[]{:S(2)}) async-start(bf16[4,64,1024]{2,1,0:T(8,128)(2,1)} %broadcast_in_dim.14), calls=%async_computation.1 | async-start | bytes 1048576 | tf_op jit(solution)/shard_map/all_to_all | solution.py:354
  18.1 0.9 copy-start.3
  19.1 0.9 copy-start.5
  20.0 0.9 copy-start.7
  21.0 0.7 copy-start.9
  21.7 0.7 copy-start.11
  22.3 0.7 copy-start.12
  30.5 0.8 copy-start.1
  31.4 83.2 %all-to-all-start = ((bf16[32,2,16,1024]{3,2,1,0:T(8,128)(2,1)}), bf16[32,2,16,1024]{3,2,1,0:T(8,128)(2,1)S(1)}, u32[]{:S(2)}, u32[]{:S(2)}) async-start(bf16[32,2,16,1024]{3,2,1,0:T(8,128)(2,1)} %get-tuple-element.12), calls=%async_computation | async-start | bytes 4194304 | tf_op jit(solution)/shard_map/all_to_all | solution.py:354
  43.4 71.1 %all-gather.2.cloned.1.call-start = ((), (), s32[]{:S(2)}) async-start(), calls=%async_computation.4 | async-start | bytes 2228224 | tf_op jit(solution)/shard_map/all_gather | solution.py:391
  44.2 183.9 %reduce-scatter.2.cloned.1.call-start = ((), (), s32[]{:S(2)}) async-start(), calls=%async_computation.5 | async-start | bytes 4456448 | tf_op jit(solution)/shard_map/reduce_scatter | solution.py:406
  44.2 21.5 %collective-permute-start.2 = (bf16[256,1024]{1,0:T(8,128)(2,1)S(1)}, bf16[256,1024]{1,0:T(8,128)(2,1)S(1)}, u32[]{:S(2)}, u32[]{:S(2)}) collective-permute-start(bf16[256,1024]{1,0:T(8,128)(2,1)S(1)} %bitcast.14), channel_id=1, source_target_pairs={{0,384},{128,0},{256,128},{384,256},{1,385},{129,1},{257,129},{385... | collective-permute-start | bytes 1572872 | tf_op jit(solution)/shard_map/ppermute | solution.py:359
  48.6 17.1 %collective-permute-start.1 = (bf16[256,1024]{1,0:T(8,128)(2,1)S(1)}, bf16[256,1024]{1,0:T(8,128)(2,1)}, u32[]{:S(2)}, u32[]{:S(2)}) collective-permute-start(bf16[256,1024]{1,0:T(8,128)(2,1)S(1)} %bitcast.15), channel_id=1, source_target_pairs={{0,256},{128,384},{256,0},{384,128},{1,257},{129,385},{257,1},{385... | collective-permute-start | bytes 1572872 | tf_op jit(solution)/shard_map/ppermute | solution.py:359
  51.1 27.9 %collective-permute-start = (bf16[256,1024]{1,0:T(8,128)(2,1)S(1)}, bf16[256,1024]{1,0:T(8,128)(2,1)}, u32[]{:S(2)}, u32[]{:S(2)}) collective-permute-start(bf16[256,1024]{1,0:T(8,128)(2,1)S(1)} %bitcast.16), channel_id=1, source_target_pairs={{0,128},{128,256},{256,384},{384,0},{1,129},{129,257},{257,385},{3... | collective-permute-start | bytes 1572872 | tf_op jit(solution)/shard_map/ppermute | solution.py:359
  80.3 1.4 copy-start
  131.4 67.8 %copy-start.2 = (f32[128,1024]{1,0:T(8,128)S(1)}, f32[128,1024]{1,0:T(8,128)}, u32[]{:S(2)}) copy-start(f32[128,1024]{1,0:T(8,128)} %copy-done.1) | copy-start | bytes 1572868
  131.4 67.8 %copy-start.4 = (bf16[128,1024]{1,0:T(8,128)(2,1)S(1)}, bf16[128,1024]{1,0:T(8,128)(2,1)}, u32[]{:S(2)}) copy-start(bf16[128,1024]{1,0:T(8,128)(2,1)} %cot_ref.3) | copy-start | bytes 786436
  131.4 67.8 %copy-start.6 = (bf16[128,1024]{1,0:T(8,128)(2,1)S(1)}, bf16[128,1024]{1,0:T(8,128)(2,1)}, u32[]{:S(2)}) copy-start(bf16[128,1024]{1,0:T(8,128)(2,1)} %x_ref.3) | copy-start | bytes 786436
  131.4 67.8 %copy-start.8 = (f32[49,1024]{1,0:T(8,128)S(1)}, f32[49,1024]{1,0:T(8,128)}, u32[]{:S(2)}) copy-start(f32[49,1024]{1,0:T(8,128)} %taps_ref.3) | copy-start | bytes 602116
  131.4 67.8 %copy-start.10 = (f32[1024]{0:T(1024)S(1)}, f32[1024]{0:T(1024)}, u32[]{:S(2)}) copy-start(f32[1024]{0:T(1024)} %param.15) | copy-start | bytes 12292
Sparse Core Ops, SparseCore 0:
  47.3 67.2 all-gather.1
  125.0 103.0 reduce-scatter.1

commit v5 on v4

--- a/solution.py
+++ b/solution.py
@@ -183,13 +183,27 @@
 SQRT_2_OVER_PI = 0.7978845608028654
 
 
-def expert_kernel(moved_ref, w_in_ref, w_out_ref, terms_ref, hidden_ref, gh_ref):
+def expert_kernel(
+    where_ref,
+    moved_ref,
+    w_in_ref,
+    w_out_ref,
+    term_ref,
+    own_ref,
+    after_ref,
+    far_ref,
+    before_ref,
+    hidden_ref,
+    gh_ref,
+    hidden_s,
+    gh_s,
+):
     step = pl.program_id(0)
-    steps = pl.num_programs(0) // 2
     sources, _, count, width = moved_ref.shape
     flat = sources * count
     block = w_in_ref.shape[1]
-    hid = hidden_ref.shape[1]
+    part = term_ref.shape[0]
+    steps = hidden_s.shape[1] // block
 
     @pl.when(step < steps)
     def _():
@@ -202,16 +216,26 @@
             SQRT_2_OVER_PI * (1.0 + (3 * 0.044715) * square)
         )
         lanes = pl.ds(pl.multiple_of(step * block, block), block)
-        hidden_ref[:, lanes] = (pre * cdf).astype(BF16)
-        gh_ref[:, lanes] = (raw * slope).astype(BF16)
+        hidden = (pre * cdf).astype(BF16)
+        gh = (raw * slope).astype(BF16)
+        hidden_s[:, lanes] = hidden
+        gh_s[:, lanes] = gh
+        hidden_ref[...] = hidden
+        gh_ref[...] = gh
 
     @pl.when(step >= steps)
     def _():
-        lanes = pl.ds(pl.multiple_of((step - steps) * block, block), block)
-        rows = moved_ref[:, 0, :, lanes].reshape(flat, block)
-        grads = moved_ref[:, 1, :, lanes].reshape(flat, block)
-        terms_ref[:, :hid] = contract_first(rows, gh_ref[...]).astype(BF16)
-        terms_ref[:, hid:] = contract_first(grads, hidden_ref[...]).astype(BF16)
+        owner = lax.rem(where_ref[0] + step - steps, width // part)
+        lanes = pl.ds(pl.multiple_of(owner * part, part), part)
+        rows = moved_ref[:, 0, :, lanes].reshape(flat, part)
+        grads = moved_ref[:, 1, :, lanes].reshape(flat, part)
+        term_ref[...] = contract_first(rows, gh_s[...]).astype(BF16)
+        value = contract_first(grads, hidden_s[...]).astype(BF16)
+        for k, out_ref in enumerate((own_ref, after_ref, far_ref, before_ref)):
+
+            @pl.when(step == steps + k)
+            def _(out_ref=out_ref):
+                out_ref[...] = value
 
 
 def return_kernel(hidden_ref, gh_ref, w_in_ref, w_out_ref, back_ref):
@@ -220,6 +244,14 @@
     back_ref[:, 0] = grad.reshape(sources, count, block)
     out = contract_last(hidden_ref[...], w_out_ref[...]).astype(BF16)
     back_ref[:, 1] = out.reshape(sources, count, block)
+
+
+def join_kernel(first_ref, own_ref, after_ref, far_ref, before_ref, out_ref):
+    half = first_ref.shape[1]
+    out_ref[:, :half] = first_ref[...]
+    total = own_ref[...].astype(F32) + after_ref[...].astype(F32)
+    total = total + far_ref[...].astype(F32) + before_ref[...].astype(F32)
+    out_ref[:, half:] = total.astype(BF16)
 
 
 def place_kernel(where_ref, *refs):
@@ -280,39 +312,60 @@
     return pltpu.with_memory_space_constraint(array, pltpu.HBM)
 
 
-def expert(moved, w_in, w_out):
+def expert(where, moved, w_in, w_out):
     sources, _, count, width = moved.shape
     flat = sources * count
     hid = w_in.shape[1]
-    block = 256
+    block = 512
     steps = hid // block
-    once = pl.Buffered(1)
-    weight = pl.BlockSpec((width, block), lambda j: (0, jnp.minimum(j, steps - 1)))
-    whole = pl.BlockSpec((flat, hid), lambda j: (0, 0))
+    part = width // 4
+    weight = pl.BlockSpec((width, block), lambda j, w: (0, jnp.minimum(j, steps - 1)))
+    piece = pl.BlockSpec((part, hid), lambda j, w: (0, 0))
+    hidden = pl.BlockSpec((flat, block), lambda j, w: (0, jnp.minimum(j, steps - 1)))
+    grid_spec = pltpu.PrefetchScalarGridSpec(
+        num_scalar_prefetch=1,
+        grid=(steps + 4,),
+        in_specs=[pl.BlockSpec(memory_space=pltpu.VMEM), weight, weight],
+        out_specs=[
+            pl.BlockSpec(
+                (part, hid), lambda j, w: (lax.rem(w[0] + jnp.maximum(j - steps, 0), 4), 0)
+            ),
+            piece,
+            piece,
+            piece,
+            piece,
+            hidden,
+            hidden,
+        ],
+        scratch_shapes=[pltpu.VMEM((flat, hid), BF16)] * 2,
+    )
     return pl.pallas_call(
         expert_kernel,
-        grid=(2 * steps,),
+        grid_spec=grid_spec,
         out_shape=(
-            pltpu.HBM((width, 2 * hid), BF16),
+            pltpu.HBM((width, hid), BF16),
+            *(pltpu.HBM((part, hid), BF16) for _ in range(4)),
             pltpu.HBM((flat, hid), BF16),
             pltpu.HBM((flat, hid), BF16),
         ),
-        in_specs=[
-            pl.BlockSpec(
-                (sources, 2, count, width), lambda j: (0, 0, 0, 0), pipeline_mode=once
-            ),
-            weight,
-            weight,
-        ],
-        out_specs=[
-            pl.BlockSpec((block, 2 * hid), lambda j: (jnp.maximum(j - steps, 0), 0)),
-            whole,
-            whole,
-        ],
-        compiler_params=params(20),
+        compiler_params=params(30),
         cost_estimate=cost(8 * flat * width * hid, 12 * MIB),
         name="expert",
-    )(moved, in_hbm(w_in), in_hbm(w_out))
+    )(where, moved, in_hbm(w_in), in_hbm(w_out))
+
+
+def join(first, pieces):
+    rows, half = first.shape
+    return pl.pallas_call(
+        join_kernel,
+        out_shape=pltpu.HBM((rows, 2 * half), BF16),
+        grid=(2,),
+        in_specs=[pl.BlockSpec((rows // 2, half), lambda i: (i, 0))] * 5,
+        out_specs=pl.BlockSpec((rows // 2, 2 * half), lambda i: (i, 0)),
+        compiler_params=params(8),
+        cost_estimate=cost(0, 3 * MIB),
+        name="join",
+    )(*(in_hbm(v) for v in (first, *pieces)))
 
 
 def return_rows(hidden, gh, w_in, w_out, sources):
@@ -402,10 +455,15 @@
     moved = exchange(sent, ep)
     along_y = gather_y(w_out[0])
     full_out = gather_by("x", along_y.reshape(-1, hid)).reshape(-1, hid)
-    partial, hidden, gh = expert(moved, full_in, full_out)
-    total = lax.psum_scatter(partial, dp, scatter_dimension=0, tiled=True).astype(F32)
+    term, own, *others, hidden, gh = expert(where_on("x"), moved, full_in, full_out)
+    over_x = lax.psum_scatter(term, "x", scatter_dimension=0, tiled=True)
     back = return_rows(hidden, gh, full_in, full_out, moved.shape[0])
     returned = exchange(back, ep)
+    got = {k: shifted(others[k - 1], "x", k) for k in (2, 1, 3)}
+    joined = join(over_x, [own, got[1], got[2], got[3]])
+    total = lax.psum_scatter(joined, "yh", scatter_dimension=0, tiled=True)
+    grad_in = total[:, :hid].astype(F32)[None]
+    grad_out = total[:, hid:].astype(F32)[None]
     mixed, grad_input = finish(
         expert_ids,
         gate_weights,
@@ -417,7 +475,7 @@
         grad_mixed,
         patches,
     )
-    return (mixed, grad_input, total[:, :hid][None], total[:, hid:][None])
+    return (mixed, grad_input, grad_in, grad_out)
 
 
 def solution(mesh):

time: 238 us -> 229 us (0.962)
  blocking collectives: 67.7 us -> 0 us
  waiting for transfers between devices: 81.2 us -> 117 us
  starting transfers between devices: 29.1 us -> 48.7 us
    all_to_all x1 -> x0, blocking collectives: 67.7 us -> none  [exchange(): return lax.all_to_all(rows, axes, split_axis=0, concat_axis=0, tiled=True)]
    ppermute x3 -> x6, waiting for transfers between devices: 25.4 us -> 54.8 us  [shifted(): return lax.ppermute(value, axis, [(i, (i + k) % n) for i in range(n)])]
    all_to_all x2 -> x3, waiting for transfers between devices: 0.01 us -> 12.2 us  [exchange(): return lax.all_to_all(rows, axes, split_axis=0, concat_axis=0, tiled=True)]
    ppermute x3 -> x6, starting transfers between devices: 9.33 us -> 19.8 us  [shifted(): return lax.ppermute(value, axis, [(i, (i + k) % n) for i in range(n)])]
    all_to_all x2 -> x3, starting transfers between devices: 19.7 us -> 28.9 us  [exchange(): return lax.all_to_all(rows, axes, split_axis=0, concat_axis=0, tiled=True)]
    reduce_scatter x1 -> x2, waiting for transfers between devices: 22.2 us -> 16.1 us  [the longest x1 16.1 us: local(): total = lax.psum_scatter(joined, 'yh', scatter_dimension=0, tiled=True)]
    unnamed x28 -> x38, local copies, waits for them, and re-layouts: 8.71 us -> 11.5 us
    pallas_call x1 -> x2, Pallas kernels: 10.3 us -> 12.4 us  [the longest x1 9.73 us: expert(): pl.pallas_call(expert_kernel, grid_spec=grid_spec, out_shape=(pltpu.HBM((...]
  transfers between devices with their start and end apart: 7 -> 12, of which waited for: 4 -> 7; matrix products, arithmetic and copies ran while one was open for 1% -> 1% of each run, Pallas kernels for 6% -> 8%
where the time goes in v5:
time: 229 us; the launch traced here: 228 us
  waiting for transfers between devices  117 us (51%)
  starting transfers between devices  48.7 us (21%)
  Pallas kernels  33.2 us (14%)
  between operations  13.9 us (6%)
  local copies, waits for them, and re-layouts  13.2 us (6%)
    ppermute x6, waiting for transfers between devices, shifted(): return lax.ppermute(value, axis, [(i, (i + k) % n) for i in range(n)])  54.8 us
    all_gather x1, waiting for transfers between devices, local(): full_in = lax.all_gather(w_in, dp, axis=1, tiled=True)[0]  33.4 us
    all_to_all x3, starting transfers between devices, exchange(): return lax.all_to_all(rows, axes, split_axis=0, concat_axis=0, tiled=True)  28.9 us
    ppermute x6, starting transfers between devices, shifted(): return lax.ppermute(value, axis, [(i, (i + k) % n) for i in range(n)])  19.8 us
    reduce_scatter x1, waiting for transfers between devices, local(): total = lax.psum_scatter(joined, 'yh', scatter_dimension=0, tiled=True)  16.1 us
    all_to_all x3, waiting for transfers between devices, exchange(): return lax.all_to_all(rows, axes, split_axis=0, concat_axis=0, tiled=True)  12.2 us
    unnamed x38, local copies, waits for them, and re-layouts  11.5 us
    pallas_call x1, Pallas kernels, expert(): pl.pallas_call(expert_kernel, grid_spec=grid_spec, out_shape=(pltpu.HBM((...  9.73 us
  transfers between devices with their start and end apart: 12, of which 7 were waited for; matrix products, arithmetic and copies ran while one was open for 1% of the time, Pallas kernels for 8%

profile of v5, /device:TPU:1, one launch (start us, length us, event | category | flops | bytes accessed | tf_op | source)
XLA Modules:
  0.0 228.0 jit_solution(3756762694897000492)
XLA Ops:
  7.2 1.8 broadcast_in_dim.20
  8.9 7.6 %all-to-all-start.1 = ((bf16[4,64,1024]{2,1,0:T(8,128)(2,1)}), bf16[4,64,1024]{2,1,0:T(8,128)(2,1)S(1)}, u32[]{:S(2)}, u32[]{:S(2)}) async-start(bf16[4,64,1024]{2,1,0:T(8,128)(2,1)} %broadcast_in_dim.20), calls=%async_computation.1 | async-start | bytes 1048576 | tf_op jit(solution)/shard_map/all_to_all | solution.py:407
  16.6 0.8 copy.16.ids_ref
  18.1 0.9 copy-done.4
  19.1 0.9 copy-done.6
  20.0 0.9 copy-done.8
  23.0 6.2 %send.1 = (bf16[32,2,16,1024]{3,2,1,0:T(8,128)(2,1)S(1)}, f32[128,1024]{1,0:T(8,128)S(1)}, f32[128,128]{1,0:T(8,128)S(1)}) custom-call(s32[128,2]{1,0:T(8,128)S(1)} %copy.16.ids_ref, f32[128,2]{1,0:T(8,128)S(1)} %copy.17.gates_ref, bf16[128,1024]{1,0:T(8,128)(2,1)S(1)} %copy-done.4, bf16[128,1024]{1,0:T(8,128)(2,1)S(1)} %copy-done.6, ...), custom_call_target="tpu_custom_call" | custom-call | flops 262144000 | bytes 2097152 | tf_op jit(solution)/shard_map/send/pallas_call | solution.py:278
  29.2 1.3 copy-done.1
  30.6 0.8 copy-done.2
  32.0 11.5 %all-to-all-start = ((bf16[32,2,16,1024]{3,2,1,0:T(8,128)(2,1)}), bf16[32,2,16,1024]{3,2,1,0:T(8,128)(2,1)S(1)}, u32[]{:S(2)}, u32[]{:S(2)}) async-start(bf16[32,2,16,1024]{3,2,1,0:T(8,128)(2,1)} %copy-done.1), calls=%async_computation | async-start | bytes 4194304 | tf_op jit(solution)/shard_map/all_to_all | solution.py:407
  44.3 4.4 %collective-permute-start.2 = (bf16[256,1024]{1,0:T(8,128)(2,1)S(1)}, bf16[256,1024]{1,0:T(8,128)(2,1)S(1)}, u32[]{:S(2)}, u32[]{:S(2)}) collective-permute-start(bf16[256,1024]{1,0:T(8,128)(2,1)S(1)} %bitcast.20), channel_id=1, source_target_pairs={{0,384},{128,0},{256,128},{384,256},{1,385},{129,1},{257,129},{385... | collective-permute-start | bytes 1572872 | tf_op jit(solution)/shard_map/ppermute | solution.py:412
  48.7 2.4 %collective-permute-start.1 = (bf16[256,1024]{1,0:T(8,128)(2,1)S(1)}, bf16[256,1024]{1,0:T(8,128)(2,1)}, u32[]{:S(2)}, u32[]{:S(2)}) collective-permute-start(bf16[256,1024]{1,0:T(8,128)(2,1)S(1)} %bitcast.21), channel_id=1, source_target_pairs={{0,256},{128,384},{256,0},{384,128},{1,257},{129,385},{257,1},{385... | collective-permute-start | bytes 1572872 | tf_op jit(solution)/shard_map/ppermute | solution.py:412
  51.2 2.5 %collective-permute-start = (bf16[256,1024]{1,0:T(8,128)(2,1)S(1)}, bf16[256,1024]{1,0:T(8,128)(2,1)}, u32[]{:S(2)}, u32[]{:S(2)}) collective-permute-start(bf16[256,1024]{1,0:T(8,128)(2,1)S(1)} %bitcast.22), channel_id=1, source_target_pairs={{0,128},{128,256},{256,384},{384,0},{1,129},{129,257},{257,385},{3... | collective-permute-start | bytes 1572872 | tf_op jit(solution)/shard_map/ppermute | solution.py:412
  53.7 12.7 %collective-permute-done.2.refs_3_ = bf16[256,1024]{1,0:T(8,128)(2,1)S(1)} collective-permute-done((bf16[256,1024]{1,0:T(8,128)(2,1)S(1)}, bf16[256,1024]{1,0:T(8,128)(2,1)S(1)}, u32[]{:S(2)}, u32[]{:S(2)}) %collective-permute-start.2) | collective-permute-done | bytes 524320 | tf_op jit(solution)/shard_map/ppermute | solution.py:412
  66.4 12.6 %collective-permute-done.refs_1_ = bf16[256,1024]{1,0:T(8,128)(2,1)} collective-permute-done((bf16[256,1024]{1,0:T(8,128)(2,1)S(1)}, bf16[256,1024]{1,0:T(8,128)(2,1)}, u32[]{:S(2)}, u32[]{:S(2)}) %collective-permute-start) | collective-permute-done | bytes 524320 | tf_op jit(solution)/shard_map/ppermute | solution.py:412
  79.0 1.3 place.1
  80.3 1.4 copy-done
  81.7 33.4 %all-gather.2.cloned.1.call-done = bf16[1,1024,1024]{2,1,0:T(8,128)(2,1)} async-done(((bf16[1,64,1024]{2,1,0:T(8,128)(2,1)}), bf16[1,1024,1024]{2,1,0:T(8,128)(2,1)}) %all-gather.2.cloned.1.call-update) | async-done | bytes 2097168 | tf_op jit(solution)/shard_map/all_gather | solution.py:444
  115.1 9.7 %expert.1 = (bf16[1024,1024]{1,0:T(8,128)(2,1)}, bf16[256,1024]{1,0:T(8,128)(2,1)}, bf16[256,1024]{1,0:T(8,128)(2,1)}, bf16[256,1024]{1,0:T(8,128)(2,1)}, bf16[2...) custom-call(s32[1]{0:T(128)} %bitcast.where_ref, ...), custom_call_target="tpu_custom_call" | custom-call | flops 4294967296 | bytes 12582912 | tf_op jit(solution)/shard_map/expert/pallas_call | solution.py:342
  124.9 6.5 %return_rows.1 = bf16[32,2,16,1024]{3,2,1,0:T(8,128)(2,1)} custom-call(bf16[512,1024]{1,0:T(8,128)(2,1)} %get-tuple-element.17.hidden_ref, bf16[512,1024]{1,0:T(8,128)(2,1)} %get-tuple-element.18.gh_ref, bf16[1024,1024]{1,0:T(8,128)(2,1)} %bitcast.29, bf16[1024,1024]{1,0:T(8,128)(2,1)} %bitcast.19), custom_call_target="tpu_custom_call" | custom-call | flops 2147483648 | bytes 8388608 | tf_op jit(solution)/shard_map/return_rows/pallas_call | solution.py:378
  131.4 9.7 %all-to-all-start.2 = ((bf16[32,2,16,1024]{3,2,1,0:T(8,128)(2,1)}), bf16[32,2,16,1024]{3,2,1,0:T(8,128)(2,1)S(1)}, u32[]{:S(2)}, u32[]{:S(2)}) async-start(bf16[32,2,16,1024]{3,2,1,0:T(8,128)(2,1)} %return_rows.1), calls=%async_computation.2 | async-start | bytes 4194304 | tf_op jit(solution)/shard_map/all_to_all | solution.py:407
  141.1 3.0 %collective-permute-start.3 = (bf16[256,1024]{1,0:T(8,128)(2,1)}, bf16[256,1024]{1,0:T(8,128)(2,1)}, u32[]{:S(2)}, u32[]{:S(2)}) collective-permute-start(bf16[256,1024]{1,0:T(8,128)(2,1)} %get-tuple-element.25), channel_id=1, source_target_pairs={{0,128},{128,256},{256,384},{384,0},{1,129},{129,257},{257,385},{3... | collective-permute-start | bytes 1572872 | tf_op jit(solution)/shard_map/ppermute | solution.py:412
  144.2 4.3 %collective-permute-start.4 = (bf16[256,1024]{1,0:T(8,128)(2,1)S(1)}, bf16[256,1024]{1,0:T(8,128)(2,1)}, u32[]{:S(2)}, u32[]{:S(2)}) collective-permute-start(bf16[256,1024]{1,0:T(8,128)(2,1)S(1)} %copy-done.17), channel_id=1, source_target_pairs={{0,256},{128,384},{256,0},{384,128},{1,257},{129,385},{257,1},{385... | collective-permute-start | bytes 1572872 | tf_op jit(solution)/shard_map/ppermute | solution.py:412
  148.5 3.1 %collective-permute-start.5 = (bf16[256,1024]{1,0:T(8,128)(2,1)S(1)}, bf16[256,1024]{1,0:T(8,128)(2,1)}, u32[]{:S(2)}, u32[]{:S(2)}) collective-permute-start(bf16[256,1024]{1,0:T(8,128)(2,1)S(1)} %copy-done.16), channel_id=1, source_target_pairs={{0,384},{128,0},{256,128},{384,256},{1,385},{129,1},{257,129},{385... | collective-permute-start | bytes 1572872 | tf_op jit(solution)/shard_map/ppermute | solution.py:412
  151.6 17.8 %collective-permute-done.3.after_ref = bf16[256,1024]{1,0:T(8,128)(2,1)} collective-permute-done((bf16[256,1024]{1,0:T(8,128)(2,1)}, bf16[256,1024]{1,0:T(8,128)(2,1)}, u32[]{:S(2)}, u32[]{:S(2)}) %collective-permute-start.3) | collective-permute-done | bytes 524320 | tf_op jit(solution)/shard_map/ppermute | solution.py:412
  169.4 11.6 %collective-permute-done.4.far_ref = bf16[256,1024]{1,0:T(8,128)(2,1)} collective-permute-done((bf16[256,1024]{1,0:T(8,128)(2,1)S(1)}, bf16[256,1024]{1,0:T(8,128)(2,1)}, u32[]{:S(2)}, u32[]{:S(2)}) %collective-permute-start.4) | collective-permute-done | bytes 524320 | tf_op jit(solution)/shard_map/ppermute | solution.py:412
  181.1 2.7 %join.1 = bf16[256,2048]{1,0:T(8,128)(2,1)} custom-call(bf16[256,1024]{1,0:T(8,128)(2,1)} %reduce-scatter.3.cloned.1.call-done.first_ref, bf16[256,1024]{1,0:T(8,128)(2,1)} %get-tuple-element.24.own_ref, bf16[256,1024]{1,0:T(8,128)(2,1)} %collective-permute-done.3.after_ref, bf16[256,1024]{1,0:T(8,128)(2,1)} %collective-permute-done.4.far_ref, ...), custom_call_target="tpu_custom_call" | custom-call | bytes 3145728 | tf_op jit(solution)/shard_map/join/pallas_call | solution.py:359
  183.8 12.2 %all-to-all-done.2.back_ref = bf16[32,2,16,1024]{3,2,1,0:T(8,128)(2,1)S(1)} async-done(((bf16[32,2,16,1024]{3,2,1,0:T(8,128)(2,1)}), bf16[32,2,16,1024]{3,2,1,0:T(8,128)(2,1)S(1)}, u32[]{:S(2)}, u32[]{:S(2)}) %all-to-all-start.2) | async-done | bytes 2097184 | tf_op jit(solution)/shard_map/all_to_all | solution.py:407
  196.1 0.8 copy-done.11
  196.9 6.7 %finish.1 = (bf16[128,1024]{1,0:T(8,128)(2,1)}, f32[128,1024]{1,0:T(8,128)}) custom-call(s32[128,2]{1,0:T(8,128)S(1)} %copy.16.ids_ref, f32[128,2]{1,0:T(8,128)S(1)} %copy.17.gates_ref, bf16[32,2,16,1024]{3,2,1,0:T(8,128)(2,1)S(1)} %all-to-all-done.2.back_ref, f32[128,1024]{1,0:T(8,128)S(1)} %copy-done.3, f32[128,128]{1,0:T(8,128)S(1)} %copy-done.11, ...), custom_call_target="tpu_custom_call" | custom-call | flops 262144000 | bytes 2097152 | tf_op jit(solution)/shard_map/finish/pallas_call | solution.py:299
  203.6 16.1 %reduce-scatter.5.cloned.1.call-done = bf16[64,2048]{1,0:T(8,128)(2,1)} async-done(((bf16[256,2048]{1,0:T(8,128)(2,1)}), bf16[64,2048]{1,0:T(8,128)(2,1)}) %reduce-scatter.5.cloned.1.call-update) | async-done | bytes 262160 | tf_op jit(solution)/shard_map/reduce_scatter | solution.py:464
  219.7 1.8 fusion
  (41 shorter events, 4.4 us)
Async XLA Ops:
  8.9 23.1 %all-to-all-start.1 = ((bf16[4,64,1024]{2,1,0:T(8,128)(2,1)}), bf16[4,64,1024]{2,1,0:T(8,128)(2,1)S(1)}, u32[]{:S(2)}, u32[]{:S(2)}) async-start(bf16[4,64,1024]{2,1,0:T(8,128)(2,1)} %broadcast_in_dim.20), calls=%async_computation.1 | async-start | bytes 1048576 | tf_op jit(solution)/shard_map/all_to_all | solution.py:407
  18.1 0.9 copy-start.4
  19.1 0.9 copy-start.6
  20.0 0.9 copy-start.8
  21.0 0.7 copy-start.12
  21.7 0.7 copy-start.14
  22.3 0.7 copy-start.15
  29.2 1.4 copy-start.1
  30.6 0.8 copy-start.2
  31.4 0.6 copy-start.10
  32.0 83.1 %all-to-all-start = ((bf16[32,2,16,1024]{3,2,1,0:T(8,128)(2,1)}), bf16[32,2,16,1024]{3,2,1,0:T(8,128)(2,1)S(1)}, u32[]{:S(2)}, u32[]{:S(2)}) async-start(bf16[32,2,16,1024]{3,2,1,0:T(8,128)(2,1)} %copy-done.1), calls=%async_computation | async-start | bytes 4194304 | tf_op jit(solution)/shard_map/all_to_all | solution.py:407
  43.5 71.6 %all-gather.2.cloned.1.call-start = ((), (), s32[]{:S(2)}) async-start(), calls=%async_computation.5 | async-start | bytes 2228224 | tf_op jit(solution)/shard_map/all_gather | solution.py:444
  44.3 136.8 %reduce-scatter.3.cloned.1.call-start = ((), (), s32[]{:S(2)}) async-start(), calls=%async_computation.6 | async-start | bytes 2621440 | tf_op jit(solution)/shard_map/reduce_scatter | solution.py:459
  44.3 22.0 %collective-permute-start.2 = (bf16[256,1024]{1,0:T(8,128)(2,1)S(1)}, bf16[256,1024]{1,0:T(8,128)(2,1)S(1)}, u32[]{:S(2)}, u32[]{:S(2)}) collective-permute-start(bf16[256,1024]{1,0:T(8,128)(2,1)S(1)} %bitcast.20), channel_id=1, source_target_pairs={{0,384},{128,0},{256,128},{384,256},{1,385},{129,1},{257,129},{385... | collective-permute-start | bytes 1572872 | tf_op jit(solution)/shard_map/ppermute | solution.py:412
  48.7 17.6 %collective-permute-start.1 = (bf16[256,1024]{1,0:T(8,128)(2,1)S(1)}, bf16[256,1024]{1,0:T(8,128)(2,1)}, u32[]{:S(2)}, u32[]{:S(2)}) collective-permute-start(bf16[256,1024]{1,0:T(8,128)(2,1)S(1)} %bitcast.21), channel_id=1, source_target_pairs={{0,256},{128,384},{256,0},{384,128},{1,257},{129,385},{257,1},{385... | collective-permute-start | bytes 1572872 | tf_op jit(solution)/shard_map/ppermute | solution.py:412
  51.2 27.8 %collective-permute-start = (bf16[256,1024]{1,0:T(8,128)(2,1)S(1)}, bf16[256,1024]{1,0:T(8,128)(2,1)}, u32[]{:S(2)}, u32[]{:S(2)}) collective-permute-start(bf16[256,1024]{1,0:T(8,128)(2,1)S(1)} %bitcast.22), channel_id=1, source_target_pairs={{0,128},{128,256},{256,384},{384,0},{1,129},{129,257},{257,385},{3... | collective-permute-start | bytes 1572872 | tf_op jit(solution)/shard_map/ppermute | solution.py:412
  80.3 1.4 copy-start
  131.4 12.8 %copy-start.17 = (bf16[256,1024]{1,0:T(8,128)(2,1)S(1)}, bf16[256,1024]{1,0:T(8,128)(2,1)}, u32[]{:S(2)}) copy-start(bf16[256,1024]{1,0:T(8,128)(2,1)} %get-tuple-element.26) | copy-start | bytes 1572868
  131.4 17.1 %copy-start.16 = (bf16[256,1024]{1,0:T(8,128)(2,1)S(1)}, bf16[256,1024]{1,0:T(8,128)(2,1)}, u32[]{:S(2)}) copy-start(bf16[256,1024]{1,0:T(8,128)(2,1)} %get-tuple-element.27) | copy-start | bytes 1572868
  131.4 64.6 %all-to-all-start.2 = ((bf16[32,2,16,1024]{3,2,1,0:T(8,128)(2,1)}), bf16[32,2,16,1024]{3,2,1,0:T(8,128)(2,1)S(1)}, u32[]{:S(2)}, u32[]{:S(2)}) async-start(bf16[32,2,16,1024]{3,2,1,0:T(8,128)(2,1)} %return_rows.1), calls=%async_computation.2 | async-start | bytes 4194304 | tf_op jit(solution)/shard_map/all_to_all | solution.py:407
  141.1 78.6 %reduce-scatter.5.cloned.1.call-start = ((), (), s32[]{:S(2)}) async-start(), calls=%async_computation.7 | async-start | bytes 1310720 | tf_op jit(solution)/shard_map/reduce_scatter | solution.py:464
  141.1 28.3 %collective-permute-start.3 = (bf16[256,1024]{1,0:T(8,128)(2,1)}, bf16[256,1024]{1,0:T(8,128)(2,1)}, u32[]{:S(2)}, u32[]{:S(2)}) collective-permute-start(bf16[256,1024]{1,0:T(8,128)(2,1)} %get-tuple-element.25), channel_id=1, source_target_pairs={{0,128},{128,256},{256,384},{384,0},{1,129},{129,257},{257,385},{3... | collective-permute-start | bytes 1572872 | tf_op jit(solution)/shard_map/ppermute | solution.py:412
  144.2 36.9 %collective-permute-start.4 = (bf16[256,1024]{1,0:T(8,128)(2,1)S(1)}, bf16[256,1024]{1,0:T(8,128)(2,1)}, u32[]{:S(2)}, u32[]{:S(2)}) collective-permute-start(bf16[256,1024]{1,0:T(8,128)(2,1)S(1)} %copy-done.17), channel_id=1, source_target_pairs={{0,256},{128,384},{256,0},{384,128},{1,257},{129,385},{257,1},{385... | collective-permute-start | bytes 1572872 | tf_op jit(solution)/shard_map/ppermute | solution.py:412
  148.5 32.5 %collective-permute-start.5 = (bf16[256,1024]{1,0:T(8,128)(2,1)S(1)}, bf16[256,1024]{1,0:T(8,128)(2,1)}, u32[]{:S(2)}, u32[]{:S(2)}) collective-permute-start(bf16[256,1024]{1,0:T(8,128)(2,1)S(1)} %copy-done.16), channel_id=1, source_target_pairs={{0,384},{128,0},{256,128},{384,256},{1,385},{129,1},{257,129},{385... | collective-permute-start | bytes 1572872 | tf_op jit(solution)/shard_map/ppermute | solution.py:412
  181.1 15.0 %copy-start.3 = (f32[128,1024]{1,0:T(8,128)S(1)}, f32[128,1024]{1,0:T(8,128)}, u32[]{:S(2)}) copy-start(f32[128,1024]{1,0:T(8,128)} %copy-done.2) | copy-start | bytes 1572868
  181.1 15.0 %copy-start.5 = (bf16[128,1024]{1,0:T(8,128)(2,1)S(1)}, bf16[128,1024]{1,0:T(8,128)(2,1)}, u32[]{:S(2)}) copy-start(bf16[128,1024]{1,0:T(8,128)(2,1)} %cot_ref.3) | copy-start | bytes 786436
  181.1 14.9 %copy-start.7 = (bf16[128,1024]{1,0:T(8,128)(2,1)S(1)}, bf16[128,1024]{1,0:T(8,128)(2,1)}, u32[]{:S(2)}) copy-start(bf16[128,1024]{1,0:T(8,128)(2,1)} %x_ref.3) | copy-start | bytes 786436
  181.1 14.9 %copy-start.9 = (f32[49,1024]{1,0:T(8,128)S(1)}, f32[49,1024]{1,0:T(8,128)}, u32[]{:S(2)}) copy-start(f32[49,1024]{1,0:T(8,128)} %taps_ref.3) | copy-start | bytes 602116
  181.1 14.9 %copy-start.13 = (f32[1024]{0:T(1024)S(1)}, f32[1024]{0:T(1024)}, u32[]{:S(2)}) copy-start(f32[1024]{0:T(1024)} %param.15) | copy-start | bytes 12292
  196.0 0.8 copy-start.11
Sparse Core Ops, SparseCore 0:
  47.4 67.7 all-gather.1
  125.0 46.3 reduce-scatter.2
  184.0 35.6 reduce-scatter.4

commit v6 on v4

--- a/solution.py
+++ b/solution.py
@@ -183,13 +183,22 @@
 SQRT_2_OVER_PI = 0.7978845608028654
 
 
-def expert_kernel(moved_ref, w_in_ref, w_out_ref, terms_ref, hidden_ref, gh_ref):
+def expert_kernel(
+    moved_ref,
+    w_in_ref,
+    w_out_ref,
+    terms_ref,
+    hidden_ref,
+    gh_ref,
+    hidden_s,
+    gh_s,
+):
     step = pl.program_id(0)
-    steps = pl.num_programs(0) // 2
     sources, _, count, width = moved_ref.shape
     flat = sources * count
     block = w_in_ref.shape[1]
-    hid = hidden_ref.shape[1]
+    part = terms_ref.shape[0]
+    steps = hidden_s.shape[1] // block
 
     @pl.when(step < steps)
     def _():
@@ -202,16 +211,21 @@
             SQRT_2_OVER_PI * (1.0 + (3 * 0.044715) * square)
         )
         lanes = pl.ds(pl.multiple_of(step * block, block), block)
-        hidden_ref[:, lanes] = (pre * cdf).astype(BF16)
-        gh_ref[:, lanes] = (raw * slope).astype(BF16)
+        hidden = (pre * cdf).astype(BF16)
+        gh = (raw * slope).astype(BF16)
+        hidden_s[:, lanes] = hidden
+        gh_s[:, lanes] = gh
+        hidden_ref[...] = hidden
+        gh_ref[...] = gh
 
     @pl.when(step >= steps)
     def _():
-        lanes = pl.ds(pl.multiple_of((step - steps) * block, block), block)
-        rows = moved_ref[:, 0, :, lanes].reshape(flat, block)
-        grads = moved_ref[:, 1, :, lanes].reshape(flat, block)
-        terms_ref[:, :hid] = contract_first(rows, gh_ref[...]).astype(BF16)
-        terms_ref[:, hid:] = contract_first(grads, hidden_ref[...]).astype(BF16)
+        lanes = pl.ds(pl.multiple_of((step - steps) * part, part), part)
+        rows = moved_ref[:, 0, :, lanes].reshape(flat, part)
+        grads = moved_ref[:, 1, :, lanes].reshape(flat, part)
+        hid = hidden_s.shape[1]
+        terms_ref[:, :hid] = contract_first(rows, gh_s[...]).astype(BF16)
+        terms_ref[:, hid:] = contract_first(grads, hidden_s[...]).astype(BF16)
 
 
 def return_kernel(hidden_ref, gh_ref, w_in_ref, w_out_ref, back_ref):
@@ -222,6 +236,12 @@
     back_ref[:, 1] = out.reshape(sources, count, block)
 
 
+def widen_kernel(sum_ref, in_ref, out_ref):
+    hid = in_ref.shape[1]
+    in_ref[...] = sum_ref[:, :hid].astype(F32)
+    out_ref[...] = sum_ref[:, hid:].astype(F32)
+
+
 def place_kernel(where_ref, *refs):
     pieces, out_ref = refs[:-1], refs[-1]
     for k, piece in enumerate(pieces):
@@ -241,25 +261,33 @@
     return jax.ShapeDtypeStruct(dims, dtype)
 
 
+def in_hbm(array):
+    return pltpu.with_memory_space_constraint(array, pltpu.HBM)
+
+
+def all_of(dims):
+    return pl.BlockSpec(dims, lambda i: (0,) * len(dims))
+
+
 def send(ids, gates, cot, x, taps, bias, gain, shift):
     width = x.shape[1]
+    rows = [bias.reshape(1, width), gain.reshape(1, width), shift.reshape(1, width)]
+    outs = [((EXPERTS, 2, CAP, width), BF16), ((TOK, width), F32), ((TOK, LANES), F32)]
+    wide = [in_hbm(v) for v in (cot, x, taps)]
     return pl.pallas_call(
         send_kernel,
-        out_shape=(
-            shape((EXPERTS, 2, CAP, width), BF16),
-            shape((TOK, width), F32),
-            shape((TOK, LANES), F32),
-        ),
-        in_specs=[VMEM] * 8,
-        out_specs=[VMEM] * 3,
+        grid=(1,),
+        out_shape=tuple(pltpu.HBM(*out) for out in outs),
+        in_specs=[VMEM] * 2 + [all_of(v.shape) for v in wide] + [VMEM] * 3,
+        out_specs=[all_of(dims) for dims, _ in outs],
         scratch_shapes=[
             pltpu.VMEM((IMG_H + KSIZE - 1, IMG_W + 16, width), F32),
             pltpu.VMEM((TOK, width), F32),
         ],
-        compiler_params=params(),
+        compiler_params=params(20),
         cost_estimate=cost(100 * TOK * width * 20, 4 * SLOTS * width),
         name="send",
-    )(ids, gates, cot, x, taps, bias.reshape(1, width), gain.reshape(1, width), shift.reshape(1, width))
+    )(ids, gates, *wide, *rows)
 
 
 def finish(ids, gates, back, xhat, rstd, gain, taps, cot, x):
@@ -276,43 +304,48 @@
     )(ids, gates, back, xhat, rstd, gain.reshape(1, width), taps, cot, x)
 
 
-def in_hbm(array):
-    return pltpu.with_memory_space_constraint(array, pltpu.HBM)
-
-
 def expert(moved, w_in, w_out):
     sources, _, count, width = moved.shape
     flat = sources * count
     hid = w_in.shape[1]
-    block = 256
+    block = 512
+    part = 256
     steps = hid // block
-    once = pl.Buffered(1)
     weight = pl.BlockSpec((width, block), lambda j: (0, jnp.minimum(j, steps - 1)))
-    whole = pl.BlockSpec((flat, hid), lambda j: (0, 0))
+    hidden = pl.BlockSpec((flat, block), lambda j: (0, jnp.minimum(j, steps - 1)))
     return pl.pallas_call(
         expert_kernel,
-        grid=(2 * steps,),
+        grid=(steps + width // part,),
         out_shape=(
             pltpu.HBM((width, 2 * hid), BF16),
             pltpu.HBM((flat, hid), BF16),
             pltpu.HBM((flat, hid), BF16),
         ),
-        in_specs=[
-            pl.BlockSpec(
-                (sources, 2, count, width), lambda j: (0, 0, 0, 0), pipeline_mode=once
-            ),
-            weight,
-            weight,
+        in_specs=[VMEM, weight, weight],
+        out_specs=[
+            pl.BlockSpec((part, 2 * hid), lambda j: (jnp.maximum(j - steps, 0), 0)),
+            hidden,
+            hidden,
         ],
-        out_specs=[
-            pl.BlockSpec((block, 2 * hid), lambda j: (jnp.maximum(j - steps, 0), 0)),
-            whole,
-            whole,
-        ],
-        compiler_params=params(20),
+        scratch_shapes=[pltpu.VMEM((flat, hid), BF16)] * 2,
+        compiler_params=params(30),
         cost_estimate=cost(8 * flat * width * hid, 12 * MIB),
         name="expert",
     )(moved, in_hbm(w_in), in_hbm(w_out))
+
+
+def widen(total):
+    rows, columns = total.shape
+    return pl.pallas_call(
+        widen_kernel,
+        out_shape=[shape((rows, columns // 2), F32)] * 2,
+        grid=(1,),
+        in_specs=[pl.BlockSpec((rows, columns), lambda i: (0, 0))],
+        out_specs=[pl.BlockSpec((rows, columns // 2), lambda i: (0, 0))] * 2,
+        compiler_params=params(4),
+        cost_estimate=cost(0, MIB),
+        name="widen",
+    )(in_hbm(total))
 
 
 def return_rows(hidden, gh, w_in, w_out, sources):
@@ -403,9 +436,11 @@
     along_y = gather_y(w_out[0])
     full_out = gather_by("x", along_y.reshape(-1, hid)).reshape(-1, hid)
     partial, hidden, gh = expert(moved, full_in, full_out)
-    total = lax.psum_scatter(partial, dp, scatter_dimension=0, tiled=True).astype(F32)
+    over_x = lax.psum_scatter(partial, "x", scatter_dimension=0, tiled=True)
     back = return_rows(hidden, gh, full_in, full_out, moved.shape[0])
     returned = exchange(back, ep)
+    total = lax.psum_scatter(over_x, "yh", scatter_dimension=0, tiled=True)
+    grad_in, grad_out = widen(total)
     mixed, grad_input = finish(
         expert_ids,
         gate_weights,
@@ -417,7 +452,7 @@
         grad_mixed,
         patches,
     )
-    return (mixed, grad_input, total[:, :hid][None], total[:, hid:][None])
+    return (mixed, grad_input, grad_in[None], grad_out[None])
 
 
 def solution(mesh):

time: 238 us -> 221 us (0.929)
  blocking collectives: 67.7 us -> 0 us
  waiting for transfers between devices: 81.2 us -> 126 us
  starting transfers between devices: 29.1 us -> 39.4 us
  local copies, waits for them, and re-layouts: 11.3 us -> 7.64 us
    all_to_all x1 -> x0, blocking collectives: 67.7 us -> none  [exchange(): return lax.all_to_all(rows, axes, split_axis=0, concat_axis=0, tiled=True)]
    reduce_scatter x1 -> x2, waiting for transfers between devices: 22.2 us -> 46.4 us  [the longest x1 35.2 us: local(): over_x = lax.psum_scatter(partial, 'x', scatter_dimension=0, tiled=True)]
    all_to_all x2 -> x3, waiting for transfers between devices: 0.01 us -> 21.7 us  [exchange(): return lax.all_to_all(rows, axes, split_axis=0, concat_axis=0, tiled=True)]
    all_to_all x2 -> x3, starting transfers between devices: 19.7 us -> 30 us  [exchange(): return lax.all_to_all(rows, axes, split_axis=0, concat_axis=0, tiled=True)]
    unnamed x28 -> x22, local copies, waits for them, and re-layouts: 8.71 us -> 5.87 us
    pallas_call x2 -> x3, Pallas kernels: 17.8 us -> 19.4 us  [the longest x1 9.07 us: expert(): pl.pallas_call(expert_kernel, grid=(steps + width // part,), out_shape=(p...]
  transfers between devices with their start and end apart: 7 -> 9, of which waited for: 4 -> 8; matrix products, arithmetic and copies ran while one was open for 1% -> 1% of each run, Pallas kernels for 6% -> 7%
where the time goes in v6:
time: 221 us; the launch traced here: 220 us
  waiting for transfers between devices  126 us (57%)
  starting transfers between devices  39.4 us (18%)
  Pallas kernels  34 us (15%)
  between operations  13.9 us (6%)
  local copies, waits for them, and re-layouts  7.64 us (3%)
    reduce_scatter x1, waiting for transfers between devices, local(): over_x = lax.psum_scatter(partial, 'x', scatter_dimension=0, tiled=True)  35.2 us
    all_gather x1, waiting for transfers between devices, local(): full_in = lax.all_gather(w_in, dp, axis=1, tiled=True)[0]  31.1 us
    all_to_all x3, starting transfers between devices, exchange(): return lax.all_to_all(rows, axes, split_axis=0, concat_axis=0, tiled=True)  30 us
    ppermute x3, waiting for transfers between devices, shifted(): return lax.ppermute(value, axis, [(i, (i + k) % n) for i in range(n)])  25.6 us
    all_to_all x3, waiting for transfers between devices, exchange(): return lax.all_to_all(rows, axes, split_axis=0, concat_axis=0, tiled=True)  21.7 us
    reduce_scatter x1, waiting for transfers between devices, local(): total = lax.psum_scatter(over_x, 'yh', scatter_dimension=0, tiled=True)  11.2 us
    ppermute x3, starting transfers between devices, shifted(): return lax.ppermute(value, axis, [(i, (i + k) % n) for i in range(n)])  9.33 us
    pallas_call x1, Pallas kernels, expert(): pl.pallas_call(expert_kernel, grid=(steps + width // part,), out_shape=(p...  9.07 us
  transfers between devices with their start and end apart: 9, of which 8 were waited for; matrix products, arithmetic and copies ran while one was open for 1% of the time, Pallas kernels for 7%

profile of v6, /device:TPU:1, one launch (start us, length us, event | category | flops | bytes accessed | tf_op | source)
XLA Modules:
  0.0 220.4 jit_solution(10591666134833489793)
XLA Ops:
  7.2 1.8 broadcast_in_dim.14
  8.9 7.6 %all-to-all-start.1 = ((bf16[4,64,1024]{2,1,0:T(8,128)(2,1)}), bf16[4,64,1024]{2,1,0:T(8,128)(2,1)S(1)}, u32[]{:S(2)}, u32[]{:S(2)}) async-start(bf16[4,64,1024]{2,1,0:T(8,128)(2,1)} %broadcast_in_dim.14), calls=%async_computation.1 | async-start | bytes 1048576 | tf_op jit(solution)/shard_map/all_to_all | solution.py:387
  16.6 0.8 copy.16.ids_ref
  17.4 0.8 copy.17.gates_ref
  18.1 0.7 copy-done.6
  18.8 0.7 copy-done.8
  19.5 0.7 copy-done.9
  20.2 8.6 %send.1 = (bf16[32,2,16,1024]{3,2,1,0:T(8,128)(2,1)}, f32[128,1024]{1,0:T(8,128)}, f32[128,128]{1,0:T(8,128)}) custom-call(s32[128,2]{1,0:T(8,128)S(1)} %copy.16.ids_ref, f32[128,2]{1,0:T(8,128)S(1)} %copy.17.gates_ref, bf16[128,1024]{1,0:T(8,128)(2,1)} %cot_ref.3, bf16[128,1024]{1,0:T(8,128)(2,1)} %x_ref.3, f32[49,1024]{1,0:T(8,128)} %taps_ref.3, ...), custom_call_target="tpu_custom_call" | custom-call | flops 262144000 | bytes 2097152 | tf_op jit(solution)/shard_map/send/pallas_call | solution.py:277
  28.8 2.0 all-to-all-done.1
  30.8 12.7 %all-to-all-start = ((bf16[32,2,16,1024]{3,2,1,0:T(8,128)(2,1)}), bf16[32,2,16,1024]{3,2,1,0:T(8,128)(2,1)S(1)}, u32[]{:S(2)}, u32[]{:S(2)}) async-start(bf16[32,2,16,1024]{3,2,1,0:T(8,128)(2,1)} %get-tuple-element.14), calls=%async_computation | async-start | bytes 4194304 | tf_op jit(solution)/shard_map/all_to_all | solution.py:387
  43.5 0.0 all-gather.2.cloned.1.call-start
  43.5 0.7 all-gather.2.cloned.1.call-update
  44.2 0.0 reduce-scatter.3.cloned.1.call-start
  44.2 4.4 %collective-permute-start.2 = (bf16[256,1024]{1,0:T(8,128)(2,1)S(1)}, bf16[256,1024]{1,0:T(8,128)(2,1)S(1)}, u32[]{:S(2)}, u32[]{:S(2)}) collective-permute-start(bf16[256,1024]{1,0:T(8,128)(2,1)S(1)} %bitcast.12), channel_id=1, source_target_pairs={{0,384},{128,0},{256,128},{384,256},{1,385},{129,1},{257,129},{385... | collective-permute-start | bytes 1572872 | tf_op jit(solution)/shard_map/ppermute | solution.py:392
  48.6 2.4 %collective-permute-start.1 = (bf16[256,1024]{1,0:T(8,128)(2,1)S(1)}, bf16[256,1024]{1,0:T(8,128)(2,1)}, u32[]{:S(2)}, u32[]{:S(2)}) collective-permute-start(bf16[256,1024]{1,0:T(8,128)(2,1)S(1)} %bitcast.13), channel_id=1, source_target_pairs={{0,256},{128,384},{256,0},{384,128},{1,257},{129,385},{257,1},{385... | collective-permute-start | bytes 1572872 | tf_op jit(solution)/shard_map/ppermute | solution.py:392
  51.1 2.5 %collective-permute-start = (bf16[256,1024]{1,0:T(8,128)(2,1)S(1)}, bf16[256,1024]{1,0:T(8,128)(2,1)}, u32[]{:S(2)}, u32[]{:S(2)}) collective-permute-start(bf16[256,1024]{1,0:T(8,128)(2,1)S(1)} %bitcast.14), channel_id=1, source_target_pairs={{0,128},{128,256},{256,384},{384,0},{1,129},{129,257},{257,385},{3... | collective-permute-start | bytes 1572872 | tf_op jit(solution)/shard_map/ppermute | solution.py:392
  53.6 10.2 %collective-permute-done.2.refs_3_ = bf16[256,1024]{1,0:T(8,128)(2,1)S(1)} collective-permute-done((bf16[256,1024]{1,0:T(8,128)(2,1)S(1)}, bf16[256,1024]{1,0:T(8,128)(2,1)S(1)}, u32[]{:S(2)}, u32[]{:S(2)}) %collective-permute-start.2) | collective-permute-done | bytes 524320 | tf_op jit(solution)/shard_map/ppermute | solution.py:392
  63.8 1.3 collective-permute-done.1.refs_2_
  65.1 14.1 %collective-permute-done.refs_1_ = bf16[256,1024]{1,0:T(8,128)(2,1)} collective-permute-done((bf16[256,1024]{1,0:T(8,128)(2,1)S(1)}, bf16[256,1024]{1,0:T(8,128)(2,1)}, u32[]{:S(2)}, u32[]{:S(2)}) %collective-permute-start) | collective-permute-done | bytes 524320 | tf_op jit(solution)/shard_map/ppermute | solution.py:392
  79.2 1.3 place.1
  80.6 1.4 copy-done
  82.0 31.1 %all-gather.2.cloned.1.call-done = bf16[1,1024,1024]{2,1,0:T(8,128)(2,1)} async-done(((bf16[1,64,1024]{2,1,0:T(8,128)(2,1)}), bf16[1,1024,1024]{2,1,0:T(8,128)(2,1)}) %all-gather.2.cloned.1.call-update) | async-done | bytes 2097168 | tf_op jit(solution)/shard_map/all_gather | solution.py:424
  113.1 9.1 %expert.1 = (bf16[1024,2048]{1,0:T(8,128)(2,1)}, bf16[512,1024]{1,0:T(8,128)(2,1)}, bf16[512,1024]{1,0:T(8,128)(2,1)}) custom-call(bf16[32,2,16,1024]{3,2,1,0:T(8,128)(2,1)S(1)} %all-to-all-done.moved_ref, bf16[1024,1024]{1,0:T(8,128)(2,1)} %bitcast.20, bf16[1024,1024]{1,0:T(8,128)(2,1)} %bitcast.10), custom_call_target="tpu_custom_call" | custom-call | flops 4294967296 | bytes 12582912 | tf_op jit(solution)/shard_map/expert/pallas_call | solution.py:316
  122.2 6.5 %return_rows.1 = bf16[32,2,16,1024]{3,2,1,0:T(8,128)(2,1)} custom-call(bf16[512,1024]{1,0:T(8,128)(2,1)} %get-tuple-element.15.hidden_ref, bf16[512,1024]{1,0:T(8,128)(2,1)} %get-tuple-element.16.gh_ref, bf16[1024,1024]{1,0:T(8,128)(2,1)} %bitcast.21, bf16[1024,1024]{1,0:T(8,128)(2,1)} %bitcast.11), custom_call_target="tpu_custom_call" | custom-call | flops 2147483648 | bytes 8388608 | tf_op jit(solution)/shard_map/return_rows/pallas_call | solution.py:358
  128.7 9.7 %all-to-all-start.2 = ((bf16[32,2,16,1024]{3,2,1,0:T(8,128)(2,1)}), bf16[32,2,16,1024]{3,2,1,0:T(8,128)(2,1)S(1)}, u32[]{:S(2)}, u32[]{:S(2)}) async-start(bf16[32,2,16,1024]{3,2,1,0:T(8,128)(2,1)} %return_rows.1), calls=%async_computation.2 | async-start | bytes 4194304 | tf_op jit(solution)/shard_map/all_to_all | solution.py:387
  138.4 0.0 reduce-scatter.5.cloned.1.call-start
  138.4 35.2 %reduce-scatter.3.cloned.1.call-done = bf16[256,2048]{1,0:T(8,128)(2,1)} async-done(((bf16[1024,2048]{1,0:T(8,128)(2,1)}), bf16[256,2048]{1,0:T(8,128)(2,1)}) %reduce-scatter.3.cloned.1.call-update) | async-done | bytes 1048592 | tf_op jit(solution)/shard_map/reduce_scatter | solution.py:439
  173.6 19.7 %all-to-all-done.2.back_ref = bf16[32,2,16,1024]{3,2,1,0:T(8,128)(2,1)S(1)} async-done(((bf16[32,2,16,1024]{3,2,1,0:T(8,128)(2,1)}), bf16[32,2,16,1024]{3,2,1,0:T(8,128)(2,1)S(1)}, u32[]{:S(2)}, u32[]{:S(2)}) %all-to-all-start.2) | async-done | bytes 2097184 | tf_op jit(solution)/shard_map/all_to_all | solution.py:387
  193.4 0.8 copy-done.5
  194.2 6.8 %finish.1 = (bf16[128,1024]{1,0:T(8,128)(2,1)}, f32[128,1024]{1,0:T(8,128)}) custom-call(s32[128,2]{1,0:T(8,128)S(1)} %copy.16.ids_ref, f32[128,2]{1,0:T(8,128)S(1)} %copy.17.gates_ref, bf16[32,2,16,1024]{3,2,1,0:T(8,128)(2,1)S(1)} %all-to-all-done.2.back_ref, f32[128,1024]{1,0:T(8,128)S(1)} %copy-done.1, f32[128,128]{1,0:T(8,128)S(1)} %copy-done.5, ...), custom_call_target="tpu_custom_call" | custom-call | flops 262144000 | bytes 2097152 | tf_op jit(solution)/shard_map/finish/pallas_call | solution.py:295
  200.9 11.2 %reduce-scatter.5.cloned.1.call-done.sum_ref = bf16[64,2048]{1,0:T(8,128)(2,1)} async-done(((bf16[256,2048]{1,0:T(8,128)(2,1)}), bf16[64,2048]{1,0:T(8,128)(2,1)}) %reduce-scatter.5.cloned.1.call-update) | async-done | bytes 262160 | tf_op jit(solution)/shard_map/reduce_scatter | solution.py:442
  212.2 1.8 widen.1
  (18 shorter events, 0.1 us)
Async XLA Ops:
  8.9 21.8 %all-to-all-start.1 = ((bf16[4,64,1024]{2,1,0:T(8,128)(2,1)}), bf16[4,64,1024]{2,1,0:T(8,128)(2,1)S(1)}, u32[]{:S(2)}, u32[]{:S(2)}) async-start(bf16[4,64,1024]{2,1,0:T(8,128)(2,1)} %broadcast_in_dim.14), calls=%async_computation.1 | async-start | bytes 1048576 | tf_op jit(solution)/shard_map/all_to_all | solution.py:387
  18.1 0.7 copy-start.6
  18.8 0.7 copy-start.8
  19.5 0.7 copy-start.9
  30.8 82.3 %all-to-all-start = ((bf16[32,2,16,1024]{3,2,1,0:T(8,128)(2,1)}), bf16[32,2,16,1024]{3,2,1,0:T(8,128)(2,1)S(1)}, u32[]{:S(2)}, u32[]{:S(2)}) async-start(bf16[32,2,16,1024]{3,2,1,0:T(8,128)(2,1)} %get-tuple-element.14), calls=%async_computation | async-start | bytes 4194304 | tf_op jit(solution)/shard_map/all_to_all | solution.py:387
  43.5 69.6 %all-gather.2.cloned.1.call-start = ((), (), s32[]{:S(2)}) async-start(), calls=%async_computation.5 | async-start | bytes 2228224 | tf_op jit(solution)/shard_map/all_gather | solution.py:424
  44.2 129.4 %reduce-scatter.3.cloned.1.call-start = ((), (), s32[]{:S(2)}) async-start(), calls=%async_computation.6 | async-start | bytes 5242880 | tf_op jit(solution)/shard_map/reduce_scatter | solution.py:439
  44.2 19.6 %collective-permute-start.2 = (bf16[256,1024]{1,0:T(8,128)(2,1)S(1)}, bf16[256,1024]{1,0:T(8,128)(2,1)S(1)}, u32[]{:S(2)}, u32[]{:S(2)}) collective-permute-start(bf16[256,1024]{1,0:T(8,128)(2,1)S(1)} %bitcast.12), channel_id=1, source_target_pairs={{0,384},{128,0},{256,128},{384,256},{1,385},{129,1},{257,129},{385... | collective-permute-start | bytes 1572872 | tf_op jit(solution)/shard_map/ppermute | solution.py:392
  48.6 16.5 %collective-permute-start.1 = (bf16[256,1024]{1,0:T(8,128)(2,1)S(1)}, bf16[256,1024]{1,0:T(8,128)(2,1)}, u32[]{:S(2)}, u32[]{:S(2)}) collective-permute-start(bf16[256,1024]{1,0:T(8,128)(2,1)S(1)} %bitcast.13), channel_id=1, source_target_pairs={{0,256},{128,384},{256,0},{384,128},{1,257},{129,385},{257,1},{385... | collective-permute-start | bytes 1572872 | tf_op jit(solution)/shard_map/ppermute | solution.py:392
  51.1 28.2 %collective-permute-start = (bf16[256,1024]{1,0:T(8,128)(2,1)S(1)}, bf16[256,1024]{1,0:T(8,128)(2,1)}, u32[]{:S(2)}, u32[]{:S(2)}) collective-permute-start(bf16[256,1024]{1,0:T(8,128)(2,1)S(1)} %bitcast.14), channel_id=1, source_target_pairs={{0,128},{128,256},{256,384},{384,0},{1,129},{129,257},{257,385},{3... | collective-permute-start | bytes 1572872 | tf_op jit(solution)/shard_map/ppermute | solution.py:392
  80.6 1.4 copy-start
  128.7 64.7 %copy-start.1 = (f32[128,1024]{1,0:T(8,128)S(1)}, f32[128,1024]{1,0:T(8,128)}, u32[]{:S(2)}) copy-start(f32[128,1024]{1,0:T(8,128)} %get-tuple-element.17.xhat_ref) | copy-start | bytes 1572868
  128.7 64.7 %copy-start.2 = (bf16[128,1024]{1,0:T(8,128)(2,1)S(1)}, bf16[128,1024]{1,0:T(8,128)(2,1)}, u32[]{:S(2)}) copy-start(bf16[128,1024]{1,0:T(8,128)(2,1)} %cot_ref.3) | copy-start | bytes 786436
  128.7 64.7 %copy-start.3 = (bf16[128,1024]{1,0:T(8,128)(2,1)S(1)}, bf16[128,1024]{1,0:T(8,128)(2,1)}, u32[]{:S(2)}) copy-start(bf16[128,1024]{1,0:T(8,128)(2,1)} %x_ref.3) | copy-start | bytes 786436
  128.7 64.7 %copy-start.4 = (f32[49,1024]{1,0:T(8,128)S(1)}, f32[49,1024]{1,0:T(8,128)}, u32[]{:S(2)}) copy-start(f32[49,1024]{1,0:T(8,128)} %taps_ref.3) | copy-start | bytes 602116
  128.7 64.7 %copy-start.7 = (f32[1024]{0:T(1024)S(1)}, f32[1024]{0:T(1024)}, u32[]{:S(2)}) copy-start(f32[1024]{0:T(1024)} %param.15) | copy-start | bytes 12292
  128.7 64.6 %all-to-all-start.2 = ((bf16[32,2,16,1024]{3,2,1,0:T(8,128)(2,1)}), bf16[32,2,16,1024]{3,2,1,0:T(8,128)(2,1)S(1)}, u32[]{:S(2)}, u32[]{:S(2)}) async-start(bf16[32,2,16,1024]{3,2,1,0:T(8,128)(2,1)} %return_rows.1), calls=%async_computation.2 | async-start | bytes 4194304 | tf_op jit(solution)/shard_map/all_to_all | solution.py:387
  138.4 73.8 %reduce-scatter.5.cloned.1.call-start = ((), (), s32[]{:S(2)}) async-start(), calls=%async_computation.7 | async-start | bytes 1310720 | tf_op jit(solution)/shard_map/reduce_scatter | solution.py:442
  193.3 0.8 copy-start.5
Sparse Core Ops, SparseCore 0:
  47.3 65.7 all-gather.1
  122.3 51.2 reduce-scatter.2
  176.4 35.6 reduce-scatter.4

commit v7 on v6

--- a/solution.py
+++ b/solution.py
@@ -84,10 +84,8 @@
     lax.fori_loop(0, padded.shape[2] // LANES, chunk, 0)
 
 
-def send_kernel(
+def front_kernel(
     ids_ref,
-    gates_ref,
-    cot_ref,
     x_ref,
     taps_ref,
     bias_ref,
@@ -123,13 +121,15 @@
     rstd_ref[...] = jnp.broadcast_to(rstd, (TOK, LANES))
     normed = (xhat * gain_ref[...] + shift_ref[...]).astype(BF16)
     select = slot_selects(ids_ref)
-    sent = dot(as_bf16(select[0] | select[1]), normed).astype(BF16)
-    sent_ref[:, 0] = sent.reshape(EXPERTS, CAP, width)
+    sent_ref[...] = dot(as_bf16(select[0] | select[1]), normed).astype(BF16)
+
+
+def send_grads_kernel(ids_ref, gates_ref, cot_ref, out_ref):
+    select = slot_selects(ids_ref)
     cot = cot_ref[...].astype(F32)
     first = (gates_ref[:, 0:1] * cot).astype(BF16)
     second = (gates_ref[:, 1:2] * cot).astype(BF16)
-    sent = (dot(as_bf16(select[0]), first) + dot(as_bf16(select[1]), second)).astype(BF16)
-    sent_ref[:, 1] = sent.reshape(EXPERTS, CAP, width)
+    out_ref[...] = (dot(as_bf16(select[0]), first) + dot(as_bf16(select[1]), second)).astype(BF16)
 
 
 def finish_kernel(
@@ -184,7 +184,8 @@
 
 
 def expert_kernel(
-    moved_ref,
+    rows_ref,
+    grads_ref,
     w_in_ref,
     w_out_ref,
     terms_ref,
@@ -194,16 +195,14 @@
     gh_s,
 ):
     step = pl.program_id(0)
-    sources, _, count, width = moved_ref.shape
-    flat = sources * count
     block = w_in_ref.shape[1]
     part = terms_ref.shape[0]
     steps = hidden_s.shape[1] // block
 
     @pl.when(step < steps)
     def _():
-        pre = dot(moved_ref[:, 0].reshape(flat, width), w_in_ref[...])
-        raw = dot(moved_ref[:, 1].reshape(flat, width), w_out_ref[...])
+        pre = dot(rows_ref[...], w_in_ref[...])
+        raw = dot(grads_ref[...], w_out_ref[...])
         square = pre * pre
         t = jnp.tanh(SQRT_2_OVER_PI * (pre + 0.044715 * (pre * square)))
         cdf = 0.5 * (1.0 + t)
@@ -221,8 +220,8 @@
     @pl.when(step >= steps)
     def _():
         lanes = pl.ds(pl.multiple_of((step - steps) * part, part), part)
-        rows = moved_ref[:, 0, :, lanes].reshape(flat, part)
-        grads = moved_ref[:, 1, :, lanes].reshape(flat, part)
+        rows = rows_ref[:, lanes]
+        grads = grads_ref[:, lanes]
         hid = hidden_s.shape[1]
         terms_ref[:, :hid] = contract_first(rows, gh_s[...]).astype(BF16)
         terms_ref[:, hid:] = contract_first(grads, hidden_s[...]).astype(BF16)
@@ -269,16 +268,30 @@
     return pl.BlockSpec(dims, lambda i: (0,) * len(dims))
 
 
-def send(ids, gates, cot, x, taps, bias, gain, shift):
+def send_grads(ids, gates, cot):
+    width = cot.shape[1]
+    return pl.pallas_call(
+        send_grads_kernel,
+        grid=(1,),
+        out_shape=pltpu.HBM((SLOTS, width), BF16),
+        in_specs=[VMEM] * 2 + [all_of(cot.shape)],
+        out_specs=all_of((SLOTS, width)),
+        compiler_params=params(),
+        cost_estimate=cost(4 * SLOTS * TOK * width, 2 * SLOTS * width),
+        name="send_grads",
+    )(ids, gates, in_hbm(cot))
+
+
+def front(ids, x, taps, bias, gain, shift):
     width = x.shape[1]
     rows = [bias.reshape(1, width), gain.reshape(1, width), shift.reshape(1, width)]
-    outs = [((EXPERTS, 2, CAP, width), BF16), ((TOK, width), F32), ((TOK, LANES), F32)]
-    wide = [in_hbm(v) for v in (cot, x, taps)]
-    return pl.pallas_call(
-        send_kernel,
+    outs = [((SLOTS, width), BF16), ((TOK, width), F32), ((TOK, LANES), F32)]
+    wide = [in_hbm(v) for v in (x, taps)]
+    return pl.pallas_call(
+        front_kernel,
         grid=(1,),
         out_shape=tuple(pltpu.HBM(*out) for out in outs),
-        in_specs=[VMEM] * 2 + [all_of(v.shape) for v in wide] + [VMEM] * 3,
+        in_specs=[VMEM] + [all_of(v.shape) for v in wide] + [VMEM] * 3,
         out_specs=[all_of(dims) for dims, _ in outs],
         scratch_shapes=[
             pltpu.VMEM((IMG_H + KSIZE - 1, IMG_W + 16, width), F32),
@@ -286,8 +299,8 @@
         ],
         compiler_params=params(20),
         cost_estimate=cost(100 * TOK * width * 20, 4 * SLOTS * width),
-        name="send",
-    )(ids, gates, *wide, *rows)
+        name="front",
+    )(ids, *wide, *rows)
 
 
 def finish(ids, gates, back, xhat, rstd, gain, taps, cot, x):
@@ -304,9 +317,8 @@
     )(ids, gates, back, xhat, rstd, gain.reshape(1, width), taps, cot, x)
 
 
-def expert(moved, w_in, w_out):
-    sources, _, count, width = moved.shape
-    flat = sources * count
+def expert(rows, grads, w_in, w_out):
+    flat, width = rows.shape
     hid = w_in.shape[1]
     block = 512
     part = 256
@@ -321,7 +333,7 @@
             pltpu.HBM((flat, hid), BF16),
             pltpu.HBM((flat, hid), BF16),
         ),
-        in_specs=[VMEM, weight, weight],
+        in_specs=[VMEM, VMEM, weight, weight],
         out_specs=[
             pl.BlockSpec((part, 2 * hid), lambda j: (jnp.maximum(j - steps, 0), 0)),
             hidden,
@@ -331,7 +343,7 @@
         compiler_params=params(30),
         cost_estimate=cost(8 * flat * width * hid, 12 * MIB),
         name="expert",
-    )(moved, in_hbm(w_in), in_hbm(w_out))
+    )(rows, grads, in_hbm(w_in), in_hbm(w_out))
 
 
 def widen(total):
@@ -387,6 +399,11 @@
     return lax.all_to_all(rows, axes, split_axis=0, concat_axis=0, tiled=True)
 
 
+def exchange_rows(rows, axes):
+    count, width = rows.shape
+    return exchange(rows.reshape(EXPERTS, CAP, width), axes).reshape(count, width)
+
+
 def shifted(value, axis, k):
     n = lax.axis_size(axis)
     return lax.ppermute(value, axis, [(i, (i + k) % n) for i in range(n)])
@@ -399,11 +416,6 @@
 def gather_by(axis, piece):
     far, after, before = (shifted(piece, axis, k) for k in (2, 1, 3))
     return place(where_on(axis), [piece, after, far, before])
-
-
-def gather_y(piece):
-    parts = lax.axis_size("yh")
-    return exchange(jnp.broadcast_to(piece[None], (parts,) + piece.shape), "yh")
 
 
 def local(
@@ -422,22 +434,17 @@
     dp = ("x", "yh")
     ep = ("z", "yl", "core")
     full_in = lax.all_gather(w_in, dp, axis=1, tiled=True)[0]
-    sent, xhat, rstd = send(
-        expert_ids,
-        gate_weights,
-        grad_mixed,
-        patches,
-        conv_weight,
-        conv_bias,
-        ln_gain,
-        ln_shift,
+    gated = send_grads(expert_ids, gate_weights, grad_mixed)
+    grads = exchange_rows(gated, ep)
+    along_y = gather_by("yh", w_out[0])
+    sent, xhat, rstd = front(
+        expert_ids, patches, conv_weight, conv_bias, ln_gain, ln_shift
     )
-    moved = exchange(sent, ep)
-    along_y = gather_y(w_out[0])
+    rows = exchange_rows(sent, ep)
     full_out = gather_by("x", along_y.reshape(-1, hid)).reshape(-1, hid)
-    partial, hidden, gh = expert(moved, full_in, full_out)
+    partial, hidden, gh = expert(rows, grads, full_in, full_out)
     over_x = lax.psum_scatter(partial, "x", scatter_dimension=0, tiled=True)
-    back = return_rows(hidden, gh, full_in, full_out, moved.shape[0])
+    back = return_rows(hidden, gh, full_in, full_out, EXPERTS)
     returned = exchange(back, ep)
     total = lax.psum_scatter(over_x, "yh", scatter_dimension=0, tiled=True)
     grad_in, grad_out = widen(total)

time: 221 us -> 240 us (1.086)
  waiting for transfers between devices: 126 us -> 138 us
  starting transfers between devices: 39.4 us -> 47.4 us
  local copies, waits for them, and re-layouts: 7.64 us -> 3.85 us
    all_gather x1, waiting for transfers between devices: 31.1 us -> 0.01 us  [local(): full_in = lax.all_gather(w_in, dp, axis=1, tiled=True)[0]]
    ppermute x3 -> x6, waiting for transfers between devices: 25.6 us -> 53.1 us  [shifted(): return lax.ppermute(value, axis, [(i, (i + k) % n) for i in range(n)])]
    all_to_all x3, waiting for transfers between devices: 21.7 us -> 41 us  [exchange(): return lax.all_to_all(rows, axes, split_axis=0, concat_axis=0, tiled=True)]
    ppermute x3 -> x6, starting transfers between devices: 9.33 us -> 22 us  [shifted(): return lax.ppermute(value, axis, [(i, (i + k) % n) for i in range(n)])]
    all_to_all x3, starting transfers between devices: 30 us -> 25.3 us  [exchange(): return lax.all_to_all(rows, axes, split_axis=0, concat_axis=0, tiled=True)]
    pallas_call x1 -> x2, Pallas kernels: 8.61 us -> 10.5 us  [the longest x1 7.59 us: front(): pl.pallas_call(front_kernel, grid=(1,), out_shape=tuple((pltpu.HBM(*out)...]
  transfers between devices with their start and end apart: 9 -> 12, of which waited for: 8 -> 9; matrix products, arithmetic and copies ran while one was open for 1% -> 0% of each run, Pallas kernels for 7% -> 9%
where the time goes in v7:
time: 240 us; the launch traced here: 239 us
  waiting for transfers between devices  138 us (58%)
  starting transfers between devices  47.4 us (20%)
  Pallas kernels  35.9 us (15%)
  between operations  14 us (6%)
  local copies, waits for them, and re-layouts  3.85 us (2%)
    ppermute x6, waiting for transfers between devices, shifted(): return lax.ppermute(value, axis, [(i, (i + k) % n) for i in range(n)])  53.1 us
    all_to_all x3, waiting for transfers between devices, exchange(): return lax.all_to_all(rows, axes, split_axis=0, concat_axis=0, tiled=True)  41 us
    reduce_scatter x1, waiting for transfers between devices, local(): over_x = lax.psum_scatter(partial, 'x', scatter_dimension=0, tiled=True)  33.7 us
    all_to_all x3, starting transfers between devices, exchange(): return lax.all_to_all(rows, axes, split_axis=0, concat_axis=0, tiled=True)  25.3 us
    ppermute x6, starting transfers between devices, shifted(): return lax.ppermute(value, axis, [(i, (i + k) % n) for i in range(n)])  22 us
    reduce_scatter x1, waiting for transfers between devices, local(): total = lax.psum_scatter(over_x, 'yh', scatter_dimension=0, tiled=True)  9.79 us
    pallas_call x1, Pallas kernels, expert(): pl.pallas_call(expert_kernel, grid=(steps + width // part,), out_shape=(p...  9.1 us
    pallas_call x1, Pallas kernels, front(): pl.pallas_call(front_kernel, grid=(1,), out_shape=tuple((pltpu.HBM(*out)...  7.59 us
  transfers between devices with their start and end apart: 12, of which 9 were waited for; matrix products, arithmetic and copies ran while one was open for 0% of the time, Pallas kernels for 9%

profile of v7, /device:TPU:1, one launch (start us, length us, event | category | flops | bytes accessed | tf_op | source)
XLA Modules:
  0.0 239.5 jit_solution(16319617178512063553)
XLA Ops:
  7.2 0.8 copy.17.ids_ref
  8.0 0.8 copy.18.gates_ref
  8.8 2.9 %send_grads.1 = bf16[512,1024]{1,0:T(8,128)(2,1)} custom-call(s32[128,2]{1,0:T(8,128)S(1)} %copy.17.ids_ref, f32[128,2]{1,0:T(8,128)S(1)} %copy.18.gates_ref, bf16[128,1024]{1,0:T(8,128)(2,1)} %cot_ref.3), custom_call_target="tpu_custom_call" | custom-call | flops 268435456 | bytes 1048576 | tf_op jit(solution)/shard_map/send_grads/pallas_call | solution.py:273
  11.7 13.0 %all-to-all-start.1 = ((bf16[32,16,1024]{2,1,0:T(8,128)(2,1)}), bf16[32,16,1024]{2,1,0:T(8,128)(2,1)S(1)}, u32[]{:S(2)}, u32[]{:S(2)}) async-start(bf16[32,16,1024]{2,1,0:T(8,128)(2,1)} %bitcast.31), calls=%async_computation.1 | async-start | bytes 2097152 | tf_op jit(solution)/shard_map/all_to_all | solution.py:399
  24.7 0.7 all-gather.2.cloned.1.call-update
  25.4 7.6 %front.1 = (bf16[512,1024]{1,0:T(8,128)(2,1)}, f32[128,1024]{1,0:T(8,128)}, f32[128,128]{1,0:T(8,128)}) custom-call(s32[128,2]{1,0:T(8,128)S(1)} %copy.17.ids_ref, bf16[128,1024]{1,0:T(8,128)(2,1)} %x_ref.3, f32[49,1024]{1,0:T(8,128)} %taps_ref.3, f32[1,1024]{1,0:T(1,128)S(1)} %bitcast.29, f32[1,1024]{1,0:T(1,128)S(1)} %bitcast.27, f32[1,1024]{1,0:T(1,128)S(1)} %bitcast.30), custom_call_target="tpu_custom_call" | custom-call | flops 262144000 | bytes 2097152 | tf_op jit(solution)/shard_map/front/pallas_call | solution.py:290
  33.0 19.9 %all-to-all-done.1 = bf16[32,16,1024]{2,1,0:T(8,128)(2,1)S(1)} async-done(((bf16[32,16,1024]{2,1,0:T(8,128)(2,1)}), bf16[32,16,1024]{2,1,0:T(8,128)(2,1)S(1)}, u32[]{:S(2)}, u32[]{:S(2)}) %all-to-all-start.1) | async-done | bytes 1048608 | tf_op jit(solution)/shard_map/all_to_all | solution.py:399
  52.9 4.2 %all-to-all-start = ((bf16[32,16,1024]{2,1,0:T(8,128)(2,1)}), bf16[32,16,1024]{2,1,0:T(8,128)(2,1)S(1)}, u32[]{:S(2)}, u32[]{:S(2)}) async-start(bf16[32,16,1024]{2,1,0:T(8,128)(2,1)} %bitcast.34), calls=%async_computation | async-start | bytes 2097152 | tf_op jit(solution)/shard_map/all_to_all | solution.py:399
  57.1 0.0 reduce-scatter.3.cloned.1.call-start
  57.2 5.0 %collective-permute-start.2 = (bf16[64,1024]{1,0:T(8,128)(2,1)S(1)}, bf16[64,1024]{1,0:T(8,128)(2,1)S(1)}, u32[]{:S(2)}, u32[]{:S(2)}) collective-permute-start(bf16[64,1024]{1,0:T(8,128)(2,1)S(1)} %bitcast.23), channel_id=1, source_target_pairs={{0,96},{32,0},{64,32},{96,64},{1,97},{33,1},{65,33},{97,65},{2,98}... | collective-permute-start | bytes 393224 | tf_op jit(solution)/shard_map/ppermute | solution.py:409
  62.2 4.4 %collective-permute-start.1 = (bf16[64,1024]{1,0:T(8,128)(2,1)S(1)}, bf16[64,1024]{1,0:T(8,128)(2,1)S(1)}, u32[]{:S(2)}, u32[]{:S(2)}) collective-permute-start(bf16[64,1024]{1,0:T(8,128)(2,1)S(1)} %bitcast.24), channel_id=1, source_target_pairs={{0,64},{32,96},{64,0},{96,32},{1,65},{33,97},{65,1},{97,33},{2,66}... | collective-permute-start | bytes 393224 | tf_op jit(solution)/shard_map/ppermute | solution.py:409
  66.6 3.3 %collective-permute-start = (bf16[64,1024]{1,0:T(8,128)(2,1)S(1)}, bf16[64,1024]{1,0:T(8,128)(2,1)S(1)}, u32[]{:S(2)}, u32[]{:S(2)}) collective-permute-start(bf16[64,1024]{1,0:T(8,128)(2,1)S(1)} %bitcast.25), channel_id=1, source_target_pairs={{0,32},{32,64},{64,96},{96,0},{1,33},{33,65},{65,97},{97,1},{2,34}... | collective-permute-start | bytes 393224 | tf_op jit(solution)/shard_map/ppermute | solution.py:409
  70.0 17.9 %collective-permute-done.1.refs_2_ = bf16[64,1024]{1,0:T(8,128)(2,1)S(1)} collective-permute-done((bf16[64,1024]{1,0:T(8,128)(2,1)S(1)}, bf16[64,1024]{1,0:T(8,128)(2,1)S(1)}, u32[]{:S(2)}, u32[]{:S(2)}) %collective-permute-start.1) | collective-permute-done | bytes 131104 | tf_op jit(solution)/shard_map/ppermute | solution.py:409
  87.9 11.5 %collective-permute-done.refs_1_ = bf16[64,1024]{1,0:T(8,128)(2,1)S(1)} collective-permute-done((bf16[64,1024]{1,0:T(8,128)(2,1)S(1)}, bf16[64,1024]{1,0:T(8,128)(2,1)S(1)}, u32[]{:S(2)}, u32[]{:S(2)}) %collective-permute-start) | collective-permute-done | bytes 131104 | tf_op jit(solution)/shard_map/ppermute | solution.py:409
  99.5 4.3 %collective-permute-start.5 = (bf16[256,1024]{1,0:T(8,128)(2,1)S(1)}, bf16[256,1024]{1,0:T(8,128)(2,1)S(1)}, u32[]{:S(2)}, u32[]{:S(2)}) collective-permute-start(bf16[256,1024]{1,0:T(8,128)(2,1)S(1)} %bitcast.17), channel_id=1, source_target_pairs={{0,384},{128,0},{256,128},{384,256},{1,385},{129,1},{257,129},{385... | collective-permute-start | bytes 1572872 | tf_op jit(solution)/shard_map/ppermute | solution.py:409
  103.8 2.4 collective-permute-start.4
  106.2 2.6 %collective-permute-start.3 = (bf16[256,1024]{1,0:T(8,128)(2,1)S(1)}, bf16[256,1024]{1,0:T(8,128)(2,1)}, u32[]{:S(2)}, u32[]{:S(2)}) collective-permute-start(bf16[256,1024]{1,0:T(8,128)(2,1)S(1)} %bitcast.19), channel_id=1, source_target_pairs={{0,128},{128,256},{256,384},{384,0},{1,129},{129,257},{257,385},{3... | collective-permute-start | bytes 1572872 | tf_op jit(solution)/shard_map/ppermute | solution.py:409
  108.7 6.1 %collective-permute-done.5.refs_3_ = bf16[256,1024]{1,0:T(8,128)(2,1)S(1)} collective-permute-done((bf16[256,1024]{1,0:T(8,128)(2,1)S(1)}, bf16[256,1024]{1,0:T(8,128)(2,1)S(1)}, u32[]{:S(2)}, u32[]{:S(2)}) %collective-permute-start.5) | collective-permute-done | bytes 524320 | tf_op jit(solution)/shard_map/ppermute | solution.py:409
  114.8 4.8 %collective-permute-done.4.refs_2_ = bf16[256,1024]{1,0:T(8,128)(2,1)} collective-permute-done((bf16[256,1024]{1,0:T(8,128)(2,1)S(1)}, bf16[256,1024]{1,0:T(8,128)(2,1)}, u32[]{:S(2)}, u32[]{:S(2)}) %collective-permute-start.4) | collective-permute-done | bytes 524320 | tf_op jit(solution)/shard_map/ppermute | solution.py:409
  119.6 12.8 %collective-permute-done.3.refs_1_ = bf16[256,1024]{1,0:T(8,128)(2,1)} collective-permute-done((bf16[256,1024]{1,0:T(8,128)(2,1)S(1)}, bf16[256,1024]{1,0:T(8,128)(2,1)}, u32[]{:S(2)}, u32[]{:S(2)}) %collective-permute-start.3) | collective-permute-done | bytes 524320 | tf_op jit(solution)/shard_map/ppermute | solution.py:409
  132.4 1.3 place.3
  133.7 1.4 copy-done
  135.1 9.1 %expert.1 = (bf16[1024,2048]{1,0:T(8,128)(2,1)}, bf16[512,1024]{1,0:T(8,128)(2,1)}, bf16[512,1024]{1,0:T(8,128)(2,1)}) custom-call(bf16[512,1024]{1,0:T(8,128)(2,1)S(1)} %bitcast.22, bf16[512,1024]{1,0:T(8,128)(2,1)S(1)} %bitcast.21, bf16[1024,1024]{1,0:T(8,128)(2,1)} %bitcast.32, bf16[1024,1024]{1,0:T(8,128)(2,1)} %bitcast.15), custom_call_target="tpu_custom_call" | custom-call | flops 4294967296 | bytes 12582912 | tf_op jit(solution)/shard_map/expert/pallas_call | solution.py:328
  144.3 6.5 %return_rows.1 = bf16[32,2,16,1024]{3,2,1,0:T(8,128)(2,1)} custom-call(bf16[512,1024]{1,0:T(8,128)(2,1)} %get-tuple-element.15.hidden_ref, bf16[512,1024]{1,0:T(8,128)(2,1)} %get-tuple-element.16.gh_ref, bf16[1024,1024]{1,0:T(8,128)(2,1)} %bitcast.33, bf16[1024,1024]{1,0:T(8,128)(2,1)} %bitcast.16), custom_call_target="tpu_custom_call" | custom-call | flops 2147483648 | bytes 8388608 | tf_op jit(solution)/shard_map/return_rows/pallas_call | solution.py:370
  150.8 8.1 %all-to-all-start.2 = ((bf16[32,2,16,1024]{3,2,1,0:T(8,128)(2,1)}), bf16[32,2,16,1024]{3,2,1,0:T(8,128)(2,1)S(1)}, u32[]{:S(2)}, u32[]{:S(2)}) async-start(bf16[32,2,16,1024]{3,2,1,0:T(8,128)(2,1)} %return_rows.1), calls=%async_computation.2 | async-start | bytes 4194304 | tf_op jit(solution)/shard_map/all_to_all | solution.py:399
  158.8 0.0 reduce-scatter.5.cloned.1.call-start
  158.9 33.7 %reduce-scatter.3.cloned.1.call-done = bf16[256,2048]{1,0:T(8,128)(2,1)} async-done(((bf16[1024,2048]{1,0:T(8,128)(2,1)}), bf16[256,2048]{1,0:T(8,128)(2,1)}) %reduce-scatter.3.cloned.1.call-update) | async-done | bytes 1048592 | tf_op jit(solution)/shard_map/reduce_scatter | solution.py:446
  192.6 21.2 %all-to-all-done.2.back_ref = bf16[32,2,16,1024]{3,2,1,0:T(8,128)(2,1)S(1)} async-done(((bf16[32,2,16,1024]{3,2,1,0:T(8,128)(2,1)}), bf16[32,2,16,1024]{3,2,1,0:T(8,128)(2,1)S(1)}, u32[]{:S(2)}, u32[]{:S(2)}) %all-to-all-start.2) | async-done | bytes 2097184 | tf_op jit(solution)/shard_map/all_to_all | solution.py:399
  213.8 0.8 copy-done.6
  214.6 6.8 %finish.1 = (bf16[128,1024]{1,0:T(8,128)(2,1)}, f32[128,1024]{1,0:T(8,128)}) custom-call(s32[128,2]{1,0:T(8,128)S(1)} %copy.17.ids_ref, f32[128,2]{1,0:T(8,128)S(1)} %copy.18.gates_ref, bf16[32,2,16,1024]{3,2,1,0:T(8,128)(2,1)S(1)} %all-to-all-done.2.back_ref, f32[128,1024]{1,0:T(8,128)S(1)} %copy-done.2, f32[128,128]{1,0:T(8,128)S(1)} %copy-done.6, ...), custom_call_target="tpu_custom_call" | custom-call | flops 262144000 | bytes 2097152 | tf_op jit(solution)/shard_map/finish/pallas_call | solution.py:308
  221.4 9.8 %reduce-scatter.5.cloned.1.call-done.sum_ref = bf16[64,2048]{1,0:T(8,128)(2,1)} async-done(((bf16[256,2048]{1,0:T(8,128)(2,1)}), bf16[64,2048]{1,0:T(8,128)(2,1)}) %reduce-scatter.5.cloned.1.call-update) | async-done | bytes 262160 | tf_op jit(solution)/shard_map/reduce_scatter | solution.py:449
  231.2 1.8 widen.1
  (25 shorter events, 0.2 us)
Async XLA Ops:
  7.2 18.2 %copy-start.9 = (f32[1024]{0:T(1024)S(1)}, f32[1024]{0:T(1024)}, u32[]{:S(2)}) copy-start(f32[1024]{0:T(1024)} %param.16) | copy-start | bytes 12292
  7.2 18.2 %copy-start.7 = (f32[1024]{0:T(1024)S(1)}, f32[1024]{0:T(1024)}, u32[]{:S(2)}) copy-start(f32[1024]{0:T(1024)} %param.15) | copy-start | bytes 12292
  7.2 18.2 %copy-start.8 = (f32[1024]{0:T(1024)S(1)}, f32[1024]{0:T(1024)}, u32[]{:S(2)}) copy-start(f32[1024]{0:T(1024)} %param.14) | copy-start | bytes 12292
  11.7 41.2 %all-to-all-start.1 = ((bf16[32,16,1024]{2,1,0:T(8,128)(2,1)}), bf16[32,16,1024]{2,1,0:T(8,128)(2,1)S(1)}, u32[]{:S(2)}, u32[]{:S(2)}) async-start(bf16[32,16,1024]{2,1,0:T(8,128)(2,1)} %bitcast.31), calls=%async_computation.1 | async-start | bytes 2097152 | tf_op jit(solution)/shard_map/all_to_all | solution.py:399
  24.7 32.5 %copy-start.5 = (bf16[1,64,1024]{2,1,0:T(8,128)(2,1)S(1)}, bf16[1,64,1024]{2,1,0:T(8,128)(2,1)}, u32[]{:S(2)}) copy-start(bf16[1,64,1024]{2,1,0:T(8,128)(2,1)} %param.18) | copy-start | bytes 393220
  24.7 110.5 %all-gather.2.cloned.1.call-start = ((), (), s32[]{:S(2)}) async-start(), calls=%async_computation.5 | async-start | bytes 2228224 | tf_op jit(solution)/shard_map/all_gather | solution.py:436
  52.9 82.2 %all-to-all-start = ((bf16[32,16,1024]{2,1,0:T(8,128)(2,1)}), bf16[32,16,1024]{2,1,0:T(8,128)(2,1)S(1)}, u32[]{:S(2)}, u32[]{:S(2)}) async-start(bf16[32,16,1024]{2,1,0:T(8,128)(2,1)} %bitcast.34), calls=%async_computation | async-start | bytes 2097152 | tf_op jit(solution)/shard_map/all_to_all | solution.py:399
  57.1 135.4 %reduce-scatter.3.cloned.1.call-start = ((), (), s32[]{:S(2)}) async-start(), calls=%async_computation.6 | async-start | bytes 5242880 | tf_op jit(solution)/shard_map/reduce_scatter | solution.py:446
  57.2 12.8 %collective-permute-start.2 = (bf16[64,1024]{1,0:T(8,128)(2,1)S(1)}, bf16[64,1024]{1,0:T(8,128)(2,1)S(1)}, u32[]{:S(2)}, u32[]{:S(2)}) collective-permute-start(bf16[64,1024]{1,0:T(8,128)(2,1)S(1)} %bitcast.23), channel_id=1, source_target_pairs={{0,96},{32,0},{64,32},{96,64},{1,97},{33,1},{65,33},{97,65},{2,98}... | collective-permute-start | bytes 393224 | tf_op jit(solution)/shard_map/ppermute | solution.py:409
  62.2 25.7 %collective-permute-start.1 = (bf16[64,1024]{1,0:T(8,128)(2,1)S(1)}, bf16[64,1024]{1,0:T(8,128)(2,1)S(1)}, u32[]{:S(2)}, u32[]{:S(2)}) collective-permute-start(bf16[64,1024]{1,0:T(8,128)(2,1)S(1)} %bitcast.24), channel_id=1, source_target_pairs={{0,64},{32,96},{64,0},{96,32},{1,65},{33,97},{65,1},{97,33},{2,66}... | collective-permute-start | bytes 393224 | tf_op jit(solution)/shard_map/ppermute | solution.py:409
  66.6 32.8 %collective-permute-start = (bf16[64,1024]{1,0:T(8,128)(2,1)S(1)}, bf16[64,1024]{1,0:T(8,128)(2,1)S(1)}, u32[]{:S(2)}, u32[]{:S(2)}) collective-permute-start(bf16[64,1024]{1,0:T(8,128)(2,1)S(1)} %bitcast.25), channel_id=1, source_target_pairs={{0,32},{32,64},{64,96},{96,0},{1,33},{33,65},{65,97},{97,1},{2,34}... | collective-permute-start | bytes 393224 | tf_op jit(solution)/shard_map/ppermute | solution.py:409
  99.5 15.4 %collective-permute-start.5 = (bf16[256,1024]{1,0:T(8,128)(2,1)S(1)}, bf16[256,1024]{1,0:T(8,128)(2,1)S(1)}, u32[]{:S(2)}, u32[]{:S(2)}) collective-permute-start(bf16[256,1024]{1,0:T(8,128)(2,1)S(1)} %bitcast.17), channel_id=1, source_target_pairs={{0,384},{128,0},{256,128},{384,256},{1,385},{129,1},{257,129},{385... | collective-permute-start | bytes 1572872 | tf_op jit(solution)/shard_map/ppermute | solution.py:409
  103.8 15.8 %collective-permute-start.4 = (bf16[256,1024]{1,0:T(8,128)(2,1)S(1)}, bf16[256,1024]{1,0:T(8,128)(2,1)}, u32[]{:S(2)}, u32[]{:S(2)}) collective-permute-start(bf16[256,1024]{1,0:T(8,128)(2,1)S(1)} %bitcast.18), channel_id=1, source_target_pairs={{0,256},{128,384},{256,0},{384,128},{1,257},{129,385},{257,1},{385... | collective-permute-start | bytes 1572872 | tf_op jit(solution)/shard_map/ppermute | solution.py:409
  106.2 26.2 %collective-permute-start.3 = (bf16[256,1024]{1,0:T(8,128)(2,1)S(1)}, bf16[256,1024]{1,0:T(8,128)(2,1)}, u32[]{:S(2)}, u32[]{:S(2)}) collective-permute-start(bf16[256,1024]{1,0:T(8,128)(2,1)S(1)} %bitcast.19), channel_id=1, source_target_pairs={{0,128},{128,256},{256,384},{384,0},{1,129},{129,257},{257,385},{3... | collective-permute-start | bytes 1572872 | tf_op jit(solution)/shard_map/ppermute | solution.py:409
  133.7 1.4 copy-start
  150.7 63.0 %copy-start.1 = (bf16[128,1024]{1,0:T(8,128)(2,1)S(1)}, bf16[128,1024]{1,0:T(8,128)(2,1)}, u32[]{:S(2)}) copy-start(bf16[128,1024]{1,0:T(8,128)(2,1)} %cot_ref.3) | copy-start | bytes 786436
  150.7 63.0 %copy-start.2 = (f32[128,1024]{1,0:T(8,128)S(1)}, f32[128,1024]{1,0:T(8,128)}, u32[]{:S(2)}) copy-start(f32[128,1024]{1,0:T(8,128)} %get-tuple-element.17.xhat_ref) | copy-start | bytes 1572868
  150.7 63.0 %copy-start.3 = (bf16[128,1024]{1,0:T(8,128)(2,1)S(1)}, bf16[128,1024]{1,0:T(8,128)(2,1)}, u32[]{:S(2)}) copy-start(bf16[128,1024]{1,0:T(8,128)(2,1)} %x_ref.3) | copy-start | bytes 786436
  150.8 63.0 %copy-start.4 = (f32[49,1024]{1,0:T(8,128)S(1)}, f32[49,1024]{1,0:T(8,128)}, u32[]{:S(2)}) copy-start(f32[49,1024]{1,0:T(8,128)} %taps_ref.3) | copy-start | bytes 602116
  150.8 63.0 %all-to-all-start.2 = ((bf16[32,2,16,1024]{3,2,1,0:T(8,128)(2,1)}), bf16[32,2,16,1024]{3,2,1,0:T(8,128)(2,1)S(1)}, u32[]{:S(2)}, u32[]{:S(2)}) async-start(bf16[32,2,16,1024]{3,2,1,0:T(8,128)(2,1)} %return_rows.1), calls=%async_computation.2 | async-start | bytes 4194304 | tf_op jit(solution)/shard_map/all_to_all | solution.py:399
  158.8 72.3 %reduce-scatter.5.cloned.1.call-start = ((), (), s32[]{:S(2)}) async-start(), calls=%async_computation.7 | async-start | bytes 1310720 | tf_op jit(solution)/shard_map/reduce_scatter | solution.py:449
  213.8 0.8 copy-start.6
Sparse Core Ops, SparseCore 0:
  28.5 75.1 all-gather.1
  144.4 48.1 reduce-scatter.2
  195.4 35.7 reduce-scatter.4

commit v8 on v6

--- a/solution.py
+++ b/solution.py
@@ -242,6 +242,11 @@
     out_ref[...] = sum_ref[:, hid:].astype(F32)
 
 
+def repeat_kernel(piece_ref, out_ref):
+    for k in range(out_ref.shape[0]):
+        out_ref[k] = piece_ref[...]
+
+
 def place_kernel(where_ref, *refs):
     pieces, out_ref = refs[:-1], refs[-1]
     for k, piece in enumerate(pieces):
@@ -403,7 +408,18 @@
 
 def gather_y(piece):
     parts = lax.axis_size("yh")
-    return exchange(jnp.broadcast_to(piece[None], (parts,) + piece.shape), "yh")
+    dims = (parts,) + piece.shape
+    copies = pl.pallas_call(
+        repeat_kernel,
+        grid=(1,),
+        out_shape=pltpu.HBM(dims, BF16),
+        in_specs=[all_of(piece.shape)],
+        out_specs=all_of(dims),
+        compiler_params=params(4),
+        cost_estimate=cost(0, MIB),
+        name="repeat",
+    )(in_hbm(piece))
+    return exchange(copies, "yh")
 
 
 def local(

time: 221 us -> 221 us (level)
  no operation moved by 1% of the time
where the time goes in v8:
time: 221 us; the launch traced here: 220 us
  waiting for transfers between devices  126 us (57%)
  starting transfers between devices  39.4 us (18%)
  Pallas kernels  35.8 us (16%)
  between operations  13.9 us (6%)
  local copies, waits for them, and re-layouts  5.87 us (3%)
    reduce_scatter x1, waiting for transfers between devices, local(): over_x = lax.psum_scatter(partial, 'x', scatter_dimension=0, tiled=True)  35.2 us
    all_gather x1, waiting for transfers between devices, local(): full_in = lax.all_gather(w_in, dp, axis=1, tiled=True)[0]  31.1 us
    all_to_all x3, starting transfers between devices, exchange(): return lax.all_to_all(rows, axes, split_axis=0, concat_axis=0, tiled=True)  30 us
    ppermute x3, waiting for transfers between devices, shifted(): return lax.ppermute(value, axis, [(i, (i + k) % n) for i in range(n)])  25.6 us
    all_to_all x3, waiting for transfers between devices, exchange(): return lax.all_to_all(rows, axes, split_axis=0, concat_axis=0, tiled=True)  21.7 us
    reduce_scatter x1, waiting for transfers between devices, local(): total = lax.psum_scatter(over_x, 'yh', scatter_dimension=0, tiled=True)  11.3 us
    ppermute x3, starting transfers between devices, shifted(): return lax.ppermute(value, axis, [(i, (i + k) % n) for i in range(n)])  9.33 us
    pallas_call x1, Pallas kernels, expert(): pl.pallas_call(expert_kernel, grid=(steps + width // part,), out_shape=(p...  9.07 us
  transfers between devices with their start and end apart: 9, of which 8 were waited for; matrix products, arithmetic and copies ran while one was open for 1% of the time, Pallas kernels for 7%

profile of v8, /device:TPU:1, one launch (start us, length us, event | category | flops | bytes accessed | tf_op | source)
XLA Modules:
  0.0 220.5 jit_solution(2752501462534546956)
XLA Ops:
  7.2 1.7 repeat.1
  8.9 7.6 %all-to-all-start.1 = ((bf16[4,64,1024]{2,1,0:T(8,128)(2,1)}), bf16[4,64,1024]{2,1,0:T(8,128)(2,1)S(1)}, u32[]{:S(2)}, u32[]{:S(2)}) async-start(bf16[4,64,1024]{2,1,0:T(8,128)(2,1)} %repeat.1), calls=%async_computation.1 | async-start | bytes 1048576 | tf_op jit(solution)/shard_map/all_to_all | solution.py:392
  16.5 0.8 copy.16.ids_ref
  17.3 0.8 copy.17.gates_ref
  18.1 0.7 copy-done.6
  18.8 0.7 copy-done.8
  19.5 0.7 copy-done.9
  20.2 8.6 %send.1 = (bf16[32,2,16,1024]{3,2,1,0:T(8,128)(2,1)}, f32[128,1024]{1,0:T(8,128)}, f32[128,128]{1,0:T(8,128)}) custom-call(s32[128,2]{1,0:T(8,128)S(1)} %copy.16.ids_ref, f32[128,2]{1,0:T(8,128)S(1)} %copy.17.gates_ref, bf16[128,1024]{1,0:T(8,128)(2,1)} %cot_ref.3, bf16[128,1024]{1,0:T(8,128)(2,1)} %x_ref.3, f32[49,1024]{1,0:T(8,128)} %taps_ref.3, ...), custom_call_target="tpu_custom_call" | custom-call | flops 262144000 | bytes 2097152 | tf_op jit(solution)/shard_map/send/pallas_call | solution.py:282
  28.8 2.0 all-to-all-done.1
  30.8 12.7 %all-to-all-start = ((bf16[32,2,16,1024]{3,2,1,0:T(8,128)(2,1)}), bf16[32,2,16,1024]{3,2,1,0:T(8,128)(2,1)S(1)}, u32[]{:S(2)}, u32[]{:S(2)}) async-start(bf16[32,2,16,1024]{3,2,1,0:T(8,128)(2,1)} %get-tuple-element.14), calls=%async_computation | async-start | bytes 4194304 | tf_op jit(solution)/shard_map/all_to_all | solution.py:392
  43.4 0.0 all-gather.2.cloned.1.call-start
  43.5 0.7 all-gather.2.cloned.1.call-update
  44.2 0.0 reduce-scatter.3.cloned.1.call-start
  44.2 4.4 %collective-permute-start.2 = (bf16[256,1024]{1,0:T(8,128)(2,1)S(1)}, bf16[256,1024]{1,0:T(8,128)(2,1)S(1)}, u32[]{:S(2)}, u32[]{:S(2)}) collective-permute-start(bf16[256,1024]{1,0:T(8,128)(2,1)S(1)} %bitcast.12), channel_id=1, source_target_pairs={{0,384},{128,0},{256,128},{384,256},{1,385},{129,1},{257,129},{385... | collective-permute-start | bytes 1572872 | tf_op jit(solution)/shard_map/ppermute | solution.py:397
  48.6 2.4 %collective-permute-start.1 = (bf16[256,1024]{1,0:T(8,128)(2,1)S(1)}, bf16[256,1024]{1,0:T(8,128)(2,1)}, u32[]{:S(2)}, u32[]{:S(2)}) collective-permute-start(bf16[256,1024]{1,0:T(8,128)(2,1)S(1)} %bitcast.13), channel_id=1, source_target_pairs={{0,256},{128,384},{256,0},{384,128},{1,257},{129,385},{257,1},{385... | collective-permute-start | bytes 1572872 | tf_op jit(solution)/shard_map/ppermute | solution.py:397
  51.0 2.5 %collective-permute-start = (bf16[256,1024]{1,0:T(8,128)(2,1)S(1)}, bf16[256,1024]{1,0:T(8,128)(2,1)}, u32[]{:S(2)}, u32[]{:S(2)}) collective-permute-start(bf16[256,1024]{1,0:T(8,128)(2,1)S(1)} %bitcast.14), channel_id=1, source_target_pairs={{0,128},{128,256},{256,384},{384,0},{1,129},{129,257},{257,385},{3... | collective-permute-start | bytes 1572872 | tf_op jit(solution)/shard_map/ppermute | solution.py:397
  53.6 10.2 %collective-permute-done.2.refs_3_ = bf16[256,1024]{1,0:T(8,128)(2,1)S(1)} collective-permute-done((bf16[256,1024]{1,0:T(8,128)(2,1)S(1)}, bf16[256,1024]{1,0:T(8,128)(2,1)S(1)}, u32[]{:S(2)}, u32[]{:S(2)}) %collective-permute-start.2) | collective-permute-done | bytes 524320 | tf_op jit(solution)/shard_map/ppermute | solution.py:397
  63.8 1.3 collective-permute-done.1.refs_2_
  65.1 14.1 %collective-permute-done.refs_1_ = bf16[256,1024]{1,0:T(8,128)(2,1)} collective-permute-done((bf16[256,1024]{1,0:T(8,128)(2,1)S(1)}, bf16[256,1024]{1,0:T(8,128)(2,1)}, u32[]{:S(2)}, u32[]{:S(2)}) %collective-permute-start) | collective-permute-done | bytes 524320 | tf_op jit(solution)/shard_map/ppermute | solution.py:397
  79.2 1.3 place.1
  80.6 1.4 copy-done
  81.9 31.1 %all-gather.2.cloned.1.call-done = bf16[1,1024,1024]{2,1,0:T(8,128)(2,1)} async-done(((bf16[1,64,1024]{2,1,0:T(8,128)(2,1)}), bf16[1,1024,1024]{2,1,0:T(8,128)(2,1)}) %all-gather.2.cloned.1.call-update) | async-done | bytes 2097168 | tf_op jit(solution)/shard_map/all_gather | solution.py:440
  113.1 9.1 %expert.1 = (bf16[1024,2048]{1,0:T(8,128)(2,1)}, bf16[512,1024]{1,0:T(8,128)(2,1)}, bf16[512,1024]{1,0:T(8,128)(2,1)}) custom-call(bf16[32,2,16,1024]{3,2,1,0:T(8,128)(2,1)S(1)} %all-to-all-done.moved_ref, bf16[1024,1024]{1,0:T(8,128)(2,1)} %bitcast.20, bf16[1024,1024]{1,0:T(8,128)(2,1)} %bitcast.10), custom_call_target="tpu_custom_call" | custom-call | flops 4294967296 | bytes 12582912 | tf_op jit(solution)/shard_map/expert/pallas_call | solution.py:321
  122.2 6.5 %return_rows.1 = bf16[32,2,16,1024]{3,2,1,0:T(8,128)(2,1)} custom-call(bf16[512,1024]{1,0:T(8,128)(2,1)} %get-tuple-element.15.hidden_ref, bf16[512,1024]{1,0:T(8,128)(2,1)} %get-tuple-element.16.gh_ref, bf16[1024,1024]{1,0:T(8,128)(2,1)} %bitcast.21, bf16[1024,1024]{1,0:T(8,128)(2,1)} %bitcast.11), custom_call_target="tpu_custom_call" | custom-call | flops 2147483648 | bytes 8388608 | tf_op jit(solution)/shard_map/return_rows/pallas_call | solution.py:363
  128.7 9.7 %all-to-all-start.2 = ((bf16[32,2,16,1024]{3,2,1,0:T(8,128)(2,1)}), bf16[32,2,16,1024]{3,2,1,0:T(8,128)(2,1)S(1)}, u32[]{:S(2)}, u32[]{:S(2)}) async-start(bf16[32,2,16,1024]{3,2,1,0:T(8,128)(2,1)} %return_rows.1), calls=%async_computation.2 | async-start | bytes 4194304 | tf_op jit(solution)/shard_map/all_to_all | solution.py:392
  138.4 0.0 reduce-scatter.5.cloned.1.call-start
  138.4 35.2 %reduce-scatter.3.cloned.1.call-done = bf16[256,2048]{1,0:T(8,128)(2,1)} async-done(((bf16[1024,2048]{1,0:T(8,128)(2,1)}), bf16[256,2048]{1,0:T(8,128)(2,1)}) %reduce-scatter.3.cloned.1.call-update) | async-done | bytes 1048592 | tf_op jit(solution)/shard_map/reduce_scatter | solution.py:455
  173.6 19.7 %all-to-all-done.2.back_ref = bf16[32,2,16,1024]{3,2,1,0:T(8,128)(2,1)S(1)} async-done(((bf16[32,2,16,1024]{3,2,1,0:T(8,128)(2,1)}), bf16[32,2,16,1024]{3,2,1,0:T(8,128)(2,1)S(1)}, u32[]{:S(2)}, u32[]{:S(2)}) %all-to-all-start.2) | async-done | bytes 2097184 | tf_op jit(solution)/shard_map/all_to_all | solution.py:392
  193.3 0.8 copy-done.5
  194.2 6.8 %finish.1 = (bf16[128,1024]{1,0:T(8,128)(2,1)}, f32[128,1024]{1,0:T(8,128)}) custom-call(s32[128,2]{1,0:T(8,128)S(1)} %copy.16.ids_ref, f32[128,2]{1,0:T(8,128)S(1)} %copy.17.gates_ref, bf16[32,2,16,1024]{3,2,1,0:T(8,128)(2,1)S(1)} %all-to-all-done.2.back_ref, f32[128,1024]{1,0:T(8,128)S(1)} %copy-done.1, f32[128,128]{1,0:T(8,128)S(1)} %copy-done.5, ...), custom_call_target="tpu_custom_call" | custom-call | flops 262144000 | bytes 2097152 | tf_op jit(solution)/shard_map/finish/pallas_call | solution.py:300
  200.9 11.3 %reduce-scatter.5.cloned.1.call-done.sum_ref = bf16[64,2048]{1,0:T(8,128)(2,1)} async-done(((bf16[256,2048]{1,0:T(8,128)(2,1)}), bf16[64,2048]{1,0:T(8,128)(2,1)}) %reduce-scatter.5.cloned.1.call-update) | async-done | bytes 262160 | tf_op jit(solution)/shard_map/reduce_scatter | solution.py:458
  212.2 1.8 widen.1
  (18 shorter events, 0.1 us)
Async XLA Ops:
  8.9 21.8 %all-to-all-start.1 = ((bf16[4,64,1024]{2,1,0:T(8,128)(2,1)}), bf16[4,64,1024]{2,1,0:T(8,128)(2,1)S(1)}, u32[]{:S(2)}, u32[]{:S(2)}) async-start(bf16[4,64,1024]{2,1,0:T(8,128)(2,1)} %repeat.1), calls=%async_computation.1 | async-start | bytes 1048576 | tf_op jit(solution)/shard_map/all_to_all | solution.py:392
  18.1 0.7 copy-start.6
  18.8 0.7 copy-start.8
  19.5 0.7 copy-start.9
  30.8 82.3 %all-to-all-start = ((bf16[32,2,16,1024]{3,2,1,0:T(8,128)(2,1)}), bf16[32,2,16,1024]{3,2,1,0:T(8,128)(2,1)S(1)}, u32[]{:S(2)}, u32[]{:S(2)}) async-start(bf16[32,2,16,1024]{3,2,1,0:T(8,128)(2,1)} %get-tuple-element.14), calls=%async_computation | async-start | bytes 4194304 | tf_op jit(solution)/shard_map/all_to_all | solution.py:392
  43.4 69.6 %all-gather.2.cloned.1.call-start = ((), (), s32[]{:S(2)}) async-start(), calls=%async_computation.5 | async-start | bytes 2228224 | tf_op jit(solution)/shard_map/all_gather | solution.py:440
  44.2 129.4 %reduce-scatter.3.cloned.1.call-start = ((), (), s32[]{:S(2)}) async-start(), calls=%async_computation.6 | async-start | bytes 5242880 | tf_op jit(solution)/shard_map/reduce_scatter | solution.py:455
  44.2 19.6 %collective-permute-start.2 = (bf16[256,1024]{1,0:T(8,128)(2,1)S(1)}, bf16[256,1024]{1,0:T(8,128)(2,1)S(1)}, u32[]{:S(2)}, u32[]{:S(2)}) collective-permute-start(bf16[256,1024]{1,0:T(8,128)(2,1)S(1)} %bitcast.12), channel_id=1, source_target_pairs={{0,384},{128,0},{256,128},{384,256},{1,385},{129,1},{257,129},{385... | collective-permute-start | bytes 1572872 | tf_op jit(solution)/shard_map/ppermute | solution.py:397
  48.6 16.5 %collective-permute-start.1 = (bf16[256,1024]{1,0:T(8,128)(2,1)S(1)}, bf16[256,1024]{1,0:T(8,128)(2,1)}, u32[]{:S(2)}, u32[]{:S(2)}) collective-permute-start(bf16[256,1024]{1,0:T(8,128)(2,1)S(1)} %bitcast.13), channel_id=1, source_target_pairs={{0,256},{128,384},{256,0},{384,128},{1,257},{129,385},{257,1},{385... | collective-permute-start | bytes 1572872 | tf_op jit(solution)/shard_map/ppermute | solution.py:397
  51.0 28.2 %collective-permute-start = (bf16[256,1024]{1,0:T(8,128)(2,1)S(1)}, bf16[256,1024]{1,0:T(8,128)(2,1)}, u32[]{:S(2)}, u32[]{:S(2)}) collective-permute-start(bf16[256,1024]{1,0:T(8,128)(2,1)S(1)} %bitcast.14), channel_id=1, source_target_pairs={{0,128},{128,256},{256,384},{384,0},{1,129},{129,257},{257,385},{3... | collective-permute-start | bytes 1572872 | tf_op jit(solution)/shard_map/ppermute | solution.py:397
  80.5 1.4 copy-start
  128.6 64.7 %copy-start.1 = (f32[128,1024]{1,0:T(8,128)S(1)}, f32[128,1024]{1,0:T(8,128)}, u32[]{:S(2)}) copy-start(f32[128,1024]{1,0:T(8,128)} %get-tuple-element.17.xhat_ref) | copy-start | bytes 1572868
  128.6 64.7 %copy-start.2 = (bf16[128,1024]{1,0:T(8,128)(2,1)S(1)}, bf16[128,1024]{1,0:T(8,128)(2,1)}, u32[]{:S(2)}) copy-start(bf16[128,1024]{1,0:T(8,128)(2,1)} %cot_ref.3) | copy-start | bytes 786436
  128.6 64.7 %copy-start.3 = (bf16[128,1024]{1,0:T(8,128)(2,1)S(1)}, bf16[128,1024]{1,0:T(8,128)(2,1)}, u32[]{:S(2)}) copy-start(bf16[128,1024]{1,0:T(8,128)(2,1)} %x_ref.3) | copy-start | bytes 786436
  128.6 64.7 %copy-start.4 = (f32[49,1024]{1,0:T(8,128)S(1)}, f32[49,1024]{1,0:T(8,128)}, u32[]{:S(2)}) copy-start(f32[49,1024]{1,0:T(8,128)} %taps_ref.3) | copy-start | bytes 602116
  128.7 64.7 %copy-start.7 = (f32[1024]{0:T(1024)S(1)}, f32[1024]{0:T(1024)}, u32[]{:S(2)}) copy-start(f32[1024]{0:T(1024)} %param.15) | copy-start | bytes 12292
  128.7 64.6 %all-to-all-start.2 = ((bf16[32,2,16,1024]{3,2,1,0:T(8,128)(2,1)}), bf16[32,2,16,1024]{3,2,1,0:T(8,128)(2,1)S(1)}, u32[]{:S(2)}, u32[]{:S(2)}) async-start(bf16[32,2,16,1024]{3,2,1,0:T(8,128)(2,1)} %return_rows.1), calls=%async_computation.2 | async-start | bytes 4194304 | tf_op jit(solution)/shard_map/all_to_all | solution.py:392
  138.4 73.8 %reduce-scatter.5.cloned.1.call-start = ((), (), s32[]{:S(2)}) async-start(), calls=%async_computation.7 | async-start | bytes 1310720 | tf_op jit(solution)/shard_map/reduce_scatter | solution.py:458
  193.3 0.8 copy-start.5
Sparse Core Ops, SparseCore 0:
  47.2 65.7 all-gather.1
  122.3 51.2 reduce-scatter.2
  176.4 35.7 reduce-scatter.4
